TPU v7x, 32 devices: a whole 2x2x4 slice. The times are simulated.
32 devices in a mesh: groups: 2 (over x), ctx: 8 (over z, y), head: 2 (over core).
Axes of the slice: x: 2, y: 2, z: 4, core: 2. Of those that a mesh axis runs over, the one named last changes fastest.
Arguments:
- query_rows: bfloat16 [4096, 2048], P(('groups', 'ctx'), 'head'), parts along dimension 0, may hold values from -6 to 6
- key_rows: bfloat16 [4096, 256], P(('groups', 'ctx'), 'head'), parts along dimension 0, may hold values from -6 to 6
- value_rows: bfloat16 [4096, 256], P(('groups', 'ctx'), 'head'), parts along dimension 0, may hold values from -6 to 6
- out_grad: bfloat16 [4096, 2048], P(('groups', 'ctx'), 'head'), parts along dimension 0, may hold values from -6 to 6
- doc_lengths: int32 [32], P('groups'), parts along dimension 0, may hold values from 1 to 256, 2048 in all
Outputs:
- attended: bfloat16 [4096, 2048], P(('groups', 'ctx'), 'head'), parts along dimension 0
- query_grad: bfloat16 [4096, 2048], P(('groups', 'ctx'), 'head'), parts along dimension 0
- key_grad: bfloat16 [4096, 256], P(('groups', 'ctx'), 'head'), parts along dimension 0
- value_grad: bfloat16 [4096, 256], P(('groups', 'ctx'), 'head'), parts along dimension 0
There are 2 independent parts, one for each index of `groups`. A program takes and returns all parts, laid end to end along the dimension named above; each array names one. Nothing has to cross between parts.
Inputs may be any that keep to these rules, and one draw needn't show every extreme that they name: `doc_lengths`: documents are laid end to end in position order and their lengths sum to 2048; the longest has exactly 256 tokens.
All inputs are finite; a program needn't handle non-finite values.
Results may differ from a plain program's by a relative error of at most 0.017.
Values may be sent and summed in bfloat16 or wider, within the bound.
No kernel may reach another device: no remote copies, remote signals or barrier semaphores. Data moves between devices by JAX's collectives and lax.ppermute only.
A program may use at most 64 MiB of HBM per device.

v0:
```python
import jax
import jax.numpy as jnp
from jax import lax
from jax.sharding import PartitionSpec as P

HEAD_DIM = 128
DOC_STRETCHES = 8


def from_behind(value, axis, by):
    count = lax.axis_size(axis)
    pairs = [(i, i + by) for i in range(count) if 0 <= i + by < count]
    return lax.ppermute(value, axis, pairs)


def documents(positions, doc_lengths):
    starts = jnp.cumsum(doc_lengths) - doc_lengths
    return jnp.sum((starts[None, :] <= positions[:, None]).astype(jnp.int32), axis=1) - 1


def fetch_direct(packed, band_reach):
    blocks = []
    for offset in range(-band_reach, band_reach + 1):
        if offset == 0:
            blocks.append(packed)
        else:
            blocks.append(from_behind(packed, "ctx", -offset))
    return jnp.stack(blocks)


def return_direct(partials, band_reach):
    summed = partials[band_reach]
    for offset in range(-band_reach, band_reach + 1):
        if offset != 0:
            summed = summed + from_behind(
                partials[offset + band_reach].astype(jnp.bfloat16), "ctx", offset
            ).astype(jnp.float32)
    return summed


def shards(query_rows, key_rows, value_rows, out_grad, doc_lengths):
    ctx_count = lax.axis_size("ctx")
    my_index = lax.axis_index("ctx")
    tok_dev = query_rows.shape[0]
    stretch_len = tok_dev // 2
    kv_width = key_rows.shape[1]
    kv_local = kv_width // HEAD_DIM
    heads_local = query_rows.shape[1] // HEAD_DIM
    group_size = heads_local // kv_local
    scaling = HEAD_DIM ** (-0.5)
    band_reach = min(DOC_STRETCHES, ctx_count // 4)
    step_total = band_reach + 1
    step_list = jnp.arange(step_total, dtype=jnp.int32)
    inside = my_index + step_list <= ctx_count - 1
    fold_shift = 2 * ctx_count - 1 - 2 * my_index
    packed = jnp.concatenate([key_rows, value_rows], axis=1)
    kv_window = fetch_direct(packed, band_reach)
    low_window = kv_window[:, :stretch_len]
    low_keys = low_window[: band_reach + 1][::-1]
    upper_pick = kv_window[band_reach:, stretch_len:]
    blank = jnp.zeros((step_total,) + low_window.shape[1:], low_window.dtype)
    padded_rev = jnp.concatenate([blank, low_window[::-1], blank], axis=0)
    fold_pick = lax.dynamic_slice_in_dim(
        padded_rev, step_total + band_reach - fold_shift, step_total, 0
    )
    high_keys = jnp.where(inside[:, None, None], upper_pick, fold_pick)
    key_rows_all = jnp.stack([low_keys, high_keys]).reshape(
        2, step_total * stretch_len, 2 * kv_width
    )
    key_block = key_rows_all[..., :kv_width].reshape(2, -1, kv_local, HEAD_DIM)
    value_block = key_rows_all[..., kv_width:].reshape(2, -1, kv_local, HEAD_DIM)
    row_offsets = jnp.arange(stretch_len, dtype=jnp.int32)
    query_ids = jnp.stack([my_index, 2 * ctx_count - 1 - my_index])
    query_pos = query_ids[:, None] * stretch_len + row_offsets[None, :]
    key_ids = query_ids[:, None] - step_list[None, :]
    key_pos = (key_ids[:, :, None] * stretch_len + row_offsets[None, None, :]).reshape(2, -1)
    key_valid = jnp.broadcast_to((key_ids >= 0)[:, :, None], (2, step_total, stretch_len)).reshape(
        2, -1
    )
    query_doc = documents(query_pos.reshape(-1), doc_lengths).reshape(2, stretch_len)
    key_doc = documents(key_pos.reshape(-1), doc_lengths).reshape(2, -1)
    key_doc = jnp.where(key_valid, key_doc, -2)
    allowed = (key_doc[:, None, :] == query_doc[:, :, None]) & (
        key_pos[:, None, :] <= query_pos[:, :, None]
    )
    allowed = allowed[:, :, None, None, :]
    query_group = query_rows.reshape(2, stretch_len, kv_local, group_size, HEAD_DIM)
    grad_group = out_grad.reshape(2, stretch_len, kv_local, group_size, HEAD_DIM)
    scores = (
        jnp.einsum("sqgjd,skgd->sqgjk", query_group, key_block, preferred_element_type=jnp.float32)
        * scaling
    )
    masked = jnp.where(allowed, scores, -jnp.inf)
    row_top = jnp.max(masked, axis=-1)
    log_total = row_top + jnp.log(jnp.sum(jnp.exp(masked - row_top[..., None]), axis=-1))
    weights = jnp.exp(jnp.where(allowed, scores - log_total[..., None], -jnp.inf))
    weights_low = weights.astype(jnp.bfloat16)
    attended_group = jnp.einsum(
        "sqgjk,skgd->sqgjd", weights_low, value_block, preferred_element_type=jnp.float32
    ).astype(jnp.bfloat16)
    attended = attended_group.reshape(tok_dev, heads_local * HEAD_DIM)
    row_delta = jnp.sum(
        grad_group.astype(jnp.float32) * attended_group.astype(jnp.float32), axis=-1
    )
    weight_grad = jnp.einsum(
        "sqgjd,skgd->sqgjk", grad_group, value_block, preferred_element_type=jnp.float32
    )
    score_grad = (weights * (weight_grad - row_delta[..., None])).astype(jnp.bfloat16)
    query_grad = (
        (
            jnp.einsum(
                "sqgjk,skgd->sqgjd", score_grad, key_block, preferred_element_type=jnp.float32
            )
            * scaling
        )
        .astype(jnp.bfloat16)
        .reshape(tok_dev, heads_local * HEAD_DIM)
    )
    key_part = (
        jnp.einsum("sqgjk,sqgjd->skgd", score_grad, query_group, preferred_element_type=jnp.float32)
        * scaling
    )
    value_part = jnp.einsum(
        "sqgjk,sqgjd->skgd", weights_low, grad_group, preferred_element_type=jnp.float32
    )
    pieces = jnp.concatenate(
        [
            key_part.reshape(2, step_total, stretch_len, kv_width),
            value_part.reshape(2, step_total, stretch_len, kv_width),
        ],
        axis=-1,
    )
    inside_mask = inside[:, None, None]
    upper_piece = jnp.where(inside_mask, pieces[1], 0.0)
    folded_rev = jnp.where(inside_mask, 0.0, pieces[1])[::-1]
    gap = jnp.zeros((band_reach, stretch_len, 2 * kv_width), jnp.float32)
    margin = jnp.zeros((step_total, stretch_len, 2 * kv_width), jnp.float32)
    spread = jnp.concatenate(
        [margin, jnp.zeros((2 * band_reach + 1, stretch_len, 2 * kv_width), jnp.float32), margin],
        axis=0,
    )
    spread = lax.dynamic_update_slice_in_dim(spread, folded_rev, step_total + fold_shift, 0)
    folded_part = spread[step_total : step_total + 2 * band_reach + 1]
    lower_half = jnp.concatenate([pieces[0][::-1], gap], axis=0) + folded_part
    upper_half = jnp.concatenate([gap, upper_piece], axis=0)
    part_window = jnp.concatenate([lower_half, upper_half], axis=1)
    returned = return_direct(part_window, band_reach)
    key_grad = returned[:, :kv_width].astype(jnp.bfloat16)
    value_grad = returned[:, kv_width:].astype(jnp.bfloat16)
    return (attended, query_grad, key_grad, value_grad)


def solution(mesh):
    placed = (
        P(("groups", "ctx"), "head"),
        P(("groups", "ctx"), "head"),
        P(("groups", "ctx"), "head"),
        P(("groups", "ctx"), "head"),
        P("groups"),
    )
    return jax.shard_map(
        shards,
        mesh=mesh,
        in_specs=placed,
        out_specs=(
            P(("groups", "ctx"), "head"),
            P(("groups", "ctx"), "head"),
            P(("groups", "ctx"), "head"),
            P(("groups", "ctx"), "head"),
        ),
        check_vma=False,
    )
```

profile of v0, /device:TPU:22, one launch (start us, length us, event | category | flops | bytes accessed | tf_op | source)
XLA Modules:
  0.0 52.8 jit_solution(11190821810330131273)
XLA Ops:
  0.7 0.9 %constant_dynamic-update-slice_fusion.1 = bf16[256,256]{1,0:T(8,128)(2,1)S(1)} fusion(bf16[256,128]{1,0:T(8,128)(2,1)} %param.6), kind=kLoop, calls=%fused_computation.74 | loop fusion | bytes 131072
  1.6 0.9 %constant_dynamic-update-slice_fusion = bf16[256,256]{1,0:T(8,128)(2,1)S(1)} fusion(bf16[256,256]{1,0:T(8,128)(2,1)S(1)} %constant_dynamic-update-slice_fusion.1, bf16[256,128]{1,0:T(8,128)(2,1)} %param.7), kind=kLoop, calls=%fused_computation.73 | loop fusion | bytes 131072 | tf_op jit(solution)/shard_map/concatenate | solution.py:56
  2.5 3.5 %collective-permute-start = (bf16[256,256]{1,0:T(8,128)(2,1)S(1)}, bf16[256,256]{1,0:T(8,128)(2,1)S(1)}, u32[]{:S(2)}, u32[]{:S(2)}) collective-permute-start(bf16[256,256]{1,0:T(8,128)(2,1)S(1)} %constant_dynamic-update-slice_fusion), channel_id=1, source_target_pairs={{0,4},{2,6},{4,8},{6,10},{8,12},{10,14},{1,5},{3,7},{5,9},{7,11},{... | collective-permute-start | bytes 393224 | tf_op jit(solution)/shard_map/ppermute | solution.py:13
  5.9 1.9 %collective-permute-start.1 = (bf16[256,256]{1,0:T(8,128)(2,1)S(1)}, bf16[256,256]{1,0:T(8,128)(2,1)}, u32[]{:S(2)}, u32[]{:S(2)}) collective-permute-start(bf16[256,256]{1,0:T(8,128)(2,1)S(1)} %constant_dynamic-update-slice_fusion), channel_id=1, source_target_pairs={{0,2},{2,4},{4,6},{6,8},{8,10},{10,12},{12,14},{1,3},{3,5},{5,7},{... | collective-permute-start | bytes 393224 | tf_op jit(solution)/shard_map/ppermute | solution.py:13
  7.9 3.9 %collective-permute-start.2 = (bf16[256,256]{1,0:T(8,128)(2,1)S(1)}, bf16[256,256]{1,0:T(8,128)(2,1)}, u32[]{:S(2)}, u32[]{:S(2)}) collective-permute-start(bf16[256,256]{1,0:T(8,128)(2,1)S(1)} %constant_dynamic-update-slice_fusion), channel_id=1, source_target_pairs={{2,0},{4,2},{6,4},{8,6},{10,8},{12,10},{14,12},{3,1},{5,3},{7,5},{... | collective-permute-start | bytes 393224 | tf_op jit(solution)/shard_map/ppermute | solution.py:13
  11.8 2.4 %collective-permute-start.3 = (bf16[256,256]{1,0:T(8,128)(2,1)S(1)}, bf16[256,256]{1,0:T(8,128)(2,1)}, u32[]{:S(2)}, u32[]{:S(2)}) collective-permute-start(bf16[256,256]{1,0:T(8,128)(2,1)S(1)} %constant_dynamic-update-slice_fusion), channel_id=1, source_target_pairs={{4,0},{6,2},{8,4},{10,6},{12,8},{14,10},{5,1},{7,3},{9,5},{11,7},{... | collective-permute-start | bytes 393224 | tf_op jit(solution)/shard_map/ppermute | solution.py:13
  14.2 0.1 broadcast_multiply_fusion
  14.5 0.7 %copy.30 = s32[16,1]{1,0:T(8,128)S(1)} copy(s32[16,1]{0,1:T(1,128)} %bitcast.209) | data formatting | bytes 128 | tf_op jit(solution)/shard_map/reshape.246
  15.3 0.1 reduce.3
  15.4 0.7 %sub.78 = s32[16]{0:T(128)S(1)} subtract(s32[16]{0:T(128)S(1)} %reduce.3, s32[16]{0:T(128)} %param.9) | non-fusion elementwise | flops 16 | bytes 192 | tf_op jit(solution)/shard_map/sub | solution.py:17
  16.0 0.1 convert_reduce_fusion
  16.3 0.1 convert_reduce_fusion.1
  16.4 1.1 %convert_bitcast_fusion = f32[32,8,8,128]{3,1,2,0:T(8,128)S(1)} fusion(bf16[256,1024]{1,0:T(8,128)(2,1)} %param.8), kind=kLoop, calls=%fused_computation.25 | loop fusion | flops 262144 | bytes 1572864
  17.6 0.1 pad.5.clone
  17.7 1.3 %pad_maximum_fusion = f32[11,128,256]{2,1,0:T(8,128)} fusion(f32[3,128,256]{2,1,0:T(8,128)S(1)} %broadcast_in_dim.82, f32[11]{0:T(128)S(1)} %pad.5.clone), kind=kLoop, calls=%fused_computation.15 | loop fusion | flops 720896 | bytes 1835052 | tf_op jit(solution)/shard_map/concatenate | solution.py:138
  19.0 0.3 compare_and_fusion
  19.3 0.1 copy.56
  19.4 0.9 %copy.58 = bf16[32,8,8,128]{3,2,1,0:T(8,128)(2,1)} copy(bf16[32,8,8,128]{3,1,2,0:T(8,128)(2,1)S(1)} %bitcast.189) | data formatting | bytes 1048576
  20.3 0.2 copy.59
  20.5 1.3 %copy.36 = f32[2,128,1,8,128]{1,4,3,0,2:T(8,128)} copy(f32[2,128,1,8,128]{4,3,1,0,2:T(8,128)S(1)} %bitcast.186) | data formatting | bytes 2097152 | tf_op jit(solution)/shard_map/convert_element_type | solution.py:103
  21.8 0.9 %constant_dynamic-update-slice_fusion.5 = bf16[5,256,256]{2,1,0:T(8,128)(2,1)S(1)} fusion(bf16[5,256,256]{2,1,0:T(8,128)(2,1)S(1)} %constant_dynamic-update-slice_fusion.6, bf16[256,256]{1,0:T(8,128)(2,1)} %collective-permute-done.1), kind=kLoop, calls=%fused_computation.78 | loop fusion | bytes 262144
  22.8 0.9 %constant_dynamic-update-slice_fusion.3 = bf16[5,256,256]{2,1,0:T(8,128)(2,1)S(1)} fusion(bf16[5,256,256]{2,1,0:T(8,128)(2,1)S(1)} %constant_dynamic-update-slice_fusion.4, bf16[256,256]{1,0:T(8,128)(2,1)} %collective-permute-done.2), kind=kLoop, calls=%fused_computation.76 | loop fusion | bytes 262144
  23.7 0.9 %constant_dynamic-update-slice_fusion.2 = bf16[5,256,256]{2,1,0:T(8,128)(2,1)S(1)} fusion(bf16[5,256,256]{2,1,0:T(8,128)(2,1)S(1)} %constant_dynamic-update-slice_fusion.3, bf16[256,256]{1,0:T(8,128)(2,1)} %collective-permute-done.3), kind=kLoop, calls=%fused_computation.75 | loop fusion | bytes 262144 | tf_op jit(solution)/shard_map/stack | solution.py:28
  24.7 1.1 %fusion.42 = (bf16[3,128,256]{2,1,0:T(8,128)(2,1)S(1)}, bf16[3,128,256]{2,1,0:T(8,128)(2,1)S(1)}) fusion(s32[]{:T(128)S(6)} %select_n.33, bf16[3,128,256]{2,1,0:T(8,128)(2,1)S(1)} %broadcast_in_dim.49, bf16[5,128,256]{2,1,0:T(8,128)(2,1)S(1)} %rev.13, bf16[1,256,256]{2,1,0:T(8,128)(2,1)} %bitcast.5, bf16[1,256,256]{2,1,0:T(8,128)(2,1)} %bitcast.4, ...), kind=kLoop, calls=%fused_computation.57 | loop fusion | flops 1867776 | bytes 1572871 | tf_op jit(solution)/shard_map/jit(_where)/select_n | solution.py:66
  25.8 0.6 %fusion.3 = (f32[2,128,8]{1,2,0:T(8,128)S(1)}, f32[2,384,128,8]{2,1,3,0:T(8,128)S(1)}) fusion(pred[2,128,384]{1,2,0:T(8,128)(4,1)S(1)} %compare_and_fusion, bf16[2,128,8,128]{3,2,1,0:T(8,128)(2,1)S(1)} %bitcast.184, bf16[1,384,256]{2,1,0:T(8,128)(2,1)S(1)} %bitcast.196, bf16[1,384,256]{2,1,0:T(8,128)(2,1)S(1)} %bitcast.192), kind=kOutput, calls=%fused_computation.8 | convolution fusion | flops 204077056 | bytes 4169728 | tf_op jit(solution)/shard_map/sqgjd,skgd->sqgjk/dot_general | solution.py:90
  26.4 0.7 %exponential_reduce_fusion = f32[2,128,8]{1,2,0:T(8,128)S(1)} fusion(f32[2,384,128,8]{2,1,3,0:T(8,128)S(1)} %get-tuple-element.21, f32[2,128,8]{1,2,0:T(8,128)S(1)} %get-tuple-element.20, pred[2,128,384]{1,2,0:T(8,128)(4,1)S(1)} %compare_and_fusion), kind=kLoop, calls=%fused_computation.7 | loop fusion | flops 3143680 | bytes 3260416 | tf_op jit(solution)/shard_map/reduce_sum | solution.py:95
  27.1 0.8 %fusion.26 = f32[2,384,128,1]{2,1,3,0:T(8,128)S(1)} fusion(bf16[2,128,8,128]{3,2,1,0:T(8,128)(2,1)S(1)} %bitcast.204, f32[2,384,128,8]{2,1,3,0:T(8,128)S(1)} %get-tuple-element.21, f32[2,128,8]{1,2,0:T(8,128)S(1)} %log_add_fusion, pred[2,128,384]{1,2,0:T(8,128)(4,1)S(1)} %compare_and_fusion), kind=kOutput, calls=%fused_computation.35 | convolution fusion | flops 204472320 | bytes 4169728 | tf_op jit(solution)/shard_map/sqgjk,sqgjd->skgd/dot_general | solution.py:123
  28.0 0.3 copy-done.2
  28.3 1.7 %multiply_reduce_fusion = (f32[2,128,8]{1,2,0:T(8,128)S(1)}, bf16[2,128,1,8,128]{1,4,3,0,2:T(8,128)(2,1)}) fusion(f32[2,128,1,8,128]{1,4,3,0,2:T(8,128)S(1)} %copy-done.2, f32[2,384,128,8]{2,1,3,0:T(8,128)S(1)} %get-tuple-element.21, f32[2,128,8]{1,2,0:T(8,128)S(1)} %log_add_fusion, pred[2,128,384]{1,2,0:T(8,128)(4,1)S(1)} %compare_and_fusion, ...), kind=kOutput, calls=%fused_computation.26 | convolution fusion | flops 205912064 | bytes 5226496 | tf_op jit(solution)/shard_map/sqgjk,skgd->sqgjd/dot_general | solution.py:98
  30.1 1.1 %fusion = bf16[2,128,1,8,384]{1,4,3,0,2:T(8,128)(2,1)S(1)} fusion(f32[2,384,128,8]{2,1,3,0:T(8,128)S(1)} %get-tuple-element.21, f32[2,128,8]{1,2,0:T(8,128)S(1)} %get-tuple-element.22, f32[2,128,8]{1,2,0:T(8,128)S(1)} %log_add_fusion, pred[2,128,384]{1,2,0:T(8,128)(4,1)S(1)} %compare_and_fusion, bf16[2,128,8,128]{3,2,1,0:T(8,128)(2,1)S(1)} %bitcast.205, ...), kind=kOutput, calls=%fused_computation.1 | convolution fusion | flops 206438400 | bytes 5750784 | tf_op jit(solution)/shard_map/sqgjd,skgd->sqgjk/dot_general | solution.py:105
  31.2 0.6 %fusion.23 = f32[2,384,128]{2,1,0:T(8,128)S(1)} fusion(bf16[2,128,1,8,384]{1,4,3,0,2:T(8,128)(2,1)S(1)} %fusion, bf16[2,128,8,128]{3,2,1,0:T(8,128)(2,1)S(1)} %bitcast.185), kind=kOutput, calls=%fused_computation.24 | convolution fusion | flops 201424896 | bytes 2490368 | tf_op jit(solution)/shard_map/sqgjk,sqgjd->skgd/dot_general | solution.py:120
  31.8 0.9 %broadcast_select_fusion.1 = (f32[3,128,256]{2,1,0:T(8,128)}, f32[3,128,256]{2,1,0:T(8,128)S(1)}) fusion(pred[3]{0:T(512)(128)(4,1)S(1)} %add_compare_fusion, f32[2,3,128,128]{3,2,1,0:T(8,128)S(1)} %bitcast.201, f32[2,3,128,128]{3,2,1,0:T(8,128)S(1)} %bitcast.188), kind=kLoop, calls=%fused_computation.67 | loop fusion | flops 294912 | bytes 1572867 | tf_op jit(solution)/shard_map/jit(_where)/select_n | solution.py:135
  32.7 0.5 fusion.17
  33.3 1.0 %reverse_dynamic-update-slice_fusion = f32[11,128,256]{2,1,0:T(8,128)S(1)} fusion(f32[11,128,256]{2,1,0:T(8,128)S(1)} %copy-done, s32[]{:T(128)S(6)} %select_n.39, f32[3,128,256]{2,1,0:T(8,128)} %get-tuple-element.6), kind=kLoop, calls=%fused_computation.47 | loop fusion | bytes 786436 | tf_op jit(solution)/shard_map/dynamic_update_slice | solution.py:142
  34.3 0.1 slice_add_fusion
  34.5 0.8 %slice_bitcast_fusion.4 = (bf16[256,256]{1,0:T(8,128)(2,1)}, bf16[256,256]{1,0:T(8,128)(2,1)}, bf16[256,256]{1,0:T(8,128)(2,1)}, bf16[256,256]{1,0:T(8,128)(2,1)}) fusion(bf16[5,256,256]{2,1,0:T(8,128)(2,1)S(1)} %fusion.59), kind=kLoop, calls=%fused_computation.71 | loop fusion | bytes 1048576 | tf_op jit(solution)/shard_map/convert_element_type | solution.py:36
  35.3 3.0 %collective-permute-start.4 = (bf16[256,256]{1,0:T(8,128)(2,1)}, bf16[256,256]{1,0:T(8,128)(2,1)S(1)}, u32[]{:S(2)}, u32[]{:S(2)}) collective-permute-start(bf16[256,256]{1,0:T(8,128)(2,1)} %get-tuple-element.8), channel_id=1, source_target_pairs={{4,0},{6,2},{8,4},{10,6},{12,8},{14,10},{5,1},{7,3},{9,5},{11,7},{... | collective-permute-start | bytes 393224 | tf_op jit(solution)/shard_map/ppermute | solution.py:13
  38.3 2.2 %collective-permute-start.5 = (bf16[256,256]{1,0:T(8,128)(2,1)}, bf16[256,256]{1,0:T(8,128)(2,1)S(1)}, u32[]{:S(2)}, u32[]{:S(2)}) collective-permute-start(bf16[256,256]{1,0:T(8,128)(2,1)} %get-tuple-element.11), channel_id=1, source_target_pairs={{2,0},{4,2},{6,4},{8,6},{10,8},{12,10},{14,12},{3,1},{5,3},{7,5},{... | collective-permute-start | bytes 393224 | tf_op jit(solution)/shard_map/ppermute | solution.py:13
  40.5 4.5 %collective-permute-start.6 = (bf16[256,256]{1,0:T(8,128)(2,1)}, bf16[256,256]{1,0:T(8,128)(2,1)S(1)}, u32[]{:S(2)}, u32[]{:S(2)}) collective-permute-start(bf16[256,256]{1,0:T(8,128)(2,1)} %get-tuple-element.10), channel_id=1, source_target_pairs={{0,2},{2,4},{4,6},{6,8},{8,10},{10,12},{12,14},{1,3},{3,5},{5,7},{... | collective-permute-start | bytes 393224 | tf_op jit(solution)/shard_map/ppermute | solution.py:13
  45.0 1.9 %collective-permute-start.7 = (bf16[256,256]{1,0:T(8,128)(2,1)}, bf16[256,256]{1,0:T(8,128)(2,1)S(1)}, u32[]{:S(2)}, u32[]{:S(2)}) collective-permute-start(bf16[256,256]{1,0:T(8,128)(2,1)} %get-tuple-element.9), channel_id=1, source_target_pairs={{0,4},{2,6},{4,8},{6,10},{8,12},{10,14},{1,5},{3,7},{5,9},{7,11},{... | collective-permute-start | bytes 393224 | tf_op jit(solution)/shard_map/ppermute | solution.py:13
  46.9 0.3 copy.39
  47.2 0.9 %copy.75 = bf16[32,8,8,128]{3,1,2,0:T(8,128)(2,1)} copy(bf16[32,8,8,128]{3,2,1,0:T(8,128)(2,1)S(1)} %bitcast.190) | data formatting | bytes 1048576
  48.1 0.3 copy.34
  48.5 0.9 %copy.76 = bf16[32,8,8,128]{3,1,2,0:T(8,128)(2,1)} copy(bf16[32,8,8,128]{3,2,1,0:T(8,128)(2,1)S(1)} %bitcast.191) | data formatting | bytes 1048576
  49.4 0.1 select_maximum_fusion
  49.5 2.6 %collective-permute-done.7 = bf16[256,256]{1,0:T(8,128)(2,1)S(1)} collective-permute-done((bf16[256,256]{1,0:T(8,128)(2,1)}, bf16[256,256]{1,0:T(8,128)(2,1)S(1)}, u32[]{:S(2)}, u32[]{:S(2)}) %collective-permute-start.7) | collective-permute-done | bytes 131104 | tf_op jit(solution)/shard_map/ppermute | solution.py:13
  52.1 0.1 fusion.39
  52.2 0.7 %fusion.60 = (bf16[256,128]{1,0:T(8,128)(2,1)}, bf16[256,128]{1,0:T(8,128)(2,1)}) fusion(bf16[256,256]{1,0:T(8,128)(2,1)S(1)} %fusion.39), kind=kLoop, calls=%fused_computation.103 | loop fusion | bytes 262144 | tf_op jit(solution)/shard_map/slice | solution.py:149
  (43 shorter events, 0.8 us)
Async XLA Ops:
  0.6 18.8 %copy-start.1 = (bf16[256,1024]{1,0:T(8,128)(2,1)S(1)}, bf16[256,1024]{1,0:T(8,128)(2,1)}, u32[]{:S(2)}) copy-start(bf16[256,1024]{1,0:T(8,128)(2,1)} %param.8) | copy-start | bytes 1572868
  0.6 18.6 %copy-start.3 = (bf16[256,1024]{1,0:T(8,128)(2,1)S(1)}, bf16[256,1024]{1,0:T(8,128)(2,1)}, u32[]{:S(2)}) copy-start(bf16[256,1024]{1,0:T(8,128)(2,1)} %param.5) | copy-start | bytes 1572868
  2.5 19.4 %collective-permute-start = (bf16[256,256]{1,0:T(8,128)(2,1)S(1)}, bf16[256,256]{1,0:T(8,128)(2,1)S(1)}, u32[]{:S(2)}, u32[]{:S(2)}) collective-permute-start(bf16[256,256]{1,0:T(8,128)(2,1)S(1)} %constant_dynamic-update-slice_fusion), channel_id=1, source_target_pairs={{0,4},{2,6},{4,8},{6,10},{8,12},{10,14},{1,5},{3,7},{5,9},{7,11},{... | collective-permute-start | bytes 393224 | tf_op jit(solution)/shard_map/ppermute | solution.py:13
  5.9 15.9 %collective-permute-start.1 = (bf16[256,256]{1,0:T(8,128)(2,1)S(1)}, bf16[256,256]{1,0:T(8,128)(2,1)}, u32[]{:S(2)}, u32[]{:S(2)}) collective-permute-start(bf16[256,256]{1,0:T(8,128)(2,1)S(1)} %constant_dynamic-update-slice_fusion), channel_id=1, source_target_pairs={{0,2},{2,4},{4,6},{6,8},{8,10},{10,12},{12,14},{1,3},{3,5},{5,7},{... | collective-permute-start | bytes 393224 | tf_op jit(solution)/shard_map/ppermute | solution.py:13
  7.9 14.9 %collective-permute-start.2 = (bf16[256,256]{1,0:T(8,128)(2,1)S(1)}, bf16[256,256]{1,0:T(8,128)(2,1)}, u32[]{:S(2)}, u32[]{:S(2)}) collective-permute-start(bf16[256,256]{1,0:T(8,128)(2,1)S(1)} %constant_dynamic-update-slice_fusion), channel_id=1, source_target_pairs={{2,0},{4,2},{6,4},{8,6},{10,8},{12,10},{14,12},{3,1},{5,3},{7,5},{... | collective-permute-start | bytes 393224 | tf_op jit(solution)/shard_map/ppermute | solution.py:13
  11.8 11.9 %collective-permute-start.3 = (bf16[256,256]{1,0:T(8,128)(2,1)S(1)}, bf16[256,256]{1,0:T(8,128)(2,1)}, u32[]{:S(2)}, u32[]{:S(2)}) collective-permute-start(bf16[256,256]{1,0:T(8,128)(2,1)S(1)} %constant_dynamic-update-slice_fusion), channel_id=1, source_target_pairs={{4,0},{6,2},{8,4},{10,6},{12,8},{14,10},{5,1},{7,3},{9,5},{11,7},{... | collective-permute-start | bytes 393224 | tf_op jit(solution)/shard_map/ppermute | solution.py:13
  25.8 1.3 %copy-start.4 = (bf16[32,8,8,128]{3,2,1,0:T(8,128)(2,1)S(1)}, bf16[32,8,8,128]{3,2,1,0:T(8,128)(2,1)}, u32[]{:S(2)}) copy-start(bf16[32,8,8,128]{3,2,1,0:T(8,128)(2,1)} %copy.58) | copy-start | bytes 1572868
  27.1 1.2 %copy-start.2 = (f32[2,128,1,8,128]{1,4,3,0,2:T(8,128)S(1)}, f32[2,128,1,8,128]{1,4,3,0,2:T(8,128)}, u32[]{:S(2)}) copy-start(f32[2,128,1,8,128]{1,4,3,0,2:T(8,128)} %copy.36) | copy-start | bytes 3145732
  31.8 1.5 %copy-start = (f32[11,128,256]{2,1,0:T(8,128)S(1)}, f32[11,128,256]{2,1,0:T(8,128)}, u32[]{:S(2)}) copy-start(f32[11,128,256]{2,1,0:T(8,128)} %pad_maximum_fusion) | copy-start | bytes 4325380
  34.4 13.7 %copy-start.5 = (bf16[2,128,1,8,128]{1,4,3,0,2:T(8,128)(2,1)S(1)}, bf16[2,128,1,8,128]{1,4,3,0,2:T(8,128)(2,1)}, u32[]{:S(2)}) copy-start(bf16[2,128,1,8,128]{1,4,3,0,2:T(8,128)(2,1)} %get-tuple-element.23) | copy-start | bytes 1572868
  35.3 14.2 %collective-permute-start.4 = (bf16[256,256]{1,0:T(8,128)(2,1)}, bf16[256,256]{1,0:T(8,128)(2,1)S(1)}, u32[]{:S(2)}, u32[]{:S(2)}) collective-permute-start(bf16[256,256]{1,0:T(8,128)(2,1)} %get-tuple-element.8), channel_id=1, source_target_pairs={{4,0},{6,2},{8,4},{10,6},{12,8},{14,10},{5,1},{7,3},{9,5},{11,7},{... | collective-permute-start | bytes 393224 | tf_op jit(solution)/shard_map/ppermute | solution.py:13
  38.3 11.2 %collective-permute-start.5 = (bf16[256,256]{1,0:T(8,128)(2,1)}, bf16[256,256]{1,0:T(8,128)(2,1)S(1)}, u32[]{:S(2)}, u32[]{:S(2)}) collective-permute-start(bf16[256,256]{1,0:T(8,128)(2,1)} %get-tuple-element.11), channel_id=1, source_target_pairs={{2,0},{4,2},{6,4},{8,6},{10,8},{12,10},{14,12},{3,1},{5,3},{7,5},{... | collective-permute-start | bytes 393224 | tf_op jit(solution)/shard_map/ppermute | solution.py:13
  40.5 9.0 %collective-permute-start.6 = (bf16[256,256]{1,0:T(8,128)(2,1)}, bf16[256,256]{1,0:T(8,128)(2,1)S(1)}, u32[]{:S(2)}, u32[]{:S(2)}) collective-permute-start(bf16[256,256]{1,0:T(8,128)(2,1)} %get-tuple-element.10), channel_id=1, source_target_pairs={{0,2},{2,4},{4,6},{6,8},{8,10},{10,12},{12,14},{1,3},{3,5},{5,7},{... | collective-permute-start | bytes 393224 | tf_op jit(solution)/shard_map/ppermute | solution.py:13
  45.0 7.1 %collective-permute-start.7 = (bf16[256,256]{1,0:T(8,128)(2,1)}, bf16[256,256]{1,0:T(8,128)(2,1)S(1)}, u32[]{:S(2)}, u32[]{:S(2)}) collective-permute-start(bf16[256,256]{1,0:T(8,128)(2,1)} %get-tuple-element.9), channel_id=1, source_target_pairs={{0,4},{2,6},{4,8},{6,10},{8,12},{10,14},{1,5},{3,7},{5,9},{7,11},{... | collective-permute-start | bytes 393224 | tf_op jit(solution)/shard_map/ppermute | solution.py:13
where the time goes:
time: 53.5 us; the launch traced here: 52.8 us
  starting transfers between devices  23.3 us (44%)
  local copies, waits for them, and re-layouts  13.4 us (25%)
  other arithmetic  7.09 us (13%)
  matrix products  5.35 us (10%)
  waiting for transfers between devices  2.6 us (5%)
  between operations  1.07 us (2%)
    ppermute x8, starting transfers between devices, from_behind(): return lax.ppermute(value, axis, pairs)  23.3 us
    unnamed x23, local copies, waits for them, and re-layouts  6.25 us
    ppermute x8, waiting for transfers between devices, from_behind(): return lax.ppermute(value, axis, pairs)  2.6 us
    dot_general x1, matrix products, shards(): jnp.einsum('sqgjk,skgd->sqgjd', weights_low, value_block, preferred_eleme...  1.74 us
    convert_element_type x1, local copies, waits for them, and re-layouts, shards(): grad_group.astype(jnp.float32) * attended_group.astype(jnp.float32)  1.32 us
    concatenate x1, other arithmetic, shards(): jnp.concatenate([margin, jnp.zeros((2 * band_reach + 1, stretch_len, 2 *...  1.31 us
    unnamed x1, other arithmetic  1.15 us
    dot_general x1, matrix products, shards(): jnp.einsum('sqgjd,skgd->sqgjk', grad_group, value_block, preferred_elemen...  1.11 us
  transfers between devices with their start and end apart: 8, of which 1 were waited for; matrix products, arithmetic and copies ran while one was open for 23% of the time, Pallas kernels for 0%

commit v1 on v0

v1 whole, which is shorter than its diff:
```python
import math

import jax
import jax.numpy as jnp
from jax import lax
from jax.experimental import pallas as pl
from jax.experimental.pallas import tpu as pltpu
from jax.sharding import PartitionSpec as P

HEAD_DIM = 128
DOC_STRETCHES = 8
MASKED = -1e30


def exchanges(ctx_count, reach):
    sets = []
    for offset in range(1, reach + 1):
        for colour in range(2):
            firsts = [b for b in range(ctx_count - offset) if (b // offset) % 2 == colour]
            if firsts:
                full = any(2 * b >= 2 * ctx_count - 1 - reach - offset for b in firsts)
                sets.append((offset, colour, full, tuple(firsts)))
    return sets


def swap(value, exchange, ctx_count, head_count):
    offset, _, _, firsts = exchange
    partner = {b: b + offset for b in firsts}
    partner.update({b + offset: b for b in firsts})
    pairs = []
    for b in range(ctx_count):
        for h in range(head_count):
            if b in partner:
                pairs.append((b * head_count + h, partner[b] * head_count + h))
            else:
                pairs.append((b * head_count + h, b * head_count + (h + 1) % head_count))
    return lax.ppermute(value, ("ctx", "head"), pairs)


def fold_offsets(slot):
    return range(-(slot - 1), slot, 2)


def pack_kernel(sets, k_ref, v_ref, *out_refs):
    me = lax.axis_index("ctx")
    length = k_ref.shape[0] // 2
    width = k_ref.shape[1]
    for (offset, colour, full, _), out in zip(sets, out_refs):
        if full:
            out[:, :width] = k_ref[...]
            out[:, width:] = v_ref[...]
        else:
            first = (me // offset) % 2 == colour
            start = pl.multiple_of(jnp.where(first, 0, length), length)
            out[:, :width] = k_ref[pl.ds(start, length), :]
            out[:, width:] = v_ref[pl.ds(start, length), :]


def main_kernel(sets, ctx_count, reach, docs_ref, q_ref, g_ref, k_ref, v_ref, *refs):
    count = len(sets)
    recs = {(s[0], s[1]): (r, s[2]) for s, r in zip(sets, refs[:count])}
    att_ref, dq_ref, own_ref = refs[count : count + 3]
    sends = {(s[0], s[1]): (r, s[2]) for s, r in zip(sets, refs[count + 3 : 2 * count + 3])}
    kv_win, bias, pb, dsb, acc, extra = refs[2 * count + 3 :]
    me = lax.axis_index("ctx")
    length = k_ref.shape[0] // 2
    width = HEAD_DIM
    heads = q_ref.shape[1] // width
    span = (reach + 1) * length
    scaling = width ** (-0.5)
    log_scale = scaling * math.log2(math.e)

    def low_part(key):
        ref, full = recs[key]
        return ref[:length, :] if full else ref[...]

    def up_part(key):
        ref, full = recs[key]
        return ref[length:, :] if full else ref[...]

    def choose(pred, a, b):
        return jnp.where(pred, a, b)

    def pick(part, offset, colour_pred):
        have = [c for c in range(2) if (offset, c) in recs]
        if len(have) == 1:
            return part((offset, have[0]))
        return choose(colour_pred, part((offset, 1)), part((offset, 0)))

    def own(half):
        rows = slice(half * length, (half + 1) * length)
        return jnp.concatenate([k_ref[rows, :], v_ref[rows, :]], axis=1)

    lows = [own(0)]
    highs = [own(1)]
    for slot in range(1, reach + 1):
        odd = (me // slot) % 2 == 1
        lows.append(pick(low_part, slot, jnp.logical_not(odd)))
        value = pick(up_part, slot, odd)
        highs.append(value)
    for slot in range(1, reach + 1):
        folded = me + slot >= ctx_count
        value = highs[slot]
        for offset in fold_offsets(slot):
            here = folded & (2 * ctx_count - 1 - 2 * me - slot == offset)
            if offset <= 0:
                value = choose(here, lows[-offset], value)
            else:
                for colour in range(2):
                    if recs.get((offset, colour), (None, False))[1]:
                        mine = here & ((me // offset) % 2 == colour)
                        value = choose(mine, low_part((offset, colour)), value)
        highs[slot] = value
    for slot in range(reach + 1):
        rows = slice(slot * length, (slot + 1) * length)
        kv_win[0, rows, :] = lows[slot]
        kv_win[1, rows, :] = highs[slot]

    row = lax.broadcasted_iota(jnp.int32, (span, length), 0)
    col = lax.broadcasted_iota(jnp.int32, (1, length), 1)
    group = 2 if heads % 2 == 0 else 1
    for s in range(2):
        stretch = me if s == 0 else 2 * ctx_count - 1 - me
        q_pos = stretch * length + col
        start = jnp.int32(0)
        doc_start = jnp.zeros((1, length), jnp.int32)
        for i in range(docs_ref.shape[0]):
            doc_start = jnp.where(q_pos >= start, start, doc_start)
            start = start + docs_ref[i]
        k_pos = row + (stretch - 2 * (row // length)) * length
        allowed = (k_pos >= doc_start) & (k_pos <= q_pos)
        bias[...] = jnp.where(allowed, 0.0, MASKED)
        k_win = kv_win[s, :, :width]
        v_win = kv_win[s, :, width:]
        k_turn = k_win.T
        v_turn = v_win.T
        rows = slice(s * length, (s + 1) * length)
        for h in range(0, heads, group):
            cols = [slice((h + i) * width, (h + i + 1) * width) for i in range(group)]
            lanes = slice(h * length, (h + group) * length)
            q_pair = jnp.concatenate([q_ref[rows, c] for c in cols], axis=0)
            g_pair = jnp.concatenate([g_ref[rows, c] for c in cols], axis=0)
            contract_last = (((1,), (1,)), ((), ()))
            raw = lax.dot_general(k_win, q_pair, contract_last, preferred_element_type=jnp.float32)
            d_p = lax.dot_general(v_win, g_pair, contract_last, preferred_element_type=jnp.float32)
            shift = bias[...]
            raw = raw + jnp.concatenate([shift] * group, axis=1)
            top = jnp.max(raw, axis=0, keepdims=True)
            weight = jnp.exp2((raw - top) * log_scale)
            total = jnp.sum(weight, axis=0, keepdims=True)
            weight = weight * (1.0 / total)
            delta = jnp.sum(weight * d_p, axis=0, keepdims=True)
            low = weight.astype(jnp.bfloat16)
            d_s = (weight * (d_p - delta)).astype(jnp.bfloat16)
            pb[s, :, lanes] = low
            dsb[s, :, lanes] = d_s
            out_t = jnp.dot(v_turn, low, preferred_element_type=jnp.float32).astype(jnp.bfloat16)
            dq_t = jnp.dot(k_turn, d_s, preferred_element_type=jnp.float32) * scaling
            dq_t = dq_t.astype(jnp.bfloat16)
            for i in range(group):
                part = slice(i * length, (i + 1) * length)
                att_ref[rows, cols[i]] = out_t[:, part].T
                dq_ref[rows, cols[i]] = dq_t[:, part].T
        q_all = jnp.concatenate(
            [q_ref[rows, h * width : (h + 1) * width] for h in range(heads)], axis=0
        )
        g_all = jnp.concatenate(
            [g_ref[rows, h * width : (h + 1) * width] for h in range(heads)], axis=0
        )
        d_k = jnp.dot(dsb[s], q_all, preferred_element_type=jnp.float32) * scaling
        d_v = jnp.dot(pb[s], g_all, preferred_element_type=jnp.float32)
        acc[s, :, :width] = d_k
        acc[s, :, width:] = d_v

    def slot_rows(slot):
        return slice(slot * length, (slot + 1) * length)

    extra[...] = jnp.zeros(extra.shape, jnp.float32)
    for slot in range(1, reach + 1):
        for offset in fold_offsets(slot):

            @pl.when((me + slot >= ctx_count) & (2 * ctx_count - 1 - 2 * me - slot == offset))
            def _():
                part = acc[1, slot_rows(slot), :]
                if offset <= 0:
                    acc[0, slot_rows(-offset), :] = acc[0, slot_rows(-offset), :] + part
                else:
                    extra[slot_rows(offset - 1), :] = part

    own_ref[:length, :] = acc[0, :length, :]
    own_ref[length:, :] = acc[1, :length, :]
    for (offset, colour), (ref, full) in sends.items():
        first = (me // offset) % 2 == colour
        to_low = acc[0, slot_rows(offset), :]
        to_up = acc[1, slot_rows(offset), :]
        if full:
            more = extra[slot_rows(offset - 1), :]
            ref[:length, :] = jnp.where(first, more, to_low).astype(jnp.bfloat16)
            ref[length:, :] = jnp.where(first, to_up, 0.0).astype(jnp.bfloat16)
        else:
            ref[...] = jnp.where(first, to_up, to_low).astype(jnp.bfloat16)


def sum_kernel(sets, ctx_count, own_ref, *refs):
    dk_ref, dv_ref = refs[len(sets) :]
    me = lax.axis_index("ctx")
    length = own_ref.shape[0] // 2
    width = dk_ref.shape[1]
    low = own_ref[:length, :]
    up = own_ref[length:, :]
    for (offset, colour, full, _), ref in zip(sets, refs):
        first = (me // offset) % 2 == colour
        as_first = first & (me + offset < ctx_count)
        as_second = jnp.logical_not(first) & (me >= offset)
        if full:
            low = low + jnp.where(as_first | as_second, ref[:length, :].astype(jnp.float32), 0.0)
            up = up + jnp.where(as_second, ref[length:, :].astype(jnp.float32), 0.0)
        else:
            part = ref[...].astype(jnp.float32)
            low = low + jnp.where(as_first, part, 0.0)
            up = up + jnp.where(as_second, part, 0.0)
    dk_ref[:length, :] = low[:, :width].astype(jnp.bfloat16)
    dk_ref[length:, :] = up[:, :width].astype(jnp.bfloat16)
    dv_ref[:length, :] = low[:, width:].astype(jnp.bfloat16)
    dv_ref[length:, :] = up[:, width:].astype(jnp.bfloat16)


def in_vmem(amount):
    return [pl.BlockSpec(memory_space=pltpu.VMEM)] * amount


def shards(query_rows, key_rows, value_rows, out_grad, doc_lengths):
    ctx_count = lax.axis_size("ctx")
    head_count = lax.axis_size("head")
    tok_dev = query_rows.shape[0]
    length = tok_dev // 2
    width = key_rows.shape[1]
    reach = min(DOC_STRETCHES, ctx_count // 4)
    span = (reach + 1) * length
    heads = query_rows.shape[1] // width
    sets = exchanges(ctx_count, reach)
    payloads = [
        jax.ShapeDtypeStruct((2 * length if s[2] else length, 2 * width), jnp.bfloat16)
        for s in sets
    ]
    count = len(sets)

    packed = pl.pallas_call(
        lambda *refs: pack_kernel(sets, *refs),
        out_shape=payloads,
        in_specs=in_vmem(2),
        out_specs=in_vmem(count),
        name="pack",
    )(key_rows, value_rows)
    received = [swap(p, s, ctx_count, head_count) for p, s in zip(packed, sets)]

    results = pl.pallas_call(
        lambda *refs: main_kernel(sets, ctx_count, reach, *refs),
        out_shape=[
            jax.ShapeDtypeStruct(query_rows.shape, jnp.bfloat16),
            jax.ShapeDtypeStruct(query_rows.shape, jnp.bfloat16),
            jax.ShapeDtypeStruct((tok_dev, 2 * width), jnp.float32),
        ]
        + payloads,
        in_specs=[pl.BlockSpec(memory_space=pltpu.SMEM)] + in_vmem(4 + count),
        out_specs=in_vmem(3 + count),
        scratch_shapes=[
            pltpu.VMEM((2, span, 2 * width), jnp.bfloat16),
            pltpu.VMEM((span, length), jnp.float32),
            pltpu.VMEM((2, span, heads * length), jnp.bfloat16),
            pltpu.VMEM((2, span, heads * length), jnp.bfloat16),
            pltpu.VMEM((2, span, 2 * width), jnp.float32),
            pltpu.VMEM((reach * length, 2 * width), jnp.float32),
        ],
        name="attend",
    )(doc_lengths, query_rows, out_grad, key_rows, value_rows, *received)
    attended, query_grad, own = results[:3]
    returned = [swap(p, s, ctx_count, head_count) for p, s in zip(results[3:], sets)]

    key_grad, value_grad = pl.pallas_call(
        lambda *refs: sum_kernel(sets, ctx_count, *refs),
        out_shape=[jax.ShapeDtypeStruct(key_rows.shape, jnp.bfloat16)] * 2,
        in_specs=in_vmem(1 + count),
        out_specs=in_vmem(2),
        name="total",
    )(own, *returned)
    return (attended, query_grad, key_grad, value_grad)


def solution(mesh):
    placed = (
        P(("groups", "ctx"), "head"),
        P(("groups", "ctx"), "head"),
        P(("groups", "ctx"), "head"),
        P(("groups", "ctx"), "head"),
        P("groups"),
    )
    return jax.shard_map(
        shards,
        mesh=mesh,
        in_specs=placed,
        out_specs=(P(("groups", "ctx"), "head"),) * 4,
        check_vma=False,
    )
```

time: 53.5 us -> 29.7 us (0.56)
  the two profiles are of different devices: /device:TPU:22 before, /device:TPU:0 now
where the time goes in v1:
time: 29.7 us; the launch traced here: 29.5 us
  Pallas kernels  10.9 us (37%)
  starting transfers between devices  8.68 us (29%)
  waiting for transfers between devices  7.25 us (24%)
  local copies, waits for them, and re-layouts  1.97 us (7%)
  between operations  0.68 us (2%)
    ppermute x8, starting transfers between devices, swap(): return lax.ppermute(value, ('ctx', 'head'), pairs)  8.68 us
    pallas_call x1, Pallas kernels, shards(): pl.pallas_call(lambda *refs: main_kernel(sets, ctx_count, reach, *refs),...  7.44 us
    ppermute x8, waiting for transfers between devices, swap(): return lax.ppermute(value, ('ctx', 'head'), pairs)  7.25 us
    unnamed x16, local copies, waits for them, and re-layouts  1.97 us
    pallas_call x1, Pallas kernels, shards(): pl.pallas_call(lambda *refs: sum_kernel(sets, ctx_count, *refs), out_shap...  1.81 us
    pallas_call x1, Pallas kernels, shards(): pl.pallas_call(lambda *refs: pack_kernel(sets, *refs), out_shape=payloads...  1.63 us
  transfers between devices with their start and end apart: 8, of which 2 were waited for; matrix products, arithmetic and copies ran while one was open for 0% of the time, Pallas kernels for 0%

profile of v1, /device:TPU:0, one launch (start us, length us, event | category | flops | bytes accessed | tf_op | source)
XLA Modules:
  0.0 29.5 jit_solution(15160853029525944783)
XLA Ops:
  0.6 1.6 %pack.1 = (bf16[256,256]{1,0:T(8,128)(2,1)}, bf16[128,256]{1,0:T(8,128)(2,1)}, bf16[128,256]{1,0:T(8,128)(2,1)}, bf16[128,256]{1,0:T(8,128)(2,1)}) custom-call(bf16[256,128]{1,0:T(8,128)(2,1)} %refs_3_.1, bf16[256,128]{1,0:T(8,128)(2,1)} %refs_4_.1), custom_call_target="tpu_custom_call" | custom-call | tf_op jit(solution)/shard_map/pack/pallas_call | solution.py:248
  2.3 3.0 %collective-permute-start = (bf16[256,256]{1,0:T(8,128)(2,1)}, bf16[256,256]{1,0:T(8,128)(2,1)S(1)}, u32[]{:S(2)}, u32[]{:S(2)}) collective-permute-start(bf16[256,256]{1,0:T(8,128)(2,1)} %get-tuple-element.17), channel_id=1, source_target_pairs={{0,2},{1,3},{2,0},{3,1},{4,6},{5,7},{6,4},{7,5},{8,10},{9,11},{10,... | collective-permute-start | bytes 393224 | tf_op jit(solution)/shard_map/ppermute | solution.py:37
  5.3 0.0 collective-permute-start.1
  5.3 1.6 %collective-permute-start.2 = (bf16[128,256]{1,0:T(8,128)(2,1)}, bf16[128,256]{1,0:T(8,128)(2,1)S(1)}, u32[]{:S(2)}, u32[]{:S(2)}) collective-permute-start(bf16[128,256]{1,0:T(8,128)(2,1)} %get-tuple-element.19), channel_id=1, source_target_pairs={{0,4},{1,5},{2,6},{3,7},{4,0},{5,1},{6,2},{7,3},{8,12},{9,13},{10,... | collective-permute-start | bytes 196616 | tf_op jit(solution)/shard_map/ppermute | solution.py:37
  6.8 0.0 collective-permute-start.3
  6.8 0.0 collective-permute-done.1.refs_6_
  6.8 0.0 copy-start.2
  6.8 3.8 %collective-permute-done.2.refs_7_ = bf16[128,256]{1,0:T(8,128)(2,1)S(1)} collective-permute-done((bf16[128,256]{1,0:T(8,128)(2,1)}, bf16[128,256]{1,0:T(8,128)(2,1)S(1)}, u32[]{:S(2)}, u32[]{:S(2)}) %collective-permute-start.2) | collective-permute-done | bytes 65568 | tf_op jit(solution)/shard_map/ppermute | solution.py:37
  10.7 0.0 copy-start.3
  10.7 0.0 collective-permute-done.3.refs_8_
  10.7 0.0 copy-start.5
  10.7 0.0 collective-permute-done.refs_5_
  10.7 0.0 copy-done.2
  10.7 0.6 %copy-done.3 = bf16[128,256]{1,0:T(8,128)(2,1)} copy-done((bf16[128,256]{1,0:T(8,128)(2,1)}, bf16[128,256]{1,0:T(8,128)(2,1)S(1)}, u32[]{:S(2)}) %copy-start.3) | copy-done | bytes 65560
  11.3 0.0 copy-done.5
  11.3 0.0 copy-start.1
  11.3 0.6 %copy-done.1 = bf16[256,256]{1,0:T(8,128)(2,1)} copy-done((bf16[256,256]{1,0:T(8,128)(2,1)}, bf16[256,256]{1,0:T(8,128)(2,1)S(1)}, u32[]{:S(2)}) %copy-start.1) | copy-done | bytes 131096
  12.0 7.4 %attend.1 = (bf16[256,1024]{1,0:T(8,128)(2,1)}, bf16[256,1024]{1,0:T(8,128)(2,1)}, f32[256,256]{1,0:T(8,128)}, bf16[256,256]{1,0:T(8,128)(2,1)}, bf16[128,256]{1...) custom-call(s32[16]{0:T(128)} %refs_0_.3, bf16[256,1024]{1,0:T(8,128)(2,1)} %refs_1_.3, ...), custom_call_target="tpu_custom_call" | custom-call | tf_op jit(solution)/shard_map/attend/pallas_call | solution.py:257
  19.4 2.1 %collective-permute-start.4 = (bf16[256,256]{1,0:T(8,128)(2,1)}, bf16[256,256]{1,0:T(8,128)(2,1)S(1)}, u32[]{:S(2)}, u32[]{:S(2)}) collective-permute-start(bf16[256,256]{1,0:T(8,128)(2,1)} %get-tuple-element.24), channel_id=1, source_target_pairs={{0,2},{1,3},{2,0},{3,1},{4,6},{5,7},{6,4},{7,5},{8,10},{9,11},{10,... | collective-permute-start | bytes 393224 | tf_op jit(solution)/shard_map/ppermute | solution.py:37
  21.5 0.0 collective-permute-start.5
  21.5 2.0 %collective-permute-start.6 = (bf16[128,256]{1,0:T(8,128)(2,1)}, bf16[128,256]{1,0:T(8,128)(2,1)S(1)}, u32[]{:S(2)}, u32[]{:S(2)}) collective-permute-start(bf16[128,256]{1,0:T(8,128)(2,1)} %get-tuple-element.26), channel_id=1, source_target_pairs={{0,4},{1,5},{2,6},{3,7},{4,0},{5,1},{6,2},{7,3},{8,12},{9,13},{10,... | collective-permute-start | bytes 196616 | tf_op jit(solution)/shard_map/ppermute | solution.py:37
  23.5 0.0 collective-permute-start.7
  23.5 0.0 collective-permute-done.5.refs_2_
  23.5 0.0 copy-start.4
  23.5 3.4 %collective-permute-done.6.refs_3_ = bf16[128,256]{1,0:T(8,128)(2,1)S(1)} collective-permute-done((bf16[128,256]{1,0:T(8,128)(2,1)}, bf16[128,256]{1,0:T(8,128)(2,1)S(1)}, u32[]{:S(2)}, u32[]{:S(2)}) %collective-permute-start.6) | collective-permute-done | bytes 65568 | tf_op jit(solution)/shard_map/ppermute | solution.py:37
  26.9 0.0 copy-start.6
  26.9 0.0 collective-permute-done.7.refs_4_
  26.9 0.0 copy-start.7
  26.9 0.0 collective-permute-done.4.refs_1_
  26.9 0.0 copy-start
  27.0 0.0 copy-done.4
  27.0 0.6 %copy-done.6 = bf16[128,256]{1,0:T(8,128)(2,1)} copy-done((bf16[128,256]{1,0:T(8,128)(2,1)}, bf16[128,256]{1,0:T(8,128)(2,1)S(1)}, u32[]{:S(2)}) %copy-start.6) | copy-done | bytes 65560
  27.5 0.0 copy-done.7
  27.6 0.1 copy-done
  27.6 1.8 %total.1 = (bf16[256,128]{1,0:T(8,128)(2,1)}, bf16[256,128]{1,0:T(8,128)(2,1)}) custom-call(f32[256,256]{1,0:T(8,128)} %get-tuple-element.23.refs_0_, bf16[256,256]{1,0:T(8,128)(2,1)} %copy-done, bf16[128,256]{1,0:T(8,128)(2,1)} %copy-done.4, bf16[128,256]{1,0:T(8,128)(2,1)} %copy-done.6, bf16[128,256]{1,0:T(8,128)(2,1)} %copy-done.7), custom_call_target="tpu_custom_call" | custom-call | tf_op jit(solution)/shard_map/total/pallas_call | solution.py:280
Async XLA Ops:
  2.3 8.4 %collective-permute-start = (bf16[256,256]{1,0:T(8,128)(2,1)}, bf16[256,256]{1,0:T(8,128)(2,1)S(1)}, u32[]{:S(2)}, u32[]{:S(2)}) collective-permute-start(bf16[256,256]{1,0:T(8,128)(2,1)} %get-tuple-element.17), channel_id=1, source_target_pairs={{0,2},{1,3},{2,0},{3,1},{4,6},{5,7},{6,4},{7,5},{8,10},{9,11},{10,... | collective-permute-start | bytes 393224 | tf_op jit(solution)/shard_map/ppermute | solution.py:37
  5.3 1.6 %collective-permute-start.1 = (bf16[128,256]{1,0:T(8,128)(2,1)}, bf16[128,256]{1,0:T(8,128)(2,1)S(1)}, u32[]{:S(2)}, u32[]{:S(2)}) collective-permute-start(bf16[128,256]{1,0:T(8,128)(2,1)} %get-tuple-element.18), channel_id=1, source_target_pairs={{0,1},{1,0},{2,4},{3,5},{4,2},{5,3},{6,8},{7,9},{8,6},{9,7},{10,12... | collective-permute-start | bytes 196616 | tf_op jit(solution)/shard_map/ppermute | solution.py:37
  5.3 5.4 %collective-permute-start.2 = (bf16[128,256]{1,0:T(8,128)(2,1)}, bf16[128,256]{1,0:T(8,128)(2,1)S(1)}, u32[]{:S(2)}, u32[]{:S(2)}) collective-permute-start(bf16[128,256]{1,0:T(8,128)(2,1)} %get-tuple-element.19), channel_id=1, source_target_pairs={{0,4},{1,5},{2,6},{3,7},{4,0},{5,1},{6,2},{7,3},{8,12},{9,13},{10,... | collective-permute-start | bytes 196616 | tf_op jit(solution)/shard_map/ppermute | solution.py:37
  6.8 3.8 %collective-permute-start.3 = (bf16[128,256]{1,0:T(8,128)(2,1)}, bf16[128,256]{1,0:T(8,128)(2,1)S(1)}, u32[]{:S(2)}, u32[]{:S(2)}) collective-permute-start(bf16[128,256]{1,0:T(8,128)(2,1)} %get-tuple-element.20), channel_id=1, source_target_pairs={{0,1},{1,0},{2,3},{3,2},{4,8},{5,9},{6,10},{7,11},{8,4},{9,5},{10,... | collective-permute-start | bytes 196616 | tf_op jit(solution)/shard_map/ppermute | solution.py:37
  6.8 3.9 %copy-start.2 = (bf16[128,256]{1,0:T(8,128)(2,1)}, bf16[128,256]{1,0:T(8,128)(2,1)S(1)}, u32[]{:S(2)}) copy-start(bf16[128,256]{1,0:T(8,128)(2,1)S(1)} %collective-permute-done.1.refs_6_) | copy-start | bytes 196612
  10.7 0.6 %copy-start.3 = (bf16[128,256]{1,0:T(8,128)(2,1)}, bf16[128,256]{1,0:T(8,128)(2,1)S(1)}, u32[]{:S(2)}) copy-start(bf16[128,256]{1,0:T(8,128)(2,1)S(1)} %collective-permute-done.2.refs_7_) | copy-start | bytes 196612
  10.7 0.6 %copy-start.5 = (bf16[128,256]{1,0:T(8,128)(2,1)}, bf16[128,256]{1,0:T(8,128)(2,1)S(1)}, u32[]{:S(2)}) copy-start(bf16[128,256]{1,0:T(8,128)(2,1)S(1)} %collective-permute-done.3.refs_8_) | copy-start | bytes 196612
  11.3 0.6 %copy-start.1 = (bf16[256,256]{1,0:T(8,128)(2,1)}, bf16[256,256]{1,0:T(8,128)(2,1)S(1)}, u32[]{:S(2)}) copy-start(bf16[256,256]{1,0:T(8,128)(2,1)S(1)} %collective-permute-done.refs_5_) | copy-start | bytes 393220
  19.4 7.5 %collective-permute-start.4 = (bf16[256,256]{1,0:T(8,128)(2,1)}, bf16[256,256]{1,0:T(8,128)(2,1)S(1)}, u32[]{:S(2)}, u32[]{:S(2)}) collective-permute-start(bf16[256,256]{1,0:T(8,128)(2,1)} %get-tuple-element.24), channel_id=1, source_target_pairs={{0,2},{1,3},{2,0},{3,1},{4,6},{5,7},{6,4},{7,5},{8,10},{9,11},{10,... | collective-permute-start | bytes 393224 | tf_op jit(solution)/shard_map/ppermute | solution.py:37
  21.5 2.0 %collective-permute-start.5 = (bf16[128,256]{1,0:T(8,128)(2,1)}, bf16[128,256]{1,0:T(8,128)(2,1)S(1)}, u32[]{:S(2)}, u32[]{:S(2)}) collective-permute-start(bf16[128,256]{1,0:T(8,128)(2,1)} %get-tuple-element.25), channel_id=1, source_target_pairs={{0,1},{1,0},{2,4},{3,5},{4,2},{5,3},{6,8},{7,9},{8,6},{9,7},{10,12... | collective-permute-start | bytes 196616 | tf_op jit(solution)/shard_map/ppermute | solution.py:37
  21.5 5.4 %collective-permute-start.6 = (bf16[128,256]{1,0:T(8,128)(2,1)}, bf16[128,256]{1,0:T(8,128)(2,1)S(1)}, u32[]{:S(2)}, u32[]{:S(2)}) collective-permute-start(bf16[128,256]{1,0:T(8,128)(2,1)} %get-tuple-element.26), channel_id=1, source_target_pairs={{0,4},{1,5},{2,6},{3,7},{4,0},{5,1},{6,2},{7,3},{8,12},{9,13},{10,... | collective-permute-start | bytes 196616 | tf_op jit(solution)/shard_map/ppermute | solution.py:37
  23.5 3.4 %collective-permute-start.7 = (bf16[128,256]{1,0:T(8,128)(2,1)}, bf16[128,256]{1,0:T(8,128)(2,1)S(1)}, u32[]{:S(2)}, u32[]{:S(2)}) collective-permute-start(bf16[128,256]{1,0:T(8,128)(2,1)} %get-tuple-element.27), channel_id=1, source_target_pairs={{0,1},{1,0},{2,3},{3,2},{4,8},{5,9},{6,10},{7,11},{8,4},{9,5},{10,... | collective-permute-start | bytes 196616 | tf_op jit(solution)/shard_map/ppermute | solution.py:37
  23.5 3.4 %copy-start.4 = (bf16[128,256]{1,0:T(8,128)(2,1)}, bf16[128,256]{1,0:T(8,128)(2,1)S(1)}, u32[]{:S(2)}) copy-start(bf16[128,256]{1,0:T(8,128)(2,1)S(1)} %collective-permute-done.5.refs_2_) | copy-start | bytes 196612
  26.9 0.6 %copy-start.6 = (bf16[128,256]{1,0:T(8,128)(2,1)}, bf16[128,256]{1,0:T(8,128)(2,1)S(1)}, u32[]{:S(2)}) copy-start(bf16[128,256]{1,0:T(8,128)(2,1)S(1)} %collective-permute-done.6.refs_3_) | copy-start | bytes 196612
  26.9 0.6 %copy-start.7 = (bf16[128,256]{1,0:T(8,128)(2,1)}, bf16[128,256]{1,0:T(8,128)(2,1)S(1)}, u32[]{:S(2)}) copy-start(bf16[128,256]{1,0:T(8,128)(2,1)S(1)} %collective-permute-done.7.refs_4_) | copy-start | bytes 196612
  26.9 0.7 %copy-start = (bf16[256,256]{1,0:T(8,128)(2,1)}, bf16[256,256]{1,0:T(8,128)(2,1)S(1)}, u32[]{:S(2)}) copy-start(bf16[256,256]{1,0:T(8,128)(2,1)S(1)} %collective-permute-done.4.refs_1_) | copy-start | bytes 393220

commit v2 on v1

v2 whole, which is shorter than its diff:
```python
import math

import jax
import jax.numpy as jnp
from jax import lax
from jax.experimental import pallas as pl
from jax.experimental.pallas import tpu as pltpu
from jax.sharding import PartitionSpec as P

HEAD_DIM = 128
DOC_STRETCHES = 8
MASKED = -1e30
VMEM_LIMIT = 24 << 20


def exchanges(ctx_count, reach):
    sets = []
    for offset in range(1, reach + 1):
        for colour in range(2):
            firsts = [b for b in range(ctx_count - offset) if (b // offset) % 2 == colour]
            if firsts:
                full = any(2 * b >= 2 * ctx_count - 1 - reach - offset for b in firsts)
                sets.append((offset, colour, full, tuple(firsts)))
    return sets


def swap(value, exchange, ctx_count, head_count):
    offset, _, _, firsts = exchange
    partner = {b: b + offset for b in firsts}
    partner.update({b + offset: b for b in firsts})
    pairs = []
    for b in range(ctx_count):
        for h in range(head_count):
            if b in partner:
                pairs.append((b * head_count + h, partner[b] * head_count + h))
            else:
                pairs.append((b * head_count + h, b * head_count + (h + 1) % head_count))
    return lax.ppermute(value, ("ctx", "head"), pairs)


def fold_offsets(slot):
    return range(-(slot - 1), slot, 2)


def pack_kernel(sets, k_hbm, v_hbm, mine, *refs):
    halves = [s for s in sets if not s[2]]
    outs, sems = refs[: len(halves)], refs[len(halves)]
    me = lax.axis_index("ctx")
    length = k_hbm.shape[0] // 2
    width = k_hbm.shape[1]
    copies = [
        pltpu.make_async_copy(k_hbm, mine.at[:, :width], sems.at[0]),
        pltpu.make_async_copy(v_hbm, mine.at[:, width:], sems.at[1]),
    ]
    for i, ((offset, colour, _, _), out) in enumerate(zip(halves, outs)):
        first = (me // offset) % 2 == colour
        rows = pl.ds(pl.multiple_of(jnp.where(first, 0, length), length), length)
        copies.append(pltpu.make_async_copy(k_hbm.at[rows, :], out.at[:, :width], sems.at[2 * i + 2]))
        copies.append(pltpu.make_async_copy(v_hbm.at[rows, :], out.at[:, width:], sems.at[2 * i + 3]))
    for copy in copies:
        copy.start()
    for copy in copies:
        copy.wait()


def stage_kernel(ctx_count, docs_ref, q_hbm, g_hbm, q_all, g_all, bias, sems):
    length = q_hbm.shape[0] // 2
    width = q_all.shape[2]
    heads = q_all.shape[1] // length
    copies = []
    for s in range(2):
        for h in range(heads):
            for a, (src, dst) in enumerate(((q_hbm, q_all), (g_hbm, g_all))):
                copies.append(
                    pltpu.make_async_copy(
                        src.at[s * length : (s + 1) * length, h * width : (h + 1) * width],
                        dst.at[s, h * length : (h + 1) * length, :],
                        sems.at[a, s, h],
                    )
                )
    for copy in copies:
        copy.start()
    me = lax.axis_index("ctx")
    merged = bias.shape[1]
    row = lax.broadcasted_iota(jnp.int32, (merged, length), 0)
    col = lax.broadcasted_iota(jnp.int32, (1, length), 1)
    for s in range(2):
        stretch = me if s == 0 else 2 * ctx_count - 1 - me
        q_pos = stretch * length + col
        start = jnp.int32(0)
        doc_start = jnp.zeros((1, length), jnp.int32)
        for i in range(docs_ref.shape[0]):
            doc_start = jnp.where(q_pos >= start, start, doc_start)
            start = start + docs_ref[i]
        k_pos = row + (stretch - 2 * (row // length)) * length
        k_pos = jnp.where(k_pos > q_pos, k_pos - merged, k_pos)
        bias[s] = jnp.where(k_pos >= doc_start, 0.0, MASKED)
    for copy in copies:
        copy.wait()


def score_kernel(sets, ctx_count, reach, bias, q_all, g_all, mine, *refs):
    halves = [s for s in sets if not s[2]]
    fulls = [s for s in sets if s[2]]
    order = fulls + halves
    count = len(order)
    recs = {(s[0], s[1]): (r, s[2]) for s, r in zip(order, refs[:count])}
    pb, dsb, kv_win, own_ref = refs[count : count + 4]
    sends = {(s[0], s[1]): (r, s[2]) for s, r in zip(order, refs[count + 4 : 2 * count + 4])}
    acc, extra = refs[2 * count + 4 :]
    me = lax.axis_index("ctx")
    length = mine.shape[0] // 2
    width = HEAD_DIM
    heads = q_all.shape[1] // length
    merged = reach * length
    scaling = width ** (-0.5)
    log_scale = scaling * math.log2(math.e)

    def low_part(key):
        ref, full = recs[key]
        return ref[:length, :] if full else ref[...]

    def up_part(key):
        ref, full = recs[key]
        return ref[length:, :] if full else ref[...]

    def pick(part, offset, colour_pred):
        have = [c for c in range(2) if (offset, c) in recs]
        if len(have) == 1:
            return part((offset, have[0]))
        return jnp.where(colour_pred, part((offset, 1)), part((offset, 0)))

    lows = [mine[:length, :]]
    highs = [mine[length:, :]]
    for slot in range(1, reach + 1):
        odd = (me // slot) % 2 == 1
        lows.append(pick(low_part, slot, jnp.logical_not(odd)))
        highs.append(pick(up_part, slot, odd))
    for slot in range(1, reach + 1):
        folded = me + slot >= ctx_count
        value = highs[slot]
        for offset in fold_offsets(slot):
            here = folded & (2 * ctx_count - 1 - 2 * me - slot == offset)
            if offset <= 0:
                value = jnp.where(here, lows[-offset], value)
            else:
                for colour in range(2):
                    if recs.get((offset, colour), (None, False))[1]:
                        where = here & ((me // offset) % 2 == colour)
                        value = jnp.where(where, low_part((offset, colour)), value)
        highs[slot] = value
    for slot in range(reach + 1):
        rows = slice(slot * length, (slot + 1) * length)
        kv_win[0, rows, :] = lows[slot]
        kv_win[1, rows, :] = highs[slot]

    tri_row = lax.broadcasted_iota(jnp.int32, (length, length), 0)
    near = tri_row <= lax.broadcasted_iota(jnp.int32, (length, length), 1)
    near_low = jnp.where(near, 1.0, 0.0).astype(jnp.bfloat16)

    def fold(value):
        return jnp.where(near, value[:length, :], value[merged:, :])

    def products(s, h):
        lanes = slice(h * length, (h + 1) * length)
        contract_last = (((1,), (1,)), ((), ()))
        raw = lax.dot_general(
            kv_win[s, :, :width], q_all[s, lanes, :], contract_last, preferred_element_type=jnp.float32
        )
        d_p = lax.dot_general(
            kv_win[s, :, width:], g_all[s, lanes, :], contract_last, preferred_element_type=jnp.float32
        )
        return raw, d_p

    def soften(s, h, raw, d_p):
        lanes = slice(h * length, (h + 1) * length)
        raw = jnp.concatenate([fold(raw), raw[length:merged, :]], axis=0) + bias[s]
        d_p = jnp.concatenate([fold(d_p), d_p[length:merged, :]], axis=0)
        top = jnp.max(raw, axis=0, keepdims=True)
        weight = jnp.exp2((raw - top) * log_scale)
        total = jnp.sum(weight, axis=0, keepdims=True)
        inverse = 1.0 / total
        delta = jnp.sum(weight * d_p, axis=0, keepdims=True) * inverse
        weight = weight * inverse
        low = weight.astype(jnp.bfloat16)
        d_s = (weight * (d_p - delta)).astype(jnp.bfloat16)
        for ref, value in ((pb, low), (dsb, d_s)):
            here = value[:length, :] * near_low
            ref[s, :length, lanes] = here
            ref[s, length:merged, lanes] = value[length:, :]
            ref[s, merged:, lanes] = value[:length, :] - here

    def gradients(s):
        acc[s, :, :width] = jnp.dot(dsb[s], q_all[s], preferred_element_type=jnp.float32) * scaling
        acc[s, :, width:] = jnp.dot(pb[s], g_all[s], preferred_element_type=jnp.float32)

    items = [(s, h) for s in range(2) for h in range(heads)]
    ready = products(*items[0])
    for i, item in enumerate(items):
        following = products(*items[i + 1]) if i + 1 < len(items) else None
        soften(*item, *ready)
        ready = following
        if item[1] == heads - 1:
            gradients(item[0])

    def slot_rows(slot):
        return slice(slot * length, (slot + 1) * length)

    extra[...] = jnp.zeros(extra.shape, jnp.float32)
    for slot in range(1, reach + 1):
        for offset in fold_offsets(slot):

            @pl.when((me + slot >= ctx_count) & (2 * ctx_count - 1 - 2 * me - slot == offset))
            def _():
                part = acc[1, slot_rows(slot), :]
                if offset <= 0:
                    acc[0, slot_rows(-offset), :] = acc[0, slot_rows(-offset), :] + part
                else:
                    extra[slot_rows(offset - 1), :] = part

    own_ref[:length, :] = acc[0, :length, :]
    own_ref[length:, :] = acc[1, :length, :]
    for (offset, colour), (ref, full) in sends.items():
        first = (me // offset) % 2 == colour
        to_low = acc[0, slot_rows(offset), :]
        to_up = acc[1, slot_rows(offset), :]
        if full:
            more = extra[slot_rows(offset - 1), :]
            ref[:length, :] = jnp.where(first, more, to_low).astype(jnp.bfloat16)
            ref[length:, :] = jnp.where(first, to_up, 0.0).astype(jnp.bfloat16)
        else:
            ref[...] = jnp.where(first, to_up, to_low).astype(jnp.bfloat16)


def output_kernel(pb, dsb, kv_win, att_hbm, dq_hbm, att, dq, sems):
    length = att.shape[0] // 2
    width = HEAD_DIM
    heads = att.shape[1] // width
    scaling = width ** (-0.5)
    group = 2 if heads % 2 == 0 else 1
    copies = []
    for s in range(2):
        rows = slice(s * length, (s + 1) * length)
        k_turn = kv_win[s, :, :width].T
        v_turn = kv_win[s, :, width:].T
        for h in range(0, heads, group):
            lanes = slice(h * length, (h + group) * length)
            out_t = jnp.dot(v_turn, pb[s, :, lanes], preferred_element_type=jnp.float32)
            dq_t = jnp.dot(k_turn, dsb[s, :, lanes], preferred_element_type=jnp.float32) * scaling
            out_t = out_t.astype(jnp.bfloat16)
            dq_t = dq_t.astype(jnp.bfloat16)
            for i in range(group):
                part = slice(i * length, (i + 1) * length)
                cols = slice((h + i) * width, (h + i + 1) * width)
                att[rows, cols] = out_t[:, part].T
                dq[rows, cols] = dq_t[:, part].T
        for a, (src, dst) in enumerate(((att, att_hbm), (dq, dq_hbm))):
            copy = pltpu.make_async_copy(src.at[rows, :], dst.at[rows, :], sems.at[s, a])
            copy.start()
            copies.append(copy)
    for copy in copies:
        copy.wait()


def sum_kernel(sets, ctx_count, own_ref, *refs):
    dk_ref, dv_ref = refs[len(sets) :]
    me = lax.axis_index("ctx")
    length = own_ref.shape[0] // 2
    width = dk_ref.shape[1]
    low = own_ref[:length, :]
    up = own_ref[length:, :]
    for (offset, colour, full, _), ref in zip(sets, refs):
        first = (me // offset) % 2 == colour
        as_first = first & (me + offset < ctx_count)
        as_second = jnp.logical_not(first) & (me >= offset)
        if full:
            low = low + jnp.where(as_first | as_second, ref[:length, :].astype(jnp.float32), 0.0)
            up = up + jnp.where(as_second, ref[length:, :].astype(jnp.float32), 0.0)
        else:
            part = ref[...].astype(jnp.float32)
            low = low + jnp.where(as_first, part, 0.0)
            up = up + jnp.where(as_second, part, 0.0)
    dk_ref[:length, :] = low[:, :width].astype(jnp.bfloat16)
    dk_ref[length:, :] = up[:, :width].astype(jnp.bfloat16)
    dv_ref[:length, :] = low[:, width:].astype(jnp.bfloat16)
    dv_ref[length:, :] = up[:, width:].astype(jnp.bfloat16)


def in_vmem(amount):
    return [pl.BlockSpec(memory_space=pltpu.VMEM)] * amount


def in_place(amount):
    return [pl.BlockSpec(memory_space=pl.ANY)] * amount


def on_chip(values):
    return [pltpu.with_memory_space_constraint(v, pltpu.VMEM) for v in values]


def off_chip(values):
    return [pltpu.with_memory_space_constraint(v, pltpu.HBM) for v in values]


def shards(query_rows, key_rows, value_rows, out_grad, doc_lengths):
    ctx_count = lax.axis_size("ctx")
    head_count = lax.axis_size("head")
    tok_dev = query_rows.shape[0]
    length = tok_dev // 2
    width = key_rows.shape[1]
    reach = min(DOC_STRETCHES, ctx_count // 4)
    span = (reach + 1) * length
    heads = query_rows.shape[1] // width
    sets = exchanges(ctx_count, reach)
    sets = [s for s in sets if s[2]] + [s for s in sets if not s[2]]
    fulls = sum(s[2] for s in sets)
    count = len(sets)
    payloads = [
        pltpu.VMEM((2 * length if s[2] else length, 2 * width), jnp.bfloat16) for s in sets
    ]
    mine, *halves = pl.pallas_call(
        lambda *refs: pack_kernel(sets, *refs),
        out_shape=[pltpu.VMEM((tok_dev, 2 * width), jnp.bfloat16)] + payloads[fulls:],
        in_specs=in_place(2),
        out_specs=in_vmem(1 + count - fulls),
        scratch_shapes=[pltpu.SemaphoreType.DMA((2 + 2 * (count - fulls),))],
        compiler_params=pltpu.CompilerParams(vmem_limit_bytes=VMEM_LIMIT),
        name="pack",
    )(*off_chip([key_rows, value_rows]))
    packed = [mine] * fulls + halves
    received = [swap(p, s, ctx_count, head_count) for p, s in zip(packed, sets)]

    stack = pltpu.VMEM((2, heads * length, width), jnp.bfloat16)
    q_all, g_all, bias = pl.pallas_call(
        lambda *refs: stage_kernel(ctx_count, *refs),
        out_shape=[stack, stack, pltpu.VMEM((2, reach * length, length), jnp.float32)],
        in_specs=[pl.BlockSpec(memory_space=pltpu.SMEM)] + in_place(2),
        out_specs=in_vmem(3),
        scratch_shapes=[pltpu.SemaphoreType.DMA((2, 2, heads))],
        compiler_params=pltpu.CompilerParams(vmem_limit_bytes=VMEM_LIMIT),
        name="stage",
    )(doc_lengths, *off_chip([query_rows, out_grad]))

    low_weights = pltpu.VMEM((2, span, heads * length), jnp.bfloat16)
    pb, dsb, kv_win, own, *partials = pl.pallas_call(
        lambda *refs: score_kernel(sets, ctx_count, reach, *refs),
        out_shape=[
            low_weights,
            low_weights,
            pltpu.VMEM((2, span, 2 * width), jnp.bfloat16),
            pltpu.VMEM((tok_dev, 2 * width), jnp.float32),
        ]
        + payloads,
        in_specs=in_vmem(4 + count),
        out_specs=in_vmem(4 + count),
        scratch_shapes=[
            pltpu.VMEM((2, span, 2 * width), jnp.float32),
            pltpu.VMEM((reach * length, 2 * width), jnp.float32),
        ],
        compiler_params=pltpu.CompilerParams(vmem_limit_bytes=VMEM_LIMIT),
        name="score",
    )(*on_chip([bias, q_all, g_all, mine, *received]))
    returned = [swap(p, s, ctx_count, head_count) for p, s in zip(partials, sets)]

    attended, query_grad = pl.pallas_call(
        output_kernel,
        out_shape=[jax.ShapeDtypeStruct(query_rows.shape, jnp.bfloat16)] * 2,
        in_specs=in_vmem(3),
        out_specs=in_place(2),
        scratch_shapes=[
            pltpu.VMEM(query_rows.shape, jnp.bfloat16),
            pltpu.VMEM(query_rows.shape, jnp.bfloat16),
            pltpu.SemaphoreType.DMA((2, 2)),
        ],
        compiler_params=pltpu.CompilerParams(vmem_limit_bytes=VMEM_LIMIT),
        name="output",
    )(*on_chip([pb, dsb, kv_win]))

    key_grad, value_grad = pl.pallas_call(
        lambda *refs: sum_kernel(sets, ctx_count, *refs),
        out_shape=[jax.ShapeDtypeStruct(key_rows.shape, jnp.bfloat16)] * 2,
        in_specs=in_vmem(1 + count),
        out_specs=in_vmem(2),
        compiler_params=pltpu.CompilerParams(vmem_limit_bytes=VMEM_LIMIT),
        name="total",
    )(*on_chip([own, *returned]))
    return (attended, query_grad, key_grad, value_grad)


def solution(mesh):
    placed = (
        P(("groups", "ctx"), "head"),
        P(("groups", "ctx"), "head"),
        P(("groups", "ctx"), "head"),
        P(("groups", "ctx"), "head"),
        P("groups"),
    )
    return jax.shard_map(
        shards,
        mesh=mesh,
        in_specs=placed,
        out_specs=(P(("groups", "ctx"), "head"),) * 4,
        check_vma=False,
    )
```

time: 29.7 us -> 21.9 us (0.74)
  waiting for transfers between devices: 7.25 us -> 2.72 us
  Pallas kernels: 10.9 us -> 8.73 us
  local copies, waits for them, and re-layouts: 1.97 us -> 0.66 us
    ppermute x8, waiting for transfers between devices: 7.25 us -> 2.72 us  [swap(): return lax.ppermute(value, ('ctx', 'head'), pairs)]
    unnamed x16 -> x2, local copies, waits for them, and re-layouts: 1.97 us -> 0.66 us
    pallas_call x2 -> x4, Pallas kernels: 9.07 us -> 7.97 us  [the longest x1 3.3 us: shards(): pl.pallas_call(lambda *refs: score_kernel(sets, ctx_count, reach, *refs),...]
    pallas_call x1, Pallas kernels: 1.81 us -> 0.76 us  [shards(): pl.pallas_call(lambda *refs: sum_kernel(sets, ctx_count, *refs), out_shap...]
  transfers between devices with their start and end apart: 8 -> 8, of which waited for: 2 -> 2; matrix products, arithmetic and copies ran while one was open for 0% -> 0% of each run, Pallas kernels for 0% -> 17%
where the time goes in v2:
time: 21.9 us; the launch traced here: 21.6 us
  starting transfers between devices  8.8 us (40%)
  Pallas kernels  8.73 us (40%)
  waiting for transfers between devices  2.72 us (12%)
  between operations  0.68 us (3%)
  local copies, waits for them, and re-layouts  0.66 us (3%)
    ppermute x8, starting transfers between devices, swap(): return lax.ppermute(value, ('ctx', 'head'), pairs)  8.8 us
    pallas_call x1, Pallas kernels, shards(): pl.pallas_call(lambda *refs: score_kernel(sets, ctx_count, reach, *refs),...  3.3 us
    ppermute x8, waiting for transfers between devices, swap(): return lax.ppermute(value, ('ctx', 'head'), pairs)  2.72 us
    pallas_call x1, Pallas kernels, shards(): pl.pallas_call(lambda *refs: stage_kernel(ctx_count, *refs), out_shape=[s...  2.01 us
    pallas_call x1, Pallas kernels, shards(): pl.pallas_call(output_kernel, out_shape=[jax.ShapeDtypeStruct(query_rows....  1.65 us
    pallas_call x1, Pallas kernels, shards(): pl.pallas_call(lambda *refs: pack_kernel(sets, *refs), out_shape=[pltpu.V...  1 us
    pallas_call x1, Pallas kernels, shards(): pl.pallas_call(lambda *refs: sum_kernel(sets, ctx_count, *refs), out_shap...  0.76 us
    unnamed x2, local copies, waits for them, and re-layouts  0.66 us
  transfers between devices with their start and end apart: 8, of which 2 were waited for; matrix products, arithmetic and copies ran while one was open for 0% of the time, Pallas kernels for 17%

profile of v2, /device:TPU:0, one launch (start us, length us, event | category | flops | bytes accessed | tf_op | source)
XLA Modules:
  0.0 21.6 jit_solution(8572679837307354969)
XLA Ops:
  0.6 1.0 %pack.1 = (bf16[256,256]{1,0:T(8,128)(2,1)S(1)}, bf16[128,256]{1,0:T(8,128)(2,1)S(1)}, bf16[128,256]{1,0:T(8,128)(2,1)S(1)}, bf16[128,256]{1,0:T(8,128)(2,1)S(1)}) custom-call(bf16[256,128]{1,0:T(8,128)(2,1)} %refs_0_.3, bf16[256,128]{1,0:T(8,128)(2,1)} %refs_1_.3), custom_call_target="tpu_custom_call" | custom-call | tf_op jit(solution)/shard_map/pack/pallas_call | solution.py:321
  1.6 3.0 %collective-permute-start = (bf16[256,256]{1,0:T(8,128)(2,1)S(1)}, bf16[256,256]{1,0:T(8,128)(2,1)S(1)}, u32[]{:S(2)}, u32[]{:S(2)}) collective-permute-start(bf16[256,256]{1,0:T(8,128)(2,1)S(1)} %get-tuple-element.26.refs_3_), channel_id=1, source_target_pairs={{0,2},{1,3},{2,0},{3,1},{4,6},{5,7},{6,4},{7,5},{8,10},{9,11},{10,... | collective-permute-start | bytes 393224 | tf_op jit(solution)/shard_map/ppermute | solution.py:38
  4.7 0.0 collective-permute-start.1
  4.7 1.6 %collective-permute-start.2 = (bf16[128,256]{1,0:T(8,128)(2,1)S(1)}, bf16[128,256]{1,0:T(8,128)(2,1)S(1)}, u32[]{:S(2)}, u32[]{:S(2)}) collective-permute-start(bf16[128,256]{1,0:T(8,128)(2,1)S(1)} %get-tuple-element.28), channel_id=1, source_target_pairs={{0,4},{1,5},{2,6},{3,7},{4,0},{5,1},{6,2},{7,3},{8,12},{9,13},{10,... | collective-permute-start | bytes 196616 | tf_op jit(solution)/shard_map/ppermute | solution.py:38
  6.3 0.0 collective-permute-start.3
  6.3 0.0 copy-start
  6.3 0.7 %copy-done = s32[16]{0:T(128)S(1)} copy-done((s32[16]{0:T(128)S(1)}, s32[16]{0:T(128)}, u32[]{:S(2)}) %copy-start) | copy-done | bytes 88
  6.9 2.0 %stage.1 = (bf16[2,1024,128]{2,1,0:T(8,128)(2,1)S(1)}, bf16[2,1024,128]{2,1,0:T(8,128)(2,1)S(1)}, f32[2,256,128]{2,1,0:T(8,128)S(1)}) custom-call(s32[16]{0:T(128)S(1)} %copy-done, bf16[256,1024]{1,0:T(8,128)(2,1)} %refs_1_.2, bf16[256,1024]{1,0:T(8,128)(2,1)} %refs_2_.1), custom_call_target="tpu_custom_call" | custom-call | tf_op jit(solution)/shard_map/stage/pallas_call | solution.py:334
  8.9 0.0 collective-permute-done.1.refs_5_
  9.0 0.9 %collective-permute-done.2.refs_6_ = bf16[128,256]{1,0:T(8,128)(2,1)S(1)} collective-permute-done((bf16[128,256]{1,0:T(8,128)(2,1)S(1)}, bf16[128,256]{1,0:T(8,128)(2,1)S(1)}, u32[]{:S(2)}, u32[]{:S(2)}) %collective-permute-start.2) | collective-permute-done | bytes 65568 | tf_op jit(solution)/shard_map/ppermute | solution.py:38
  9.9 0.0 collective-permute-done.3.refs_7_
  9.9 0.0 collective-permute-done.refs_4_
  9.9 3.3 %score.1 = (bf16[2,384,1024]{2,1,0:T(8,128)(2,1)S(1)}, bf16[2,384,1024]{2,1,0:T(8,128)(2,1)S(1)}, bf16[2,384,256]{2,1,0:T(8,128)(2,1)S(1)}, f32[256,256]{1,0:T(8...) custom-call(f32[2,256,128]{2,1,0:T(8,128)S(1)} %get-tuple-element.23, ...), custom_call_target="tpu_custom_call" | custom-call | tf_op jit(solution)/shard_map/score/pallas_call | solution.py:345
  13.2 2.2 %collective-permute-start.4 = (bf16[256,256]{1,0:T(8,128)(2,1)S(1)}, bf16[256,256]{1,0:T(8,128)(2,1)S(1)}, u32[]{:S(2)}, u32[]{:S(2)}) collective-permute-start(bf16[256,256]{1,0:T(8,128)(2,1)S(1)} %get-tuple-element.36), channel_id=1, source_target_pairs={{0,2},{1,3},{2,0},{3,1},{4,6},{5,7},{6,4},{7,5},{8,10},{9,11},{10,... | collective-permute-start | bytes 393224 | tf_op jit(solution)/shard_map/ppermute | solution.py:38
  15.4 0.2 %collective-permute-start.5 = (bf16[128,256]{1,0:T(8,128)(2,1)S(1)}, bf16[128,256]{1,0:T(8,128)(2,1)S(1)}, u32[]{:S(2)}, u32[]{:S(2)}) collective-permute-start(bf16[128,256]{1,0:T(8,128)(2,1)S(1)} %get-tuple-element.37), channel_id=1, source_target_pairs={{0,1},{1,0},{2,4},{3,5},{4,2},{5,3},{6,8},{7,9},{8,6},{9,7},{10,12... | collective-permute-start | bytes 196616 | tf_op jit(solution)/shard_map/ppermute | solution.py:38
  15.6 1.8 %collective-permute-start.6 = (bf16[128,256]{1,0:T(8,128)(2,1)S(1)}, bf16[128,256]{1,0:T(8,128)(2,1)S(1)}, u32[]{:S(2)}, u32[]{:S(2)}) collective-permute-start(bf16[128,256]{1,0:T(8,128)(2,1)S(1)} %get-tuple-element.38), channel_id=1, source_target_pairs={{0,4},{1,5},{2,6},{3,7},{4,0},{5,1},{6,2},{7,3},{8,12},{9,13},{10,... | collective-permute-start | bytes 196616 | tf_op jit(solution)/shard_map/ppermute | solution.py:38
  17.4 0.0 collective-permute-start.7
  17.4 1.6 %output.1 = (bf16[256,1024]{1,0:T(8,128)(2,1)}, bf16[256,1024]{1,0:T(8,128)(2,1)}) custom-call(bf16[2,384,1024]{2,1,0:T(8,128)(2,1)S(1)} %get-tuple-element.30.pb, bf16[2,384,1024]{2,1,0:T(8,128)(2,1)S(1)} %get-tuple-element.31.dsb, bf16[2,384,256]{2,1,0:T(8,128)(2,1)S(1)} %get-tuple-element.32.kv_win), custom_call_target="tpu_custom_call" | custom-call | tf_op jit(solution)/shard_map/output/pallas_call | solution.py:365
  19.1 0.0 collective-permute-done.5.refs_2_
  19.1 1.8 %collective-permute-done.6.refs_3_ = bf16[128,256]{1,0:T(8,128)(2,1)S(1)} collective-permute-done((bf16[128,256]{1,0:T(8,128)(2,1)S(1)}, bf16[128,256]{1,0:T(8,128)(2,1)S(1)}, u32[]{:S(2)}, u32[]{:S(2)}) %collective-permute-start.6) | collective-permute-done | bytes 65568 | tf_op jit(solution)/shard_map/ppermute | solution.py:38
  20.8 0.0 collective-permute-done.7.refs_4_
  20.8 0.0 collective-permute-done.4.refs_1_
  20.8 0.8 %total.1 = (bf16[256,128]{1,0:T(8,128)(2,1)}, bf16[256,128]{1,0:T(8,128)(2,1)}) custom-call(f32[256,256]{1,0:T(8,128)S(1)} %get-tuple-element.35.refs_0_, bf16[256,256]{1,0:T(8,128)(2,1)S(1)} %collective-permute-done.4.refs_1_, bf16[128,256]{1,0:T(8,128)(2,1)S(1)} %collective-permute-done.5.refs_2_, bf16[128,256]{1,0:T(8,128)(2,1)S(1)} %collective-permute-done.6.refs_3_, ...), custom_call_target="tpu_custom_call" | custom-call | tf_op jit(solution)/shard_map/total/pallas_call | solution.py:379
Async XLA Ops:
  1.6 8.3 %collective-permute-start = (bf16[256,256]{1,0:T(8,128)(2,1)S(1)}, bf16[256,256]{1,0:T(8,128)(2,1)S(1)}, u32[]{:S(2)}, u32[]{:S(2)}) collective-permute-start(bf16[256,256]{1,0:T(8,128)(2,1)S(1)} %get-tuple-element.26.refs_3_), channel_id=1, source_target_pairs={{0,2},{1,3},{2,0},{3,1},{4,6},{5,7},{6,4},{7,5},{8,10},{9,11},{10,... | collective-permute-start | bytes 393224 | tf_op jit(solution)/shard_map/ppermute | solution.py:38
  4.7 4.3 %collective-permute-start.1 = (bf16[128,256]{1,0:T(8,128)(2,1)S(1)}, bf16[128,256]{1,0:T(8,128)(2,1)S(1)}, u32[]{:S(2)}, u32[]{:S(2)}) collective-permute-start(bf16[128,256]{1,0:T(8,128)(2,1)S(1)} %get-tuple-element.27), channel_id=1, source_target_pairs={{0,1},{1,0},{2,4},{3,5},{4,2},{5,3},{6,8},{7,9},{8,6},{9,7},{10,12... | collective-permute-start | bytes 196616 | tf_op jit(solution)/shard_map/ppermute | solution.py:38
  4.7 5.2 %collective-permute-start.2 = (bf16[128,256]{1,0:T(8,128)(2,1)S(1)}, bf16[128,256]{1,0:T(8,128)(2,1)S(1)}, u32[]{:S(2)}, u32[]{:S(2)}) collective-permute-start(bf16[128,256]{1,0:T(8,128)(2,1)S(1)} %get-tuple-element.28), channel_id=1, source_target_pairs={{0,4},{1,5},{2,6},{3,7},{4,0},{5,1},{6,2},{7,3},{8,12},{9,13},{10,... | collective-permute-start | bytes 196616 | tf_op jit(solution)/shard_map/ppermute | solution.py:38
  6.3 3.6 %collective-permute-start.3 = (bf16[128,256]{1,0:T(8,128)(2,1)S(1)}, bf16[128,256]{1,0:T(8,128)(2,1)S(1)}, u32[]{:S(2)}, u32[]{:S(2)}) collective-permute-start(bf16[128,256]{1,0:T(8,128)(2,1)S(1)} %get-tuple-element.29), channel_id=1, source_target_pairs={{0,1},{1,0},{2,3},{3,2},{4,8},{5,9},{6,10},{7,11},{8,4},{9,5},{10,... | collective-permute-start | bytes 196616 | tf_op jit(solution)/shard_map/ppermute | solution.py:38
  6.3 0.7 %copy-start = (s32[16]{0:T(128)S(1)}, s32[16]{0:T(128)}, u32[]{:S(2)}) copy-start(s32[16]{0:T(128)} %refs_0_.2) | copy-start | bytes 196
  13.2 7.6 %collective-permute-start.4 = (bf16[256,256]{1,0:T(8,128)(2,1)S(1)}, bf16[256,256]{1,0:T(8,128)(2,1)S(1)}, u32[]{:S(2)}, u32[]{:S(2)}) collective-permute-start(bf16[256,256]{1,0:T(8,128)(2,1)S(1)} %get-tuple-element.36), channel_id=1, source_target_pairs={{0,2},{1,3},{2,0},{3,1},{4,6},{5,7},{6,4},{7,5},{8,10},{9,11},{10,... | collective-permute-start | bytes 393224 | tf_op jit(solution)/shard_map/ppermute | solution.py:38
  15.4 3.7 %collective-permute-start.5 = (bf16[128,256]{1,0:T(8,128)(2,1)S(1)}, bf16[128,256]{1,0:T(8,128)(2,1)S(1)}, u32[]{:S(2)}, u32[]{:S(2)}) collective-permute-start(bf16[128,256]{1,0:T(8,128)(2,1)S(1)} %get-tuple-element.37), channel_id=1, source_target_pairs={{0,1},{1,0},{2,4},{3,5},{4,2},{5,3},{6,8},{7,9},{8,6},{9,7},{10,12... | collective-permute-start | bytes 196616 | tf_op jit(solution)/shard_map/ppermute | solution.py:38
  15.6 5.2 %collective-permute-start.6 = (bf16[128,256]{1,0:T(8,128)(2,1)S(1)}, bf16[128,256]{1,0:T(8,128)(2,1)S(1)}, u32[]{:S(2)}, u32[]{:S(2)}) collective-permute-start(bf16[128,256]{1,0:T(8,128)(2,1)S(1)} %get-tuple-element.38), channel_id=1, source_target_pairs={{0,4},{1,5},{2,6},{3,7},{4,0},{5,1},{6,2},{7,3},{8,12},{9,13},{10,... | collective-permute-start | bytes 196616 | tf_op jit(solution)/shard_map/ppermute | solution.py:38
  17.4 3.4 %collective-permute-start.7 = (bf16[128,256]{1,0:T(8,128)(2,1)S(1)}, bf16[128,256]{1,0:T(8,128)(2,1)S(1)}, u32[]{:S(2)}, u32[]{:S(2)}) collective-permute-start(bf16[128,256]{1,0:T(8,128)(2,1)S(1)} %get-tuple-element.39), channel_id=1, source_target_pairs={{0,1},{1,0},{2,3},{3,2},{4,8},{5,9},{6,10},{7,11},{8,4},{9,5},{10,... | collective-permute-start | bytes 196616 | tf_op jit(solution)/shard_map/ppermute | solution.py:38

commit v3 on v2

v3 whole, which is shorter than its diff:
```python
import math

import jax
import jax.numpy as jnp
from jax import lax
from jax.experimental import pallas as pl
from jax.experimental.pallas import tpu as pltpu
from jax.sharding import PartitionSpec as P

HEAD_DIM = 128
DOC_STRETCHES = 8
MASKED = -1e30
VMEM_LIMIT = 24 << 20
CHUNK = 4


def exchanges(ctx_count, reach):
    sets = []
    for offset in range(1, reach + 1):
        for colour in range(2):
            firsts = [b for b in range(ctx_count - offset) if (b // offset) % 2 == colour]
            if firsts:
                sets.append(dict(offset=offset, colour=colour, full=False, firsts=firsts, folds=[]))
    while not place_folds(sets, ctx_count, reach):
        pass
    return sorted(sets, key=lambda entry: not entry["full"])


def place_folds(sets, ctx_count, reach):
    for entry in sets:
        entry["folds"] = []
    for entry in sets:
        offset = entry["offset"]
        for b in entry["firsts"]:
            if entry["full"] or 2 * b < 2 * ctx_count - 1 - reach - offset:
                continue
            for other in sets:
                busy = [x for f in other["firsts"] for x in (f, f + other["offset"])]
                busy += [x for pair in other["folds"] for x in pair]
                sends_low = ((b + offset) // other["offset"]) % 2 == other["colour"]
                if b not in busy and b + offset not in busy and sends_low and not other["full"]:
                    other["folds"].append((b, b + offset))
                    break
            else:
                entry["full"] = True
                return False
    return True


def key_of(entry):
    return entry["offset"], entry["colour"]


def swap(value, exchange, ctx_count, head_count, phase):
    partner = {}
    pairs = [(b, b + exchange["offset"]) for b in exchange["firsts"]] + exchange["folds"]
    for a, b in pairs:
        partner[a], partner[b] = b, a
    pairs = []
    for b in range(ctx_count):
        for h in range(head_count):
            if b in partner:
                pairs.append((b * head_count + h, partner[b] * head_count + h))
            else:
                pairs.append((b * head_count + h, b * head_count + (h + 1) % head_count))
    with jax.named_scope(f"{phase}_{exchange['offset']}_{exchange['colour']}"):
        return lax.ppermute(value, ("ctx", "head"), pairs)


def fold_offsets(slot):
    return range(-(slot - 1), slot, 2)


def pack_kernel(sets, k_hbm, v_hbm, mine, *refs):
    halves = [s for s in sets if not s["full"]]
    outs, sems = refs[: len(halves)], refs[len(halves)]
    me = lax.axis_index("ctx")
    length = k_hbm.shape[0] // 2
    width = k_hbm.shape[1]
    copies = [
        pltpu.make_async_copy(k_hbm, mine.at[:, :width], sems.at[0]),
        pltpu.make_async_copy(v_hbm, mine.at[:, width:], sems.at[1]),
    ]
    for i, (entry, out) in enumerate(zip(halves, outs)):
        first = (me // entry["offset"]) % 2 == entry["colour"]
        rows = pl.ds(pl.multiple_of(jnp.where(first, 0, length), length), length)
        copies.append(pltpu.make_async_copy(k_hbm.at[rows, :], out.at[:, :width], sems.at[2 * i + 2]))
        copies.append(pltpu.make_async_copy(v_hbm.at[rows, :], out.at[:, width:], sems.at[2 * i + 3]))
    for copy in copies:
        copy.start()
    for copy in copies:
        copy.wait()


def stage_kernel(ctx_count, docs_hbm, q_hbm, g_hbm, q_all, g_all, bias, docs_ref, sems):
    length = q_hbm.shape[0] // 2
    heads, _, width = q_all.shape
    lengths = pltpu.make_async_copy(docs_hbm, docs_ref, sems.at[2, 0])
    lengths.start()
    copies = []
    for h in range(heads):
        cols = slice(h * width, (h + 1) * width)
        for a, (src, dst) in enumerate(((q_hbm, q_all), (g_hbm, g_all))):
            copies.append(pltpu.make_async_copy(src.at[:, cols], dst.at[h], sems.at[a, h]))
    for copy in copies:
        copy.start()
    lengths.wait()
    me = lax.axis_index("ctx")
    merged = bias.shape[1]
    row = lax.broadcasted_iota(jnp.int32, (merged, length), 0)
    col = lax.broadcasted_iota(jnp.int32, (1, length), 1)
    for s in range(2):
        stretch = me if s == 0 else 2 * ctx_count - 1 - me
        q_pos = stretch * length + col
        start = jnp.int32(0)
        doc_start = jnp.zeros((1, length), jnp.int32)
        for i in range(docs_ref.shape[0]):
            doc_start = jnp.where(q_pos >= start, start, doc_start)
            start = start + docs_ref[i]
        k_pos = row + (stretch - 2 * (row // length)) * length
        k_pos = jnp.where(k_pos > q_pos, k_pos - merged, k_pos)
        bias[s] = jnp.where(k_pos >= doc_start, 0.0, MASKED)
    for copy in copies:
        copy.wait()


def stacked(ref, s, first=0, last=None):
    length = ref.shape[1] // 2
    value = ref[first:last, s * length : (s + 1) * length, :]
    return value.reshape(-1, ref.shape[2])


def beside(ref, s, rows, heads=None):
    heads = range(ref.shape[1]) if heads is None else heads
    return jnp.concatenate([ref[s, h, rows, :] for h in heads], axis=1)


def score_kernel(sets, ctx_count, reach, bias, q_all, g_all, mine, *refs):
    count = len(sets)
    recs = {key_of(s): (r, s["full"]) for s, r in zip(sets, refs[:count])}
    pb, dsb, kv_win, own_ref = refs[count : count + 4]
    send_refs = refs[count + 4 : 2 * count + 4]
    acc, extra = refs[2 * count + 4 :]
    me = lax.axis_index("ctx")
    length = mine.shape[0] // 2
    width = HEAD_DIM
    heads = q_all.shape[0]
    merged = reach * length
    scaling = width ** (-0.5)
    log_scale = scaling * math.log2(math.e)

    def low_part(key):
        ref, full = recs[key]
        return ref[:length, :] if full else ref[...]

    def up_part(key):
        ref, full = recs[key]
        return ref[length:, :] if full else ref[...]

    def pick(part, offset, colour_pred):
        have = [c for c in range(2) if (offset, c) in recs]
        if len(have) == 1:
            return part((offset, have[0]))
        return jnp.where(colour_pred, part((offset, 1)), part((offset, 0)))

    lows = [mine[:length, :]]
    highs = [mine[length:, :]]
    for slot in range(1, reach + 1):
        odd = (me // slot) % 2 == 1
        lows.append(pick(low_part, slot, jnp.logical_not(odd)))
        highs.append(pick(up_part, slot, odd))
    for slot in range(1, reach + 1):
        folded = me + slot >= ctx_count
        value = highs[slot]
        for offset in fold_offsets(slot):
            here = folded & (2 * ctx_count - 1 - 2 * me - slot == offset)
            if offset <= 0:
                value = jnp.where(here, lows[-offset], value)
            else:
                for colour in range(2):
                    if recs.get((offset, colour), (None, False))[1]:
                        where = here & ((me // offset) % 2 == colour)
                        value = jnp.where(where, low_part((offset, colour)), value)
                for entry in sets:
                    for pair in entry["folds"]:
                        if pair[1] - pair[0] == offset:
                            where = here & (me == pair[0])
                            value = jnp.where(where, recs[key_of(entry)][0][...], value)
        highs[slot] = value
    for slot in range(reach + 1):
        rows = slice(slot * length, (slot + 1) * length)
        kv_win[0, rows, :] = lows[slot]
        kv_win[1, rows, :] = highs[slot]

    tri_row = lax.broadcasted_iota(jnp.int32, (length, length), 0)
    near = tri_row <= lax.broadcasted_iota(jnp.int32, (length, length), 1)
    near_low = jnp.where(near, 1.0, 0.0).astype(jnp.bfloat16)

    def fold(value):
        return jnp.where(near, value[:length, :], value[merged:, :])

    def products(s, h):
        contract_last = (((1,), (1,)), ((), ()))
        raw = lax.dot_general(
            kv_win[s, :, :width],
            stacked(q_all, s, h, h + group),
            contract_last,
            preferred_element_type=jnp.float32,
        )
        d_p = lax.dot_general(
            kv_win[s, :, width:],
            stacked(g_all, s, h, h + group),
            contract_last,
            preferred_element_type=jnp.float32,
        )
        return raw, d_p

    def soften(s, h, raw, d_p):
        raw = jnp.concatenate([fold(raw), raw[length:merged, :]], axis=0) + bias[s]
        d_p = jnp.concatenate([fold(d_p), d_p[length:merged, :]], axis=0)
        top = jnp.max(raw, axis=0, keepdims=True)
        weight = jnp.exp2((raw - top) * log_scale)
        total = jnp.sum(weight, axis=0, keepdims=True)
        inverse = 1.0 / total
        delta = jnp.sum(weight * d_p, axis=0, keepdims=True) * inverse
        weight = weight * inverse
        low = weight.astype(jnp.bfloat16)
        d_s = (weight * (d_p - delta)).astype(jnp.bfloat16)
        for ref, value in ((pb, low), (dsb, d_s)):
            here = value[:length, :] * near_low
            ref[s, h, :length, :] = here
            ref[s, h, length:merged, :] = value[length:, :]
            ref[s, h, merged:, :] = value[:length, :] - here

    def gradients(s, first, last):
        part = slice(length, None)
        d_k = jnp.dot(
            beside(dsb, s, part, range(first, last)),
            stacked(q_all, s, first, last),
            preferred_element_type=jnp.float32,
        )
        d_v = jnp.dot(
            beside(pb, s, part, range(first, last)),
            stacked(g_all, s, first, last),
            preferred_element_type=jnp.float32,
        )
        if first > 0:
            d_k = d_k + acc[s, part, :width]
            d_v = d_v + acc[s, part, width:]
        if last == heads:
            d_k = d_k * scaling
        acc[s, part, :width] = d_k
        acc[s, part, width:] = d_v

    chunk = CHUNK if heads % CHUNK == 0 else heads
    group = 2 if heads % 2 == 0 else 1
    items = [(s, h) for s in range(2) for h in range(0, heads, group)]
    ready = products(*items[0])
    for i, (s, h) in enumerate(items):
        following = products(*items[i + 1]) if i + 1 < len(items) else None
        for j in range(group):
            part = slice(j * length, (j + 1) * length)
            soften(s, h + j, ready[0][:, part], ready[1][:, part])
        ready = following
        if (h + group) % chunk == 0:
            gradients(s, h + group - chunk, h + group)

    def slot_rows(slot):
        return slice(slot * length, (slot + 1) * length)

    extra[...] = jnp.zeros(extra.shape, jnp.float32)
    for slot in range(1, reach + 1):
        for offset in fold_offsets(slot):

            @pl.when((me + slot >= ctx_count) & (2 * ctx_count - 1 - 2 * me - slot == offset))
            def _():
                part = acc[1, slot_rows(slot), :]
                if offset < 0:
                    acc[0, slot_rows(-offset), :] = acc[0, slot_rows(-offset), :] + part
                else:
                    extra[slot_rows(offset), :] = part

    own_ref[...] = extra[:length, :]
    for entry, ref in zip(sets, send_refs):
        offset = entry["offset"]
        first = (me // offset) % 2 == entry["colour"]
        to_low = acc[0, slot_rows(offset), :]
        to_up = acc[1, slot_rows(offset), :]
        if entry["full"]:
            more = extra[slot_rows(offset), :]
            ref[:length, :] = jnp.where(first, more, to_low).astype(jnp.bfloat16)
            ref[length:, :] = jnp.where(first, to_up, 0.0).astype(jnp.bfloat16)
        else:
            part = jnp.where(first, to_up, to_low)
            for pair in entry["folds"]:
                part = jnp.where(me == pair[0], extra[slot_rows(pair[1] - pair[0]), :], part)
            ref[...] = part.astype(jnp.bfloat16)


def output_kernel(pb, dsb, kv_win, q_all, g_all, att_hbm, dq_hbm, own_ref, att, dq, sems):
    length = att.shape[0] // 2
    width = HEAD_DIM
    heads = att.shape[1] // width
    scaling = width ** (-0.5)
    group = 2 if heads % 2 == 0 else 1
    copies = []
    for s in range(2):
        rows = slice(s * length, (s + 1) * length)
        k_turn = kv_win[s, :, :width].T
        v_turn = kv_win[s, :, width:].T
        for h in range(0, heads, group):
            pair = range(h, h + group)
            out_t = jnp.dot(v_turn, beside(pb, s, slice(None), pair), preferred_element_type=jnp.float32)
            dq_t = jnp.dot(k_turn, beside(dsb, s, slice(None), pair), preferred_element_type=jnp.float32) * scaling
            out_t = out_t.astype(jnp.bfloat16)
            dq_t = dq_t.astype(jnp.bfloat16)
            for i in range(group):
                part = slice(i * length, (i + 1) * length)
                cols = slice((h + i) * width, (h + i + 1) * width)
                att[rows, cols] = out_t[:, part].T
                dq[rows, cols] = dq_t[:, part].T
        for a, (src, dst) in enumerate(((att, att_hbm), (dq, dq_hbm))):
            copy = pltpu.make_async_copy(src.at[rows, :], dst.at[rows, :], sems.at[s, a])
            copy.start()
            copies.append(copy)
        d_k = jnp.dot(beside(dsb, s, slice(0, length)), stacked(q_all, s), preferred_element_type=jnp.float32)
        d_v = jnp.dot(beside(pb, s, slice(0, length)), stacked(g_all, s), preferred_element_type=jnp.float32)
        own_ref[rows, :width] = d_k * scaling
        own_ref[rows, width:] = d_v
    for copy in copies:
        copy.wait()


def sum_kernel(sets, ctx_count, own_ref, fold_ref, *refs):
    dk_ref, dv_ref = refs[len(sets) :]
    me = lax.axis_index("ctx")
    length = own_ref.shape[0] // 2
    width = dk_ref.shape[1]
    low = own_ref[:length, :] + fold_ref[...]
    up = own_ref[length:, :]
    for entry, ref in zip(sets, refs):
        offset = entry["offset"]
        first = (me // offset) % 2 == entry["colour"]
        as_first = first & (me + offset < ctx_count)
        as_second = jnp.logical_not(first) & (me >= offset)
        if entry["full"]:
            low = low + jnp.where(as_first | as_second, ref[:length, :].astype(jnp.float32), 0.0)
            up = up + jnp.where(as_second, ref[length:, :].astype(jnp.float32), 0.0)
        else:
            part = ref[...].astype(jnp.float32)
            for pair in entry["folds"]:
                as_first = as_first & (me != pair[0]) | (me == pair[1])
            low = low + jnp.where(as_first, part, 0.0)
            up = up + jnp.where(as_second, part, 0.0)
    dk_ref[:length, :] = low[:, :width].astype(jnp.bfloat16)
    dk_ref[length:, :] = up[:, :width].astype(jnp.bfloat16)
    dv_ref[:length, :] = low[:, width:].astype(jnp.bfloat16)
    dv_ref[length:, :] = up[:, width:].astype(jnp.bfloat16)


def in_vmem(amount):
    return [pl.BlockSpec(memory_space=pltpu.VMEM)] * amount


def in_place(amount):
    return [pl.BlockSpec(memory_space=pl.ANY)] * amount


def on_chip(values):
    return [pltpu.with_memory_space_constraint(v, pltpu.VMEM) for v in values]


def off_chip(values):
    return [pltpu.with_memory_space_constraint(v, pltpu.HBM) for v in values]


def shards(query_rows, key_rows, value_rows, out_grad, doc_lengths):
    ctx_count = lax.axis_size("ctx")
    head_count = lax.axis_size("head")
    tok_dev = query_rows.shape[0]
    length = tok_dev // 2
    width = key_rows.shape[1]
    reach = min(DOC_STRETCHES, ctx_count // 4)
    span = (reach + 1) * length
    heads = query_rows.shape[1] // width
    sets = exchanges(ctx_count, reach)
    fulls = sum(s["full"] for s in sets)
    count = len(sets)
    payloads = [
        pltpu.VMEM((2 * length if s["full"] else length, 2 * width), jnp.bfloat16) for s in sets
    ]
    mine, *halves = pl.pallas_call(
        lambda *refs: pack_kernel(sets, *refs),
        out_shape=[pltpu.VMEM((tok_dev, 2 * width), jnp.bfloat16)] + payloads[fulls:],
        in_specs=in_place(2),
        out_specs=in_vmem(1 + count - fulls),
        scratch_shapes=[pltpu.SemaphoreType.DMA((2 + 2 * (count - fulls),))],
        compiler_params=pltpu.CompilerParams(vmem_limit_bytes=VMEM_LIMIT),
        name="pack",
    )(*off_chip([key_rows, value_rows]))
    packed = [mine] * fulls + halves
    received = [swap(p, s, ctx_count, head_count, "fetch") for p, s in zip(packed, sets)]

    stack = pltpu.VMEM((heads, tok_dev, width), jnp.bfloat16)
    q_all, g_all, bias = pl.pallas_call(
        lambda *refs: stage_kernel(ctx_count, *refs),
        out_shape=[stack, stack, pltpu.VMEM((2, reach * length, length), jnp.float32)],
        in_specs=in_place(3),
        out_specs=in_vmem(3),
        scratch_shapes=[
            pltpu.SMEM(doc_lengths.shape, jnp.int32),
            pltpu.SemaphoreType.DMA((3, heads)),
        ],
        compiler_params=pltpu.CompilerParams(vmem_limit_bytes=VMEM_LIMIT),
        name="stage",
    )(*off_chip([doc_lengths, query_rows, out_grad]))

    low_weights = pltpu.VMEM((2, heads, span, length), jnp.bfloat16)
    pb, dsb, kv_win, folded, *partials = pl.pallas_call(
        lambda *refs: score_kernel(sets, ctx_count, reach, *refs),
        out_shape=[
            low_weights,
            low_weights,
            pltpu.VMEM((2, span, 2 * width), jnp.bfloat16),
            pltpu.VMEM((length, 2 * width), jnp.float32),
        ]
        + payloads,
        in_specs=in_vmem(4 + count),
        out_specs=in_vmem(4 + count),
        scratch_shapes=[
            pltpu.VMEM((2, span, 2 * width), jnp.float32),
            pltpu.VMEM((reach * length, 2 * width), jnp.float32),
        ],
        compiler_params=pltpu.CompilerParams(vmem_limit_bytes=VMEM_LIMIT),
        name="score",
    )(*on_chip([bias, q_all, g_all, mine, *received]))
    returned = [swap(p, s, ctx_count, head_count, "give") for p, s in zip(partials, sets)]

    attended, query_grad, own = pl.pallas_call(
        output_kernel,
        out_shape=[jax.ShapeDtypeStruct(query_rows.shape, jnp.bfloat16)] * 2
        + [pltpu.VMEM((tok_dev, 2 * width), jnp.float32)],
        in_specs=in_vmem(5),
        out_specs=in_place(2) + in_vmem(1),
        scratch_shapes=[
            pltpu.VMEM(query_rows.shape, jnp.bfloat16),
            pltpu.VMEM(query_rows.shape, jnp.bfloat16),
            pltpu.SemaphoreType.DMA((2, 2)),
        ],
        compiler_params=pltpu.CompilerParams(vmem_limit_bytes=VMEM_LIMIT),
        name="output",
    )(*on_chip([pb, dsb, kv_win, q_all, g_all]))

    key_grad, value_grad = pl.pallas_call(
        lambda *refs: sum_kernel(sets, ctx_count, *refs),
        out_shape=[jax.ShapeDtypeStruct(key_rows.shape, jnp.bfloat16)] * 2,
        in_specs=in_vmem(2 + count),
        out_specs=in_vmem(2),
        compiler_params=pltpu.CompilerParams(vmem_limit_bytes=VMEM_LIMIT),
        name="total",
    )(*on_chip([own, folded, *returned]))
    return (attended, query_grad, key_grad, value_grad)


def solution(mesh):
    placed = (
        P(("groups", "ctx"), "head"),
        P(("groups", "ctx"), "head"),
        P(("groups", "ctx"), "head"),
        P(("groups", "ctx"), "head"),
        P("groups"),
    )
    return jax.shard_map(
        shards,
        mesh=mesh,
        in_specs=placed,
        out_specs=(P(("groups", "ctx"), "head"),) * 4,
        check_vma=False,
    )
```

time: 21.9 us -> 20.8 us (0.950)
  Pallas kernels: 8.73 us -> 7.51 us
  waiting for transfers between devices: 2.72 us -> 3.48 us
  local copies, waits for them, and re-layouts: 0.66 us -> 0 us
    pallas_call x1, Pallas kernels: 3.3 us -> 2.41 us  [shards(): pl.pallas_call(lambda *refs: score_kernel(sets, ctx_count, reach, *refs),...]
    ppermute x8, waiting for transfers between devices: 2.72 us -> 3.48 us  [swap(): return lax.ppermute(value, ('ctx', 'head'), pairs)]
    unnamed x2 -> x0, local copies, waits for them, and re-layouts: 0.66 us -> none
    pallas_call x1, Pallas kernels: 2.01 us -> 1.47 us  [shards(): pl.pallas_call(lambda *refs: stage_kernel(ctx_count, *refs), out_shape=[s...]
  transfers between devices with their start and end apart: 8 -> 8, of which waited for: 2 -> 2; matrix products, arithmetic and copies ran while one was open for 0% -> 0% of each run, Pallas kernels for 17% -> 16%
where the time goes in v3:
time: 20.8 us; the launch traced here: 20.5 us
  starting transfers between devices  8.84 us (42%)
  Pallas kernels  7.51 us (36%)
  waiting for transfers between devices  3.48 us (17%)
  between operations  0.7 us (3%)
    ppermute x8, starting transfers between devices, swap(): return lax.ppermute(value, ('ctx', 'head'), pairs)  8.84 us
    ppermute x8, waiting for transfers between devices, swap(): return lax.ppermute(value, ('ctx', 'head'), pairs)  3.48 us
    pallas_call x1, Pallas kernels, shards(): pl.pallas_call(lambda *refs: score_kernel(sets, ctx_count, reach, *refs),...  2.41 us
    pallas_call x1, Pallas kernels, shards(): pl.pallas_call(output_kernel, out_shape=[jax.ShapeDtypeStruct(query_rows....  1.81 us
    pallas_call x1, Pallas kernels, shards(): pl.pallas_call(lambda *refs: stage_kernel(ctx_count, *refs), out_shape=[s...  1.47 us
    pallas_call x1, Pallas kernels, shards(): pl.pallas_call(lambda *refs: pack_kernel(sets, *refs), out_shape=[pltpu.V...  1.06 us
    pallas_call x1, Pallas kernels, shards(): pl.pallas_call(lambda *refs: sum_kernel(sets, ctx_count, *refs), out_shap...  0.77 us
  transfers between devices with their start and end apart: 8, of which 2 were waited for; matrix products, arithmetic and copies ran while one was open for 0% of the time, Pallas kernels for 16%

profile of v3, /device:TPU:0, one launch (start us, length us, event | category | flops | bytes accessed | tf_op | source)
XLA Modules:
  0.0 20.5 jit_solution(8266641195122782244)
XLA Ops:
  0.6 1.1 %pack.1 = (bf16[256,256]{1,0:T(8,128)(2,1)S(1)}, bf16[128,256]{1,0:T(8,128)(2,1)S(1)}, bf16[128,256]{1,0:T(8,128)(2,1)S(1)}, bf16[128,256]{1,0:T(8,128)(2,1)S(1)}, bf16[128,256]{1,0:T(8,128)(2,1)S(1)}) custom-call(bf16[256,128]{1,0:T(8,128)(2,1)} %refs_0_.3, bf16[256,128]{1,0:T(8,128)(2,1)} %refs_1_.3), custom_call_target="tpu_custom_call" | custom-call | tf_op jit(solution)/shard_map/pack/pallas_call | solution.py:392
  1.7 3.1 %collective-permute-start = (bf16[128,256]{1,0:T(8,128)(2,1)S(1)}, bf16[128,256]{1,0:T(8,128)(2,1)S(1)}, u32[]{:S(2)}, u32[]{:S(2)}) collective-permute-start(bf16[128,256]{1,0:T(8,128)(2,1)S(1)} %get-tuple-element.29), channel_id=1, source_target_pairs={{0,2},{1,3},{2,0},{3,1},{4,6},{5,7},{6,4},{7,5},{8,10},{9,11},{10,... | collective-permute-start | bytes 196616 | tf_op jit(solution)/shard_map/fetch_1_0/ppermute | solution.py:67
  4.8 0.0 collective-permute-start.1
  4.8 1.6 %collective-permute-start.2 = (bf16[128,256]{1,0:T(8,128)(2,1)S(1)}, bf16[128,256]{1,0:T(8,128)(2,1)S(1)}, u32[]{:S(2)}, u32[]{:S(2)}) collective-permute-start(bf16[128,256]{1,0:T(8,128)(2,1)S(1)} %get-tuple-element.31), channel_id=1, source_target_pairs={{0,4},{1,5},{2,6},{3,7},{4,0},{5,1},{6,2},{7,3},{8,12},{9,13},{10,... | collective-permute-start | bytes 196616 | tf_op jit(solution)/shard_map/fetch_2_0/ppermute | solution.py:67
  6.3 0.0 collective-permute-start.3
  6.3 1.5 %stage.1 = (bf16[8,256,128]{2,1,0:T(8,128)(2,1)S(1)}, bf16[8,256,128]{2,1,0:T(8,128)(2,1)S(1)}, f32[2,256,128]{2,1,0:T(8,128)S(1)}) custom-call(s32[16]{0:T(128)} %refs_0_.2, bf16[256,1024]{1,0:T(8,128)(2,1)} %refs_1_.2, bf16[256,1024]{1,0:T(8,128)(2,1)} %refs_2_.1), custom_call_target="tpu_custom_call" | custom-call | tf_op jit(solution)/shard_map/stage/pallas_call | solution.py:405
  7.8 0.0 collective-permute-done.refs_4_
  7.8 0.0 collective-permute-done.1.refs_5_
  7.8 2.1 %collective-permute-done.2.refs_6_ = bf16[128,256]{1,0:T(8,128)(2,1)S(1)} collective-permute-done((bf16[128,256]{1,0:T(8,128)(2,1)S(1)}, bf16[128,256]{1,0:T(8,128)(2,1)S(1)}, u32[]{:S(2)}, u32[]{:S(2)}) %collective-permute-start.2) | collective-permute-done | bytes 65568 | tf_op jit(solution)/shard_map/fetch_2_0/ppermute | solution.py:67
  10.0 0.0 collective-permute-done.3.refs_7_
  10.0 2.4 %score.1 = (bf16[2,8,384,128]{3,2,1,0:T(8,128)(2,1)S(1)}, bf16[2,8,384,128]{3,2,1,0:T(8,128)(2,1)S(1)}, bf16[2,384,256]{2,1,0:T(8,128)(2,1)S(1)}, f32[128,256]{1...) custom-call(f32[2,256,128]{2,1,0:T(8,128)S(1)} %get-tuple-element.25, ...), custom_call_target="tpu_custom_call" | custom-call | tf_op jit(solution)/shard_map/score/pallas_call | solution.py:419
  12.4 2.2 %collective-permute-start.4 = (bf16[128,256]{1,0:T(8,128)(2,1)S(1)}, bf16[128,256]{1,0:T(8,128)(2,1)S(1)}, u32[]{:S(2)}, u32[]{:S(2)}) collective-permute-start(bf16[128,256]{1,0:T(8,128)(2,1)S(1)} %get-tuple-element.40), channel_id=1, source_target_pairs={{0,2},{1,3},{2,0},{3,1},{4,6},{5,7},{6,4},{7,5},{8,10},{9,11},{10,... | collective-permute-start | bytes 196616 | tf_op jit(solution)/shard_map/give_1_0/ppermute | solution.py:67
  14.5 0.0 collective-permute-start.5
  14.6 2.0 %collective-permute-start.6 = (bf16[128,256]{1,0:T(8,128)(2,1)S(1)}, bf16[128,256]{1,0:T(8,128)(2,1)S(1)}, u32[]{:S(2)}, u32[]{:S(2)}) collective-permute-start(bf16[128,256]{1,0:T(8,128)(2,1)S(1)} %get-tuple-element.42), channel_id=1, source_target_pairs={{0,4},{1,5},{2,6},{3,7},{4,0},{5,1},{6,2},{7,3},{8,12},{9,13},{10,... | collective-permute-start | bytes 196616 | tf_op jit(solution)/shard_map/give_2_0/ppermute | solution.py:67
  16.6 0.0 collective-permute-start.7
  16.6 1.8 %output.1 = (bf16[256,1024]{1,0:T(8,128)(2,1)}, bf16[256,1024]{1,0:T(8,128)(2,1)}, f32[256,256]{1,0:T(8,128)S(1)}) custom-call(bf16[2,8,384,128]{3,2,1,0:T(8,128)(2,1)S(1)} %get-tuple-element.33.pb, bf16[2,8,384,128]{3,2,1,0:T(8,128)(2,1)S(1)} %get-tuple-element.34.dsb, bf16[2,384,256]{2,1,0:T(8,128)(2,1)S(1)} %get-tuple-element.35.kv_win, ...), custom_call_target="tpu_custom_call" | custom-call | tf_op jit(solution)/shard_map/output/pallas_call | solution.py:439
  18.4 0.0 collective-permute-done.4.refs_2_
  18.4 0.0 collective-permute-done.5.refs_3_
  18.4 1.3 %collective-permute-done.6.refs_4_ = bf16[128,256]{1,0:T(8,128)(2,1)S(1)} collective-permute-done((bf16[128,256]{1,0:T(8,128)(2,1)S(1)}, bf16[128,256]{1,0:T(8,128)(2,1)S(1)}, u32[]{:S(2)}, u32[]{:S(2)}) %collective-permute-start.6) | collective-permute-done | bytes 65568 | tf_op jit(solution)/shard_map/give_2_0/ppermute | solution.py:67
  19.8 0.0 collective-permute-done.7.refs_5_
  19.8 0.8 %total.1 = (bf16[256,128]{1,0:T(8,128)(2,1)}, bf16[256,128]{1,0:T(8,128)(2,1)}) custom-call(f32[256,256]{1,0:T(8,128)S(1)} %get-tuple-element.38.refs_0_, f32[128,256]{1,0:T(8,128)S(1)} %get-tuple-element.39.refs_1_, bf16[128,256]{1,0:T(8,128)(2,1)S(1)} %collective-permute-done.4.refs_2_, bf16[128,256]{1,0:T(8,128)(2,1)S(1)} %collective-permute-done.5.refs_3_, ...), custom_call_target="tpu_custom_call" | custom-call | tf_op jit(solution)/shard_map/total/pallas_call | solution.py:454
Async XLA Ops:
  1.7 6.1 %collective-permute-start = (bf16[128,256]{1,0:T(8,128)(2,1)S(1)}, bf16[128,256]{1,0:T(8,128)(2,1)S(1)}, u32[]{:S(2)}, u32[]{:S(2)}) collective-permute-start(bf16[128,256]{1,0:T(8,128)(2,1)S(1)} %get-tuple-element.29), channel_id=1, source_target_pairs={{0,2},{1,3},{2,0},{3,1},{4,6},{5,7},{6,4},{7,5},{8,10},{9,11},{10,... | collective-permute-start | bytes 196616 | tf_op jit(solution)/shard_map/fetch_1_0/ppermute | solution.py:67
  4.8 3.1 %collective-permute-start.1 = (bf16[128,256]{1,0:T(8,128)(2,1)S(1)}, bf16[128,256]{1,0:T(8,128)(2,1)S(1)}, u32[]{:S(2)}, u32[]{:S(2)}) collective-permute-start(bf16[128,256]{1,0:T(8,128)(2,1)S(1)} %get-tuple-element.30), channel_id=1, source_target_pairs={{0,1},{1,0},{2,4},{3,5},{4,2},{5,3},{6,8},{7,9},{8,6},{9,7},{10,12... | collective-permute-start | bytes 196616 | tf_op jit(solution)/shard_map/fetch_1_1/ppermute | solution.py:67
  4.8 5.2 %collective-permute-start.2 = (bf16[128,256]{1,0:T(8,128)(2,1)S(1)}, bf16[128,256]{1,0:T(8,128)(2,1)S(1)}, u32[]{:S(2)}, u32[]{:S(2)}) collective-permute-start(bf16[128,256]{1,0:T(8,128)(2,1)S(1)} %get-tuple-element.31), channel_id=1, source_target_pairs={{0,4},{1,5},{2,6},{3,7},{4,0},{5,1},{6,2},{7,3},{8,12},{9,13},{10,... | collective-permute-start | bytes 196616 | tf_op jit(solution)/shard_map/fetch_2_0/ppermute | solution.py:67
  6.3 3.6 %collective-permute-start.3 = (bf16[128,256]{1,0:T(8,128)(2,1)S(1)}, bf16[128,256]{1,0:T(8,128)(2,1)S(1)}, u32[]{:S(2)}, u32[]{:S(2)}) collective-permute-start(bf16[128,256]{1,0:T(8,128)(2,1)S(1)} %get-tuple-element.32), channel_id=1, source_target_pairs={{0,1},{1,0},{2,3},{3,2},{4,8},{5,9},{6,10},{7,11},{8,4},{9,5},{10,... | collective-permute-start | bytes 196616 | tf_op jit(solution)/shard_map/fetch_2_1/ppermute | solution.py:67
  12.4 6.0 %collective-permute-start.4 = (bf16[128,256]{1,0:T(8,128)(2,1)S(1)}, bf16[128,256]{1,0:T(8,128)(2,1)S(1)}, u32[]{:S(2)}, u32[]{:S(2)}) collective-permute-start(bf16[128,256]{1,0:T(8,128)(2,1)S(1)} %get-tuple-element.40), channel_id=1, source_target_pairs={{0,2},{1,3},{2,0},{3,1},{4,6},{5,7},{6,4},{7,5},{8,10},{9,11},{10,... | collective-permute-start | bytes 196616 | tf_op jit(solution)/shard_map/give_1_0/ppermute | solution.py:67
  14.5 3.9 %collective-permute-start.5 = (bf16[128,256]{1,0:T(8,128)(2,1)S(1)}, bf16[128,256]{1,0:T(8,128)(2,1)S(1)}, u32[]{:S(2)}, u32[]{:S(2)}) collective-permute-start(bf16[128,256]{1,0:T(8,128)(2,1)S(1)} %get-tuple-element.41), channel_id=1, source_target_pairs={{0,1},{1,0},{2,4},{3,5},{4,2},{5,3},{6,8},{7,9},{8,6},{9,7},{10,12... | collective-permute-start | bytes 196616 | tf_op jit(solution)/shard_map/give_1_1/ppermute | solution.py:67
  14.6 5.2 %collective-permute-start.6 = (bf16[128,256]{1,0:T(8,128)(2,1)S(1)}, bf16[128,256]{1,0:T(8,128)(2,1)S(1)}, u32[]{:S(2)}, u32[]{:S(2)}) collective-permute-start(bf16[128,256]{1,0:T(8,128)(2,1)S(1)} %get-tuple-element.42), channel_id=1, source_target_pairs={{0,4},{1,5},{2,6},{3,7},{4,0},{5,1},{6,2},{7,3},{8,12},{9,13},{10,... | collective-permute-start | bytes 196616 | tf_op jit(solution)/shard_map/give_2_0/ppermute | solution.py:67
  16.6 3.2 %collective-permute-start.7 = (bf16[128,256]{1,0:T(8,128)(2,1)S(1)}, bf16[128,256]{1,0:T(8,128)(2,1)S(1)}, u32[]{:S(2)}, u32[]{:S(2)}) collective-permute-start(bf16[128,256]{1,0:T(8,128)(2,1)S(1)} %get-tuple-element.43), channel_id=1, source_target_pairs={{0,1},{1,0},{2,3},{3,2},{4,8},{5,9},{6,10},{7,11},{8,4},{9,5},{10,... | collective-permute-start | bytes 196616 | tf_op jit(solution)/shard_map/give_2_1/ppermute | solution.py:67

commit v4 on v3

--- a/solution.py
+++ b/solution.py
@@ -11,7 +11,6 @@
 DOC_STRETCHES = 8
 MASKED = -1e30
 VMEM_LIMIT = 24 << 20
-CHUNK = 4
 
 
 def exchanges(ctx_count, reach):
@@ -130,9 +129,11 @@
     return value.reshape(-1, ref.shape[2])
 
 
-def beside(ref, s, rows, heads=None):
-    heads = range(ref.shape[1]) if heads is None else heads
-    return jnp.concatenate([ref[s, h, rows, :] for h in heads], axis=1)
+def unfolded(ref, s, h, near_low):
+    length = ref.shape[3]
+    value = ref[s, h]
+    own = value[:length, :] * near_low
+    return jnp.concatenate([own, value[length:, :], value[:length, :] - own], axis=0)
 
 
 def score_kernel(sets, ctx_count, reach, bias, q_all, g_all, mine, *refs):
@@ -194,7 +195,7 @@
 
     tri_row = lax.broadcasted_iota(jnp.int32, (length, length), 0)
     near = tri_row <= lax.broadcasted_iota(jnp.int32, (length, length), 1)
-    near_low = jnp.where(near, 1.0, 0.0).astype(jnp.bfloat16)
+    far_low = jnp.where(near, 0.0, 1.0).astype(jnp.bfloat16)
 
     def fold(value):
         return jnp.where(near, value[:length, :], value[merged:, :])
@@ -224,26 +225,20 @@
         inverse = 1.0 / total
         delta = jnp.sum(weight * d_p, axis=0, keepdims=True) * inverse
         weight = weight * inverse
-        low = weight.astype(jnp.bfloat16)
-        d_s = (weight * (d_p - delta)).astype(jnp.bfloat16)
-        for ref, value in ((pb, low), (dsb, d_s)):
-            here = value[:length, :] * near_low
-            ref[s, h, :length, :] = here
-            ref[s, h, length:merged, :] = value[length:, :]
-            ref[s, h, merged:, :] = value[:length, :] - here
-
-    def gradients(s, first, last):
+        others = []
+        for ref, value in ((pb, weight), (dsb, weight * (d_p - delta))):
+            value = value.astype(jnp.bfloat16)
+            ref[s, h] = value
+            others.append(jnp.concatenate([value[length:, :], value[:length, :] * far_low], axis=0))
+        return others
+
+    def gradients(s, first, last, done):
         part = slice(length, None)
+        weights, d_scores = [jnp.concatenate(values, axis=1) for values in zip(*done)]
         d_k = jnp.dot(
-            beside(dsb, s, part, range(first, last)),
-            stacked(q_all, s, first, last),
-            preferred_element_type=jnp.float32,
+            d_scores, stacked(q_all, s, first, last), preferred_element_type=jnp.float32
         )
-        d_v = jnp.dot(
-            beside(pb, s, part, range(first, last)),
-            stacked(g_all, s, first, last),
-            preferred_element_type=jnp.float32,
-        )
+        d_v = jnp.dot(weights, stacked(g_all, s, first, last), preferred_element_type=jnp.float32)
         if first > 0:
             d_k = d_k + acc[s, part, :width]
             d_v = d_v + acc[s, part, width:]
@@ -252,18 +247,20 @@
         acc[s, part, :width] = d_k
         acc[s, part, width:] = d_v
 
-    chunk = CHUNK if heads % CHUNK == 0 else heads
     group = 2 if heads % 2 == 0 else 1
     items = [(s, h) for s in range(2) for h in range(0, heads, group)]
+    stops = [{heads // 2, heads}, {heads - group, heads}]
+    done = []
     ready = products(*items[0])
     for i, (s, h) in enumerate(items):
         following = products(*items[i + 1]) if i + 1 < len(items) else None
         for j in range(group):
             part = slice(j * length, (j + 1) * length)
-            soften(s, h + j, ready[0][:, part], ready[1][:, part])
+            done.append(soften(s, h + j, ready[0][:, part], ready[1][:, part]))
         ready = following
-        if (h + group) % chunk == 0:
-            gradients(s, h + group - chunk, h + group)
+        if h + group in stops[s]:
+            gradients(s, h + group - len(done), h + group, done)
+            done = []
 
     def slot_rows(slot):
         return slice(slot * length, (slot + 1) * length)
@@ -284,14 +281,15 @@
     for entry, ref in zip(sets, send_refs):
         offset = entry["offset"]
         first = (me // offset) % 2 == entry["colour"]
-        to_low = acc[0, slot_rows(offset), :]
-        to_up = acc[1, slot_rows(offset), :]
+        side = jnp.where(first, 1, 0)
         if entry["full"]:
+            to_low = acc[0, slot_rows(offset), :]
+            to_up = acc[1, slot_rows(offset), :]
             more = extra[slot_rows(offset), :]
             ref[:length, :] = jnp.where(first, more, to_low).astype(jnp.bfloat16)
             ref[length:, :] = jnp.where(first, to_up, 0.0).astype(jnp.bfloat16)
         else:
-            part = jnp.where(first, to_up, to_low)
+            part = acc[side, slot_rows(offset), :]
             for pair in entry["folds"]:
                 part = jnp.where(me == pair[0], extra[slot_rows(pair[1] - pair[0]), :], part)
             ref[...] = part.astype(jnp.bfloat16)
@@ -303,17 +301,28 @@
     heads = att.shape[1] // width
     scaling = width ** (-0.5)
     group = 2 if heads % 2 == 0 else 1
+    tri_row = lax.broadcasted_iota(jnp.int32, (length, length), 0)
+    tri_col = lax.broadcasted_iota(jnp.int32, (length, length), 1)
+    near_low = jnp.where(tri_row <= tri_col, 1.0, 0.0).astype(jnp.bfloat16)
     copies = []
     for s in range(2):
         rows = slice(s * length, (s + 1) * length)
         k_turn = kv_win[s, :, :width].T
         v_turn = kv_win[s, :, width:].T
+        own_weights, own_scores = [], []
         for h in range(0, heads, group):
-            pair = range(h, h + group)
-            out_t = jnp.dot(v_turn, beside(pb, s, slice(None), pair), preferred_element_type=jnp.float32)
-            dq_t = jnp.dot(k_turn, beside(dsb, s, slice(None), pair), preferred_element_type=jnp.float32) * scaling
+            weights = [unfolded(pb, s, h + i, near_low) for i in range(group)]
+            d_scores = [unfolded(dsb, s, h + i, near_low) for i in range(group)]
+            own_weights += [value[:length, :] for value in weights]
+            own_scores += [value[:length, :] for value in d_scores]
+            out_t = jnp.dot(
+                v_turn, jnp.concatenate(weights, axis=1), preferred_element_type=jnp.float32
+            )
+            dq_t = jnp.dot(
+                k_turn, jnp.concatenate(d_scores, axis=1), preferred_element_type=jnp.float32
+            )
             out_t = out_t.astype(jnp.bfloat16)
-            dq_t = dq_t.astype(jnp.bfloat16)
+            dq_t = (dq_t * scaling).astype(jnp.bfloat16)
             for i in range(group):
                 part = slice(i * length, (i + 1) * length)
                 cols = slice((h + i) * width, (h + i + 1) * width)
@@ -323,8 +332,16 @@
             copy = pltpu.make_async_copy(src.at[rows, :], dst.at[rows, :], sems.at[s, a])
             copy.start()
             copies.append(copy)
-        d_k = jnp.dot(beside(dsb, s, slice(0, length)), stacked(q_all, s), preferred_element_type=jnp.float32)
-        d_v = jnp.dot(beside(pb, s, slice(0, length)), stacked(g_all, s), preferred_element_type=jnp.float32)
+        d_k = jnp.dot(
+            jnp.concatenate(own_scores, axis=1),
+            stacked(q_all, s),
+            preferred_element_type=jnp.float32,
+        )
+        d_v = jnp.dot(
+            jnp.concatenate(own_weights, axis=1),
+            stacked(g_all, s),
+            preferred_element_type=jnp.float32,
+        )
         own_ref[rows, :width] = d_k * scaling
         own_ref[rows, width:] = d_v
     for copy in copies:
@@ -415,7 +432,7 @@
         name="stage",
     )(*off_chip([doc_lengths, query_rows, out_grad]))
 
-    low_weights = pltpu.VMEM((2, heads, span, length), jnp.bfloat16)
+    low_weights = pltpu.VMEM((2, heads, reach * length, length), jnp.bfloat16)
     pb, dsb, kv_win, folded, *partials = pl.pallas_call(
         lambda *refs: score_kernel(sets, ctx_count, reach, *refs),
         out_shape=[

time: 20.8 us -> 20.4 us (0.981)
  Pallas kernels: 7.51 us -> 7.19 us
    pallas_call x1, Pallas kernels: 2.41 us -> 2.06 us  [shards(): pl.pallas_call(lambda *refs: score_kernel(sets, ctx_count, reach, *refs),...]
where the time goes in v4:
time: 20.4 us; the launch traced here: 20.2 us
  starting transfers between devices  8.84 us (43%)
  Pallas kernels  7.19 us (35%)
  waiting for transfers between devices  3.46 us (17%)
  between operations  0.7 us (3%)
    ppermute x8, starting transfers between devices, swap(): return lax.ppermute(value, ('ctx', 'head'), pairs)  8.84 us
    ppermute x8, waiting for transfers between devices, swap(): return lax.ppermute(value, ('ctx', 'head'), pairs)  3.46 us
    pallas_call x1, Pallas kernels, shards(): pl.pallas_call(lambda *refs: score_kernel(sets, ctx_count, reach, *refs),...  2.06 us
    pallas_call x1, Pallas kernels, shards(): pl.pallas_call(output_kernel, out_shape=[jax.ShapeDtypeStruct(query_rows....  1.83 us
    pallas_call x1, Pallas kernels, shards(): pl.pallas_call(lambda *refs: stage_kernel(ctx_count, *refs), out_shape=[s...  1.47 us
    pallas_call x1, Pallas kernels, shards(): pl.pallas_call(lambda *refs: pack_kernel(sets, *refs), out_shape=[pltpu.V...  1.06 us
    pallas_call x1, Pallas kernels, shards(): pl.pallas_call(lambda *refs: sum_kernel(sets, ctx_count, *refs), out_shap...  0.77 us
  transfers between devices with their start and end apart: 8, of which 2 were waited for; matrix products, arithmetic and copies ran while one was open for 0% of the time, Pallas kernels for 16%

profile of v4, /device:TPU:0, one launch (start us, length us, event | category | flops | bytes accessed | tf_op | source)
XLA Modules:
  0.0 20.2 jit_solution(1171822764013442662)
XLA Ops:
  0.6 1.1 %pack.1 = (bf16[256,256]{1,0:T(8,128)(2,1)S(1)}, bf16[128,256]{1,0:T(8,128)(2,1)S(1)}, bf16[128,256]{1,0:T(8,128)(2,1)S(1)}, bf16[128,256]{1,0:T(8,128)(2,1)S(1)}, bf16[128,256]{1,0:T(8,128)(2,1)S(1)}) custom-call(bf16[256,128]{1,0:T(8,128)(2,1)} %refs_0_.3, bf16[256,128]{1,0:T(8,128)(2,1)} %refs_1_.3), custom_call_target="tpu_custom_call" | custom-call | tf_op jit(solution)/shard_map/pack/pallas_call | solution.py:409
  1.7 3.1 %collective-permute-start = (bf16[128,256]{1,0:T(8,128)(2,1)S(1)}, bf16[128,256]{1,0:T(8,128)(2,1)S(1)}, u32[]{:S(2)}, u32[]{:S(2)}) collective-permute-start(bf16[128,256]{1,0:T(8,128)(2,1)S(1)} %get-tuple-element.29), channel_id=1, source_target_pairs={{0,2},{1,3},{2,0},{3,1},{4,6},{5,7},{6,4},{7,5},{8,10},{9,11},{10,... | collective-permute-start | bytes 196616 | tf_op jit(solution)/shard_map/fetch_1_0/ppermute | solution.py:66
  4.8 0.0 collective-permute-start.1
  4.8 1.6 %collective-permute-start.2 = (bf16[128,256]{1,0:T(8,128)(2,1)S(1)}, bf16[128,256]{1,0:T(8,128)(2,1)S(1)}, u32[]{:S(2)}, u32[]{:S(2)}) collective-permute-start(bf16[128,256]{1,0:T(8,128)(2,1)S(1)} %get-tuple-element.31), channel_id=1, source_target_pairs={{0,4},{1,5},{2,6},{3,7},{4,0},{5,1},{6,2},{7,3},{8,12},{9,13},{10,... | collective-permute-start | bytes 196616 | tf_op jit(solution)/shard_map/fetch_2_0/ppermute | solution.py:66
  6.3 0.0 collective-permute-start.3
  6.3 1.5 %stage.1 = (bf16[8,256,128]{2,1,0:T(8,128)(2,1)S(1)}, bf16[8,256,128]{2,1,0:T(8,128)(2,1)S(1)}, f32[2,256,128]{2,1,0:T(8,128)S(1)}) custom-call(s32[16]{0:T(128)} %refs_0_.2, bf16[256,1024]{1,0:T(8,128)(2,1)} %refs_1_.2, bf16[256,1024]{1,0:T(8,128)(2,1)} %refs_2_.1), custom_call_target="tpu_custom_call" | custom-call | tf_op jit(solution)/shard_map/stage/pallas_call | solution.py:422
  7.8 0.0 collective-permute-done.refs_4_
  7.8 0.0 collective-permute-done.1.refs_5_
  7.8 2.1 %collective-permute-done.2.refs_6_ = bf16[128,256]{1,0:T(8,128)(2,1)S(1)} collective-permute-done((bf16[128,256]{1,0:T(8,128)(2,1)S(1)}, bf16[128,256]{1,0:T(8,128)(2,1)S(1)}, u32[]{:S(2)}, u32[]{:S(2)}) %collective-permute-start.2) | collective-permute-done | bytes 65568 | tf_op jit(solution)/shard_map/fetch_2_0/ppermute | solution.py:66
  10.0 0.0 collective-permute-done.3.refs_7_
  10.0 2.1 %score.1 = (bf16[2,8,256,128]{3,2,1,0:T(8,128)(2,1)S(1)}, bf16[2,8,256,128]{3,2,1,0:T(8,128)(2,1)S(1)}, bf16[2,384,256]{2,1,0:T(8,128)(2,1)S(1)}, f32[128,256]{1...) custom-call(f32[2,256,128]{2,1,0:T(8,128)S(1)} %get-tuple-element.25, ...), custom_call_target="tpu_custom_call" | custom-call | tf_op jit(solution)/shard_map/score/pallas_call | solution.py:436
  12.0 2.2 %collective-permute-start.4 = (bf16[128,256]{1,0:T(8,128)(2,1)S(1)}, bf16[128,256]{1,0:T(8,128)(2,1)S(1)}, u32[]{:S(2)}, u32[]{:S(2)}) collective-permute-start(bf16[128,256]{1,0:T(8,128)(2,1)S(1)} %get-tuple-element.40), channel_id=1, source_target_pairs={{0,2},{1,3},{2,0},{3,1},{4,6},{5,7},{6,4},{7,5},{8,10},{9,11},{10,... | collective-permute-start | bytes 196616 | tf_op jit(solution)/shard_map/give_1_0/ppermute | solution.py:66
  14.2 0.0 collective-permute-start.5
  14.2 2.0 %collective-permute-start.6 = (bf16[128,256]{1,0:T(8,128)(2,1)S(1)}, bf16[128,256]{1,0:T(8,128)(2,1)S(1)}, u32[]{:S(2)}, u32[]{:S(2)}) collective-permute-start(bf16[128,256]{1,0:T(8,128)(2,1)S(1)} %get-tuple-element.42), channel_id=1, source_target_pairs={{0,4},{1,5},{2,6},{3,7},{4,0},{5,1},{6,2},{7,3},{8,12},{9,13},{10,... | collective-permute-start | bytes 196616 | tf_op jit(solution)/shard_map/give_2_0/ppermute | solution.py:66
  16.2 0.0 collective-permute-start.7
  16.2 1.8 %output.1 = (bf16[256,1024]{1,0:T(8,128)(2,1)}, bf16[256,1024]{1,0:T(8,128)(2,1)}, f32[256,256]{1,0:T(8,128)S(1)}) custom-call(bf16[2,8,256,128]{3,2,1,0:T(8,128)(2,1)S(1)} %get-tuple-element.33.pb, bf16[2,8,256,128]{3,2,1,0:T(8,128)(2,1)S(1)} %get-tuple-element.34.dsb, bf16[2,384,256]{2,1,0:T(8,128)(2,1)S(1)} %get-tuple-element.35.kv_win, ...), custom_call_target="tpu_custom_call" | custom-call | tf_op jit(solution)/shard_map/output/pallas_call | solution.py:456
  18.1 0.0 collective-permute-done.4.refs_2_
  18.1 0.0 collective-permute-done.5.refs_3_
  18.1 1.3 %collective-permute-done.6.refs_4_ = bf16[128,256]{1,0:T(8,128)(2,1)S(1)} collective-permute-done((bf16[128,256]{1,0:T(8,128)(2,1)S(1)}, bf16[128,256]{1,0:T(8,128)(2,1)S(1)}, u32[]{:S(2)}, u32[]{:S(2)}) %collective-permute-start.6) | collective-permute-done | bytes 65568 | tf_op jit(solution)/shard_map/give_2_0/ppermute | solution.py:66
  19.4 0.0 collective-permute-done.7.refs_5_
  19.4 0.8 %total.1 = (bf16[256,128]{1,0:T(8,128)(2,1)}, bf16[256,128]{1,0:T(8,128)(2,1)}) custom-call(f32[256,256]{1,0:T(8,128)S(1)} %get-tuple-element.38.refs_0_, f32[128,256]{1,0:T(8,128)S(1)} %get-tuple-element.39.refs_1_, bf16[128,256]{1,0:T(8,128)(2,1)S(1)} %collective-permute-done.4.refs_2_, bf16[128,256]{1,0:T(8,128)(2,1)S(1)} %collective-permute-done.5.refs_3_, ...), custom_call_target="tpu_custom_call" | custom-call | tf_op jit(solution)/shard_map/total/pallas_call | solution.py:471
Async XLA Ops:
  1.7 6.1 %collective-permute-start = (bf16[128,256]{1,0:T(8,128)(2,1)S(1)}, bf16[128,256]{1,0:T(8,128)(2,1)S(1)}, u32[]{:S(2)}, u32[]{:S(2)}) collective-permute-start(bf16[128,256]{1,0:T(8,128)(2,1)S(1)} %get-tuple-element.29), channel_id=1, source_target_pairs={{0,2},{1,3},{2,0},{3,1},{4,6},{5,7},{6,4},{7,5},{8,10},{9,11},{10,... | collective-permute-start | bytes 196616 | tf_op jit(solution)/shard_map/fetch_1_0/ppermute | solution.py:66
  4.8 3.1 %collective-permute-start.1 = (bf16[128,256]{1,0:T(8,128)(2,1)S(1)}, bf16[128,256]{1,0:T(8,128)(2,1)S(1)}, u32[]{:S(2)}, u32[]{:S(2)}) collective-permute-start(bf16[128,256]{1,0:T(8,128)(2,1)S(1)} %get-tuple-element.30), channel_id=1, source_target_pairs={{0,1},{1,0},{2,4},{3,5},{4,2},{5,3},{6,8},{7,9},{8,6},{9,7},{10,12... | collective-permute-start | bytes 196616 | tf_op jit(solution)/shard_map/fetch_1_1/ppermute | solution.py:66
  4.8 5.2 %collective-permute-start.2 = (bf16[128,256]{1,0:T(8,128)(2,1)S(1)}, bf16[128,256]{1,0:T(8,128)(2,1)S(1)}, u32[]{:S(2)}, u32[]{:S(2)}) collective-permute-start(bf16[128,256]{1,0:T(8,128)(2,1)S(1)} %get-tuple-element.31), channel_id=1, source_target_pairs={{0,4},{1,5},{2,6},{3,7},{4,0},{5,1},{6,2},{7,3},{8,12},{9,13},{10,... | collective-permute-start | bytes 196616 | tf_op jit(solution)/shard_map/fetch_2_0/ppermute | solution.py:66
  6.3 3.6 %collective-permute-start.3 = (bf16[128,256]{1,0:T(8,128)(2,1)S(1)}, bf16[128,256]{1,0:T(8,128)(2,1)S(1)}, u32[]{:S(2)}, u32[]{:S(2)}) collective-permute-start(bf16[128,256]{1,0:T(8,128)(2,1)S(1)} %get-tuple-element.32), channel_id=1, source_target_pairs={{0,1},{1,0},{2,3},{3,2},{4,8},{5,9},{6,10},{7,11},{8,4},{9,5},{10,... | collective-permute-start | bytes 196616 | tf_op jit(solution)/shard_map/fetch_2_1/ppermute | solution.py:66
  12.0 6.0 %collective-permute-start.4 = (bf16[128,256]{1,0:T(8,128)(2,1)S(1)}, bf16[128,256]{1,0:T(8,128)(2,1)S(1)}, u32[]{:S(2)}, u32[]{:S(2)}) collective-permute-start(bf16[128,256]{1,0:T(8,128)(2,1)S(1)} %get-tuple-element.40), channel_id=1, source_target_pairs={{0,2},{1,3},{2,0},{3,1},{4,6},{5,7},{6,4},{7,5},{8,10},{9,11},{10,... | collective-permute-start | bytes 196616 | tf_op jit(solution)/shard_map/give_1_0/ppermute | solution.py:66
  14.2 3.9 %collective-permute-start.5 = (bf16[128,256]{1,0:T(8,128)(2,1)S(1)}, bf16[128,256]{1,0:T(8,128)(2,1)S(1)}, u32[]{:S(2)}, u32[]{:S(2)}) collective-permute-start(bf16[128,256]{1,0:T(8,128)(2,1)S(1)} %get-tuple-element.41), channel_id=1, source_target_pairs={{0,1},{1,0},{2,4},{3,5},{4,2},{5,3},{6,8},{7,9},{8,6},{9,7},{10,12... | collective-permute-start | bytes 196616 | tf_op jit(solution)/shard_map/give_1_1/ppermute | solution.py:66
  14.2 5.2 %collective-permute-start.6 = (bf16[128,256]{1,0:T(8,128)(2,1)S(1)}, bf16[128,256]{1,0:T(8,128)(2,1)S(1)}, u32[]{:S(2)}, u32[]{:S(2)}) collective-permute-start(bf16[128,256]{1,0:T(8,128)(2,1)S(1)} %get-tuple-element.42), channel_id=1, source_target_pairs={{0,4},{1,5},{2,6},{3,7},{4,0},{5,1},{6,2},{7,3},{8,12},{9,13},{10,... | collective-permute-start | bytes 196616 | tf_op jit(solution)/shard_map/give_2_0/ppermute | solution.py:66
  16.2 3.2 %collective-permute-start.7 = (bf16[128,256]{1,0:T(8,128)(2,1)S(1)}, bf16[128,256]{1,0:T(8,128)(2,1)S(1)}, u32[]{:S(2)}, u32[]{:S(2)}) collective-permute-start(bf16[128,256]{1,0:T(8,128)(2,1)S(1)} %get-tuple-element.43), channel_id=1, source_target_pairs={{0,1},{1,0},{2,3},{3,2},{4,8},{5,9},{6,10},{7,11},{8,4},{9,5},{10,... | collective-permute-start | bytes 196616 | tf_op jit(solution)/shard_map/give_2_1/ppermute | solution.py:66

commit v5 on v4

--- a/solution.py
+++ b/solution.py
@@ -105,12 +105,13 @@
         copy.start()
     lengths.wait()
     me = lax.axis_index("ctx")
-    merged = bias.shape[1]
+    merged = bias.shape[2]
     row = lax.broadcasted_iota(jnp.int32, (merged, length), 0)
-    col = lax.broadcasted_iota(jnp.int32, (1, length), 1)
-    for s in range(2):
+    half = length // 2
+    col = lax.broadcasted_iota(jnp.int32, (1, length), 1) % half
+    for s, u in ((0, 0), (0, 1), (1, 0), (1, 1)):
         stretch = me if s == 0 else 2 * ctx_count - 1 - me
-        q_pos = stretch * length + col
+        q_pos = stretch * length + u * half + col
         start = jnp.int32(0)
         doc_start = jnp.zeros((1, length), jnp.int32)
         for i in range(docs_ref.shape[0]):
@@ -118,15 +119,15 @@
             start = start + docs_ref[i]
         k_pos = row + (stretch - 2 * (row // length)) * length
         k_pos = jnp.where(k_pos > q_pos, k_pos - merged, k_pos)
-        bias[s] = jnp.where(k_pos >= doc_start, 0.0, MASKED)
+        bias[s, u] = jnp.where(k_pos >= doc_start, 0.0, MASKED)
     for copy in copies:
         copy.wait()
 
 
-def stacked(ref, s, first=0, last=None):
-    length = ref.shape[1] // 2
-    value = ref[first:last, s * length : (s + 1) * length, :]
-    return value.reshape(-1, ref.shape[2])
+def stacked(ref, s, u, first=0, last=None):
+    half = ref.shape[1] // 4
+    start = (2 * s + u) * half
+    return ref[first:last, start : start + half, :].reshape(-1, ref.shape[2])
 
 
 def unfolded(ref, s, h, near_low):
@@ -193,32 +194,51 @@
         kv_win[0, rows, :] = lows[slot]
         kv_win[1, rows, :] = highs[slot]
 
-    tri_row = lax.broadcasted_iota(jnp.int32, (length, length), 0)
-    near = tri_row <= lax.broadcasted_iota(jnp.int32, (length, length), 1)
+    half = length // 2
+    group = next(g for g in (4, 2) if heads % g == 0)
+    lanes = 2 * half
+    tri_row = lax.broadcasted_iota(jnp.int32, (half, lanes), 0)
+    near = tri_row <= lax.broadcasted_iota(jnp.int32, (half, lanes), 1) % half
     far_low = jnp.where(near, 0.0, 1.0).astype(jnp.bfloat16)
-
-    def fold(value):
-        return jnp.where(near, value[:length, :], value[merged:, :])
-
-    def products(s, h):
-        contract_last = (((1,), (1,)), ((), ()))
+    contract_last = (((1,), (1,)), ((), ()))
+
+    def products(s, u, h):
+        own_rows = slice(0, length if u else half)
+        last_rows = slice(merged + half if u else merged, None)
+
+        def window(cols):
+            parts = [kv_win[s, own_rows, cols], kv_win[s, length:merged, cols]]
+            return jnp.concatenate(parts + [kv_win[s, last_rows, cols]], axis=0)
+
         raw = lax.dot_general(
-            kv_win[s, :, :width],
-            stacked(q_all, s, h, h + group),
+            window(slice(0, width)),
+            stacked(q_all, s, u, h, h + group),
             contract_last,
             preferred_element_type=jnp.float32,
         )
         d_p = lax.dot_general(
-            kv_win[s, :, width:],
-            stacked(g_all, s, h, h + group),
+            window(slice(width, None)),
+            stacked(g_all, s, u, h, h + group),
             contract_last,
             preferred_element_type=jnp.float32,
         )
         return raw, d_p
 
-    def soften(s, h, raw, d_p):
-        raw = jnp.concatenate([fold(raw), raw[length:merged, :]], axis=0) + bias[s]
-        d_p = jnp.concatenate([fold(d_p), d_p[length:merged, :]], axis=0)
+    def fold(u, value):
+        if u:
+            top = value[:half, :]
+            low = jnp.where(near, value[half:length, :], value[merged:, :])
+            middle = value[length:merged, :]
+        else:
+            last = value[merged - half :, :]
+            top = jnp.where(near, value[:half, :], last[:half, :])
+            low = last[half:, :]
+            middle = value[half : merged - half, :]
+        return jnp.concatenate([top, low, middle], axis=0)
+
+    def soften(s, u, block, raw, d_p):
+        raw = fold(u, raw) + bias[s, u]
+        d_p = fold(u, d_p)
         top = jnp.max(raw, axis=0, keepdims=True)
         weight = jnp.exp2((raw - top) * log_scale)
         total = jnp.sum(weight, axis=0, keepdims=True)
@@ -228,38 +248,47 @@
         others = []
         for ref, value in ((pb, weight), (dsb, weight * (d_p - delta))):
             value = value.astype(jnp.bfloat16)
-            ref[s, h] = value
-            others.append(jnp.concatenate([value[length:, :], value[:length, :] * far_low], axis=0))
+            ref[s, block] = value
+            if u:
+                last = [value[half:length, :] * far_low]
+            else:
+                last = [value[:half, :] * far_low, value[half:length, :]]
+            others.append(jnp.concatenate([value[length:, :]] + last, axis=0))
         return others
 
-    def gradients(s, first, last, done):
-        part = slice(length, None)
+    def gradients(s, u, first, last, start, done):
         weights, d_scores = [jnp.concatenate(values, axis=1) for values in zip(*done)]
-        d_k = jnp.dot(
-            d_scores, stacked(q_all, s, first, last), preferred_element_type=jnp.float32
-        )
-        d_v = jnp.dot(weights, stacked(g_all, s, first, last), preferred_element_type=jnp.float32)
-        if first > 0:
-            d_k = d_k + acc[s, part, :width]
-            d_v = d_v + acc[s, part, width:]
-        if last == heads:
-            d_k = d_k * scaling
-        acc[s, part, :width] = d_k
-        acc[s, part, width:] = d_v
-
-    group = 2 if heads % 2 == 0 else 1
-    items = [(s, h) for s in range(2) for h in range(0, heads, group)]
-    stops = [{heads // 2, heads}, {heads - group, heads}]
+        parts = [(slice(length, merged), slice(0, merged - length))] if merged > length else []
+        parts.append((slice(merged + u * half, merged + length), slice(merged - length, None)))
+        for cols, left, right in (
+            (slice(0, width), d_scores, q_all),
+            (slice(width, None), weights, g_all),
+        ):
+            value = jnp.dot(
+                left, stacked(right, s, u, first, last), preferred_element_type=jnp.float32
+            )
+            if right is q_all:
+                value = value * scaling
+            for rows, part in parts:
+                if start:
+                    acc[s, rows, cols] = value[part, :]
+                else:
+                    acc[s, rows, cols] = acc[s, rows, cols] + value[part, :]
+
+    items = [(s, u, h) for s in range(2) for u in range(2) for h in range(0, heads, group)]
     done = []
     ready = products(*items[0])
-    for i, (s, h) in enumerate(items):
+    for i, (s, u, h) in enumerate(items):
         following = products(*items[i + 1]) if i + 1 < len(items) else None
-        for j in range(group):
-            part = slice(j * length, (j + 1) * length)
-            done.append(soften(s, h + j, ready[0][:, part], ready[1][:, part]))
+        for j in range(0, group, 2):
+            part = slice(j // 2 * lanes, (j // 2 + 1) * lanes)
+            block = (u * heads + h + j) // 2
+            done.append(soften(s, u, block, ready[0][:, part], ready[1][:, part]))
         ready = following
-        if h + group in stops[s]:
-            gradients(s, h + group - len(done), h + group, done)
+        last = h + group
+        if last == heads or (s, u) == (1, 1) and last == heads - group:
+            first = last - 2 * len(done)
+            gradients(s, u, first, last, u == 0, done)
             done = []
 
     def slot_rows(slot):
@@ -300,46 +329,51 @@
     width = HEAD_DIM
     heads = att.shape[1] // width
     scaling = width ** (-0.5)
-    group = 2 if heads % 2 == 0 else 1
-    tri_row = lax.broadcasted_iota(jnp.int32, (length, length), 0)
-    tri_col = lax.broadcasted_iota(jnp.int32, (length, length), 1)
-    near_low = jnp.where(tri_row <= tri_col, 1.0, 0.0).astype(jnp.bfloat16)
+    group = next(g for g in (4, 2) if heads % g == 0)
+    half = length // 2
+    tri_row = lax.broadcasted_iota(jnp.int32, (length, 2 * half), 0)
+    tri_col = lax.broadcasted_iota(jnp.int32, (length, 2 * half), 1) % half
     copies = []
     for s in range(2):
-        rows = slice(s * length, (s + 1) * length)
         k_turn = kv_win[s, :, :width].T
         v_turn = kv_win[s, :, width:].T
         own_weights, own_scores = [], []
-        for h in range(0, heads, group):
-            weights = [unfolded(pb, s, h + i, near_low) for i in range(group)]
-            d_scores = [unfolded(dsb, s, h + i, near_low) for i in range(group)]
-            own_weights += [value[:length, :] for value in weights]
-            own_scores += [value[:length, :] for value in d_scores]
-            out_t = jnp.dot(
-                v_turn, jnp.concatenate(weights, axis=1), preferred_element_type=jnp.float32
-            )
-            dq_t = jnp.dot(
-                k_turn, jnp.concatenate(d_scores, axis=1), preferred_element_type=jnp.float32
-            )
-            out_t = out_t.astype(jnp.bfloat16)
-            dq_t = (dq_t * scaling).astype(jnp.bfloat16)
-            for i in range(group):
-                part = slice(i * length, (i + 1) * length)
-                cols = slice((h + i) * width, (h + i + 1) * width)
-                att[rows, cols] = out_t[:, part].T
-                dq[rows, cols] = dq_t[:, part].T
+        for u in range(2):
+            near_low = jnp.where(tri_row <= tri_col + u * half, 1.0, 0.0).astype(jnp.bfloat16)
+            for h in range(0, heads, group):
+                blocks = [(u * heads + h + j) // 2 for j in range(0, group, 2)]
+                weights = [unfolded(pb, s, block, near_low) for block in blocks]
+                d_scores = [unfolded(dsb, s, block, near_low) for block in blocks]
+                own_weights += [value[:length, :] for value in weights]
+                own_scores += [value[:length, :] for value in d_scores]
+                out_t = jnp.dot(
+                    v_turn, jnp.concatenate(weights, axis=1), preferred_element_type=jnp.float32
+                )
+                dq_t = jnp.dot(
+                    k_turn, jnp.concatenate(d_scores, axis=1), preferred_element_type=jnp.float32
+                )
+                out_t = out_t.astype(jnp.bfloat16)
+                dq_t = (dq_t * scaling).astype(jnp.bfloat16)
+                rows = slice((2 * s + u) * half, (2 * s + u + 1) * half)
+                for j in range(0, group, 2):
+                    part = slice(j * half, (j + 2) * half)
+                    for ref, value in ((att, out_t[:, part].T), (dq, dq_t[:, part].T)):
+                        for i in range(2):
+                            cols = slice((h + j + i) * width, (h + j + i + 1) * width)
+                            ref[rows, cols] = value[i * half : (i + 1) * half, :]
+        rows = slice(s * length, (s + 1) * length)
         for a, (src, dst) in enumerate(((att, att_hbm), (dq, dq_hbm))):
             copy = pltpu.make_async_copy(src.at[rows, :], dst.at[rows, :], sems.at[s, a])
             copy.start()
             copies.append(copy)
         d_k = jnp.dot(
             jnp.concatenate(own_scores, axis=1),
-            stacked(q_all, s),
+            jnp.concatenate([stacked(q_all, s, u) for u in range(2)], axis=0),
             preferred_element_type=jnp.float32,
         )
         d_v = jnp.dot(
             jnp.concatenate(own_weights, axis=1),
-            stacked(g_all, s),
+            jnp.concatenate([stacked(g_all, s, u) for u in range(2)], axis=0),
             preferred_element_type=jnp.float32,
         )
         own_ref[rows, :width] = d_k * scaling
@@ -421,7 +455,7 @@
     stack = pltpu.VMEM((heads, tok_dev, width), jnp.bfloat16)
     q_all, g_all, bias = pl.pallas_call(
         lambda *refs: stage_kernel(ctx_count, *refs),
-        out_shape=[stack, stack, pltpu.VMEM((2, reach * length, length), jnp.float32)],
+        out_shape=[stack, stack, pltpu.VMEM((2, 2, reach * length, length), jnp.float32)],
         in_specs=in_place(3),
         out_specs=in_vmem(3),
         scratch_shapes=[

time: 20.4 us -> 20.3 us (level)
  no operation moved by 1% of the time
where the time goes in v5:
time: 20.3 us; the launch traced here: 20.1 us
  starting transfers between devices  8.84 us (44%)
  Pallas kernels  7.06 us (35%)
  waiting for transfers between devices  3.47 us (17%)
  between operations  0.7 us (3%)
    ppermute x8, starting transfers between devices, swap(): return lax.ppermute(value, ('ctx', 'head'), pairs)  8.84 us
    ppermute x8, waiting for transfers between devices, swap(): return lax.ppermute(value, ('ctx', 'head'), pairs)  3.47 us
    pallas_call x1, Pallas kernels, shards(): pl.pallas_call(lambda *refs: score_kernel(sets, ctx_count, reach, *refs),...  1.95 us
    pallas_call x1, Pallas kernels, shards(): pl.pallas_call(output_kernel, out_shape=[jax.ShapeDtypeStruct(query_rows....  1.82 us
    pallas_call x1, Pallas kernels, shards(): pl.pallas_call(lambda *refs: stage_kernel(ctx_count, *refs), out_shape=[s...  1.47 us
    pallas_call x1, Pallas kernels, shards(): pl.pallas_call(lambda *refs: pack_kernel(sets, *refs), out_shape=[pltpu.V...  1.06 us
    pallas_call x1, Pallas kernels, shards(): pl.pallas_call(lambda *refs: sum_kernel(sets, ctx_count, *refs), out_shap...  0.77 us
  transfers between devices with their start and end apart: 8, of which 2 were waited for; matrix products, arithmetic and copies ran while one was open for 0% of the time, Pallas kernels for 16%

profile of v5, /device:TPU:0, one launch (start us, length us, event | category | flops | bytes accessed | tf_op | source)
XLA Modules:
  0.0 20.1 jit_solution(5934603749652695223)
XLA Ops:
  0.6 1.1 %pack.1 = (bf16[256,256]{1,0:T(8,128)(2,1)S(1)}, bf16[128,256]{1,0:T(8,128)(2,1)S(1)}, bf16[128,256]{1,0:T(8,128)(2,1)S(1)}, bf16[128,256]{1,0:T(8,128)(2,1)S(1)}, bf16[128,256]{1,0:T(8,128)(2,1)S(1)}) custom-call(bf16[256,128]{1,0:T(8,128)(2,1)} %refs_0_.3, bf16[256,128]{1,0:T(8,128)(2,1)} %refs_1_.3), custom_call_target="tpu_custom_call" | custom-call | tf_op jit(solution)/shard_map/pack/pallas_call | solution.py:443
  1.7 3.1 %collective-permute-start = (bf16[128,256]{1,0:T(8,128)(2,1)S(1)}, bf16[128,256]{1,0:T(8,128)(2,1)S(1)}, u32[]{:S(2)}, u32[]{:S(2)}) collective-permute-start(bf16[128,256]{1,0:T(8,128)(2,1)S(1)} %get-tuple-element.29), channel_id=1, source_target_pairs={{0,2},{1,3},{2,0},{3,1},{4,6},{5,7},{6,4},{7,5},{8,10},{9,11},{10,... | collective-permute-start | bytes 196616 | tf_op jit(solution)/shard_map/fetch_1_0/ppermute | solution.py:66
  4.8 0.0 collective-permute-start.1
  4.8 1.6 %collective-permute-start.2 = (bf16[128,256]{1,0:T(8,128)(2,1)S(1)}, bf16[128,256]{1,0:T(8,128)(2,1)S(1)}, u32[]{:S(2)}, u32[]{:S(2)}) collective-permute-start(bf16[128,256]{1,0:T(8,128)(2,1)S(1)} %get-tuple-element.31), channel_id=1, source_target_pairs={{0,4},{1,5},{2,6},{3,7},{4,0},{5,1},{6,2},{7,3},{8,12},{9,13},{10,... | collective-permute-start | bytes 196616 | tf_op jit(solution)/shard_map/fetch_2_0/ppermute | solution.py:66
  6.3 0.0 collective-permute-start.3
  6.3 1.5 %stage.1 = (bf16[8,256,128]{2,1,0:T(8,128)(2,1)S(1)}, bf16[8,256,128]{2,1,0:T(8,128)(2,1)S(1)}, f32[2,2,256,128]{3,2,1,0:T(8,128)S(1)}) custom-call(s32[16]{0:T(128)} %refs_0_.2, bf16[256,1024]{1,0:T(8,128)(2,1)} %refs_1_.2, bf16[256,1024]{1,0:T(8,128)(2,1)} %refs_2_.1), custom_call_target="tpu_custom_call" | custom-call | tf_op jit(solution)/shard_map/stage/pallas_call | solution.py:456
  7.8 0.0 collective-permute-done.refs_4_
  7.8 0.0 collective-permute-done.1.refs_5_
  7.8 2.1 %collective-permute-done.2.refs_6_ = bf16[128,256]{1,0:T(8,128)(2,1)S(1)} collective-permute-done((bf16[128,256]{1,0:T(8,128)(2,1)S(1)}, bf16[128,256]{1,0:T(8,128)(2,1)S(1)}, u32[]{:S(2)}, u32[]{:S(2)}) %collective-permute-start.2) | collective-permute-done | bytes 65568 | tf_op jit(solution)/shard_map/fetch_2_0/ppermute | solution.py:66
  10.0 0.0 collective-permute-done.3.refs_7_
  10.0 1.9 %score.1 = (bf16[2,8,256,128]{3,2,1,0:T(8,128)(2,1)S(1)}, bf16[2,8,256,128]{3,2,1,0:T(8,128)(2,1)S(1)}, bf16[2,384,256]{2,1,0:T(8,128)(2,1)S(1)}, f32[128,256]{1...) custom-call(f32[2,2,256,128]{3,2,1,0:T(8,128)S(1)} %get-tuple-elemen, ...), custom_call_target="tpu_custom_call" | custom-call | tf_op jit(solution)/shard_map/score/pallas_call | solution.py:470
  11.9 2.2 %collective-permute-start.4 = (bf16[128,256]{1,0:T(8,128)(2,1)S(1)}, bf16[128,256]{1,0:T(8,128)(2,1)S(1)}, u32[]{:S(2)}, u32[]{:S(2)}) collective-permute-start(bf16[128,256]{1,0:T(8,128)(2,1)S(1)} %get-tuple-element.40), channel_id=1, source_target_pairs={{0,2},{1,3},{2,0},{3,1},{4,6},{5,7},{6,4},{7,5},{8,10},{9,11},{10,... | collective-permute-start | bytes 196616 | tf_op jit(solution)/shard_map/give_1_0/ppermute | solution.py:66
  14.1 0.0 collective-permute-start.5
  14.1 2.0 %collective-permute-start.6 = (bf16[128,256]{1,0:T(8,128)(2,1)S(1)}, bf16[128,256]{1,0:T(8,128)(2,1)S(1)}, u32[]{:S(2)}, u32[]{:S(2)}) collective-permute-start(bf16[128,256]{1,0:T(8,128)(2,1)S(1)} %get-tuple-element.42), channel_id=1, source_target_pairs={{0,4},{1,5},{2,6},{3,7},{4,0},{5,1},{6,2},{7,3},{8,12},{9,13},{10,... | collective-permute-start | bytes 196616 | tf_op jit(solution)/shard_map/give_2_0/ppermute | solution.py:66
  16.1 0.0 collective-permute-start.7
  16.1 1.8 %output.1 = (bf16[256,1024]{1,0:T(8,128)(2,1)}, bf16[256,1024]{1,0:T(8,128)(2,1)}, f32[256,256]{1,0:T(8,128)S(1)}) custom-call(bf16[2,8,256,128]{3,2,1,0:T(8,128)(2,1)S(1)} %get-tuple-element.33.pb, bf16[2,8,256,128]{3,2,1,0:T(8,128)(2,1)S(1)} %get-tuple-element.34.dsb, bf16[2,384,256]{2,1,0:T(8,128)(2,1)S(1)} %get-tuple-element.35.kv_win, ...), custom_call_target="tpu_custom_call" | custom-call | tf_op jit(solution)/shard_map/output/pallas_call | solution.py:490
  17.9 0.0 collective-permute-done.4.refs_2_
  18.0 0.0 collective-permute-done.5.refs_3_
  18.0 1.3 %collective-permute-done.6.refs_4_ = bf16[128,256]{1,0:T(8,128)(2,1)S(1)} collective-permute-done((bf16[128,256]{1,0:T(8,128)(2,1)S(1)}, bf16[128,256]{1,0:T(8,128)(2,1)S(1)}, u32[]{:S(2)}, u32[]{:S(2)}) %collective-permute-start.6) | collective-permute-done | bytes 65568 | tf_op jit(solution)/shard_map/give_2_0/ppermute | solution.py:66
  19.3 0.0 collective-permute-done.7.refs_5_
  19.3 0.8 %total.1 = (bf16[256,128]{1,0:T(8,128)(2,1)}, bf16[256,128]{1,0:T(8,128)(2,1)}) custom-call(f32[256,256]{1,0:T(8,128)S(1)} %get-tuple-element.38.refs_0_, f32[128,256]{1,0:T(8,128)S(1)} %get-tuple-element.39.refs_1_, bf16[128,256]{1,0:T(8,128)(2,1)S(1)} %collective-permute-done.4.refs_2_, bf16[128,256]{1,0:T(8,128)(2,1)S(1)} %collective-permute-done.5.refs_3_, ...), custom_call_target="tpu_custom_call" | custom-call | tf_op jit(solution)/shard_map/total/pallas_call | solution.py:505
Async XLA Ops:
  1.7 6.1 %collective-permute-start = (bf16[128,256]{1,0:T(8,128)(2,1)S(1)}, bf16[128,256]{1,0:T(8,128)(2,1)S(1)}, u32[]{:S(2)}, u32[]{:S(2)}) collective-permute-start(bf16[128,256]{1,0:T(8,128)(2,1)S(1)} %get-tuple-element.29), channel_id=1, source_target_pairs={{0,2},{1,3},{2,0},{3,1},{4,6},{5,7},{6,4},{7,5},{8,10},{9,11},{10,... | collective-permute-start | bytes 196616 | tf_op jit(solution)/shard_map/fetch_1_0/ppermute | solution.py:66
  4.8 3.1 %collective-permute-start.1 = (bf16[128,256]{1,0:T(8,128)(2,1)S(1)}, bf16[128,256]{1,0:T(8,128)(2,1)S(1)}, u32[]{:S(2)}, u32[]{:S(2)}) collective-permute-start(bf16[128,256]{1,0:T(8,128)(2,1)S(1)} %get-tuple-element.30), channel_id=1, source_target_pairs={{0,1},{1,0},{2,4},{3,5},{4,2},{5,3},{6,8},{7,9},{8,6},{9,7},{10,12... | collective-permute-start | bytes 196616 | tf_op jit(solution)/shard_map/fetch_1_1/ppermute | solution.py:66
  4.8 5.2 %collective-permute-start.2 = (bf16[128,256]{1,0:T(8,128)(2,1)S(1)}, bf16[128,256]{1,0:T(8,128)(2,1)S(1)}, u32[]{:S(2)}, u32[]{:S(2)}) collective-permute-start(bf16[128,256]{1,0:T(8,128)(2,1)S(1)} %get-tuple-element.31), channel_id=1, source_target_pairs={{0,4},{1,5},{2,6},{3,7},{4,0},{5,1},{6,2},{7,3},{8,12},{9,13},{10,... | collective-permute-start | bytes 196616 | tf_op jit(solution)/shard_map/fetch_2_0/ppermute | solution.py:66
  6.3 3.6 %collective-permute-start.3 = (bf16[128,256]{1,0:T(8,128)(2,1)S(1)}, bf16[128,256]{1,0:T(8,128)(2,1)S(1)}, u32[]{:S(2)}, u32[]{:S(2)}) collective-permute-start(bf16[128,256]{1,0:T(8,128)(2,1)S(1)} %get-tuple-element.32), channel_id=1, source_target_pairs={{0,1},{1,0},{2,3},{3,2},{4,8},{5,9},{6,10},{7,11},{8,4},{9,5},{10,... | collective-permute-start | bytes 196616 | tf_op jit(solution)/shard_map/fetch_2_1/ppermute | solution.py:66
  11.9 6.0 %collective-permute-start.4 = (bf16[128,256]{1,0:T(8,128)(2,1)S(1)}, bf16[128,256]{1,0:T(8,128)(2,1)S(1)}, u32[]{:S(2)}, u32[]{:S(2)}) collective-permute-start(bf16[128,256]{1,0:T(8,128)(2,1)S(1)} %get-tuple-element.40), channel_id=1, source_target_pairs={{0,2},{1,3},{2,0},{3,1},{4,6},{5,7},{6,4},{7,5},{8,10},{9,11},{10,... | collective-permute-start | bytes 196616 | tf_op jit(solution)/shard_map/give_1_0/ppermute | solution.py:66
  14.1 3.9 %collective-permute-start.5 = (bf16[128,256]{1,0:T(8,128)(2,1)S(1)}, bf16[128,256]{1,0:T(8,128)(2,1)S(1)}, u32[]{:S(2)}, u32[]{:S(2)}) collective-permute-start(bf16[128,256]{1,0:T(8,128)(2,1)S(1)} %get-tuple-element.41), channel_id=1, source_target_pairs={{0,1},{1,0},{2,4},{3,5},{4,2},{5,3},{6,8},{7,9},{8,6},{9,7},{10,12... | collective-permute-start | bytes 196616 | tf_op jit(solution)/shard_map/give_1_1/ppermute | solution.py:66
  14.1 5.2 %collective-permute-start.6 = (bf16[128,256]{1,0:T(8,128)(2,1)S(1)}, bf16[128,256]{1,0:T(8,128)(2,1)S(1)}, u32[]{:S(2)}, u32[]{:S(2)}) collective-permute-start(bf16[128,256]{1,0:T(8,128)(2,1)S(1)} %get-tuple-element.42), channel_id=1, source_target_pairs={{0,4},{1,5},{2,6},{3,7},{4,0},{5,1},{6,2},{7,3},{8,12},{9,13},{10,... | collective-permute-start | bytes 196616 | tf_op jit(solution)/shard_map/give_2_0/ppermute | solution.py:66
  16.1 3.2 %collective-permute-start.7 = (bf16[128,256]{1,0:T(8,128)(2,1)S(1)}, bf16[128,256]{1,0:T(8,128)(2,1)S(1)}, u32[]{:S(2)}, u32[]{:S(2)}) collective-permute-start(bf16[128,256]{1,0:T(8,128)(2,1)S(1)} %get-tuple-element.43), channel_id=1, source_target_pairs={{0,1},{1,0},{2,3},{3,2},{4,8},{5,9},{6,10},{7,11},{8,4},{9,5},{10,... | collective-permute-start | bytes 196616 | tf_op jit(solution)/shard_map/give_2_1/ppermute | solution.py:66

commit v6 on v5

--- a/solution.py
+++ b/solution.py
@@ -6,6 +6,7 @@
 from jax.experimental import pallas as pl
 from jax.experimental.pallas import tpu as pltpu
 from jax.sharding import PartitionSpec as P
+
 
 HEAD_DIM = 128
 DOC_STRETCHES = 8
@@ -50,7 +51,7 @@
     return entry["offset"], entry["colour"]
 
 
-def swap(value, exchange, ctx_count, head_count, phase):
+def swap(value, exchange, ctx_count, head_count):
     partner = {}
     pairs = [(b, b + exchange["offset"]) for b in exchange["firsts"]] + exchange["folds"]
     for a, b in pairs:
@@ -62,8 +63,7 @@
                 pairs.append((b * head_count + h, partner[b] * head_count + h))
             else:
                 pairs.append((b * head_count + h, b * head_count + (h + 1) % head_count))
-    with jax.named_scope(f"{phase}_{exchange['offset']}_{exchange['colour']}"):
-        return lax.ppermute(value, ("ctx", "head"), pairs)
+    return lax.ppermute(value, ("ctx", "head"), pairs)
 
 
 def fold_offsets(slot):
@@ -425,7 +425,7 @@
     return [pltpu.with_memory_space_constraint(v, pltpu.HBM) for v in values]
 
 
-def shards(query_rows, key_rows, value_rows, out_grad, doc_lengths):
+def attention(query_rows, key_rows, value_rows, out_grad, doc_lengths):
     ctx_count = lax.axis_size("ctx")
     head_count = lax.axis_size("head")
     tok_dev = query_rows.shape[0]
@@ -450,7 +450,7 @@
         name="pack",
     )(*off_chip([key_rows, value_rows]))
     packed = [mine] * fulls + halves
-    received = [swap(p, s, ctx_count, head_count, "fetch") for p, s in zip(packed, sets)]
+    received = [swap(p, s, ctx_count, head_count) for p, s in zip(packed, sets)]
 
     stack = pltpu.VMEM((heads, tok_dev, width), jnp.bfloat16)
     q_all, g_all, bias = pl.pallas_call(
@@ -485,7 +485,7 @@
         compiler_params=pltpu.CompilerParams(vmem_limit_bytes=VMEM_LIMIT),
         name="score",
     )(*on_chip([bias, q_all, g_all, mine, *received]))
-    returned = [swap(p, s, ctx_count, head_count, "give") for p, s in zip(partials, sets)]
+    returned = [swap(p, s, ctx_count, head_count) for p, s in zip(partials, sets)]
 
     attended, query_grad, own = pl.pallas_call(
         output_kernel,
@@ -522,7 +522,7 @@
         P("groups"),
     )
     return jax.shard_map(
-        shards,
+        attention,
         mesh=mesh,
         in_specs=placed,
         out_specs=(P(("groups", "ctx"), "head"),) * 4,

time: 20.3 us -> 20.3 us (level)
  no operation moved by 1% of the time
where the time goes in v6:
time: 20.3 us; the launch traced here: 20.1 us
  starting transfers between devices  8.84 us (44%)
  Pallas kernels  7.06 us (35%)
  waiting for transfers between devices  3.47 us (17%)
  between operations  0.7 us (3%)
    ppermute x8, starting transfers between devices, swap(): return lax.ppermute(value, ('ctx', 'head'), pairs)  8.84 us
    ppermute x8, waiting for transfers between devices, swap(): return lax.ppermute(value, ('ctx', 'head'), pairs)  3.47 us
    pallas_call x1, Pallas kernels, attention(): pl.pallas_call(lambda *refs: score_kernel(sets, ctx_count, reach, *refs),...  1.95 us
    pallas_call x1, Pallas kernels, attention(): pl.pallas_call(output_kernel, out_shape=[jax.ShapeDtypeStruct(query_rows....  1.82 us
    pallas_call x1, Pallas kernels, attention(): pl.pallas_call(lambda *refs: stage_kernel(ctx_count, *refs), out_shape=[s...  1.47 us
    pallas_call x1, Pallas kernels, attention(): pl.pallas_call(lambda *refs: pack_kernel(sets, *refs), out_shape=[pltpu.V...  1.06 us
    pallas_call x1, Pallas kernels, attention(): pl.pallas_call(lambda *refs: sum_kernel(sets, ctx_count, *refs), out_shap...  0.77 us
  transfers between devices with their start and end apart: 8, of which 2 were waited for; matrix products, arithmetic and copies ran while one was open for 0% of the time, Pallas kernels for 16%

profile of v6, /device:TPU:0, one launch (start us, length us, event | category | flops | bytes accessed | tf_op | source)
XLA Modules:
  0.0 20.1 jit_solution(5934603749652695223)
XLA Ops:
  0.6 1.1 %pack.1 = (bf16[256,256]{1,0:T(8,128)(2,1)S(1)}, bf16[128,256]{1,0:T(8,128)(2,1)S(1)}, bf16[128,256]{1,0:T(8,128)(2,1)S(1)}, bf16[128,256]{1,0:T(8,128)(2,1)S(1)}, bf16[128,256]{1,0:T(8,128)(2,1)S(1)}) custom-call(bf16[256,128]{1,0:T(8,128)(2,1)} %refs_0_.3, bf16[256,128]{1,0:T(8,128)(2,1)} %refs_1_.3), custom_call_target="tpu_custom_call" | custom-call | tf_op jit(solution)/shard_map/pack/pallas_call | solution.py:443
  1.7 3.1 %collective-permute-start = (bf16[128,256]{1,0:T(8,128)(2,1)S(1)}, bf16[128,256]{1,0:T(8,128)(2,1)S(1)}, u32[]{:S(2)}, u32[]{:S(2)}) collective-permute-start(bf16[128,256]{1,0:T(8,128)(2,1)S(1)} %get-tuple-element.29), channel_id=1, source_target_pairs={{0,2},{1,3},{2,0},{3,1},{4,6},{5,7},{6,4},{7,5},{8,10},{9,11},{10,... | collective-permute-start | bytes 196616 | tf_op jit(solution)/shard_map/ppermute | solution.py:66
  4.8 0.0 collective-permute-start.1
  4.8 1.6 %collective-permute-start.2 = (bf16[128,256]{1,0:T(8,128)(2,1)S(1)}, bf16[128,256]{1,0:T(8,128)(2,1)S(1)}, u32[]{:S(2)}, u32[]{:S(2)}) collective-permute-start(bf16[128,256]{1,0:T(8,128)(2,1)S(1)} %get-tuple-element.31), channel_id=1, source_target_pairs={{0,4},{1,5},{2,6},{3,7},{4,0},{5,1},{6,2},{7,3},{8,12},{9,13},{10,... | collective-permute-start | bytes 196616 | tf_op jit(solution)/shard_map/ppermute | solution.py:66
  6.3 0.0 collective-permute-start.3
  6.3 1.5 %stage.1 = (bf16[8,256,128]{2,1,0:T(8,128)(2,1)S(1)}, bf16[8,256,128]{2,1,0:T(8,128)(2,1)S(1)}, f32[2,2,256,128]{3,2,1,0:T(8,128)S(1)}) custom-call(s32[16]{0:T(128)} %refs_0_.2, bf16[256,1024]{1,0:T(8,128)(2,1)} %refs_1_.2, bf16[256,1024]{1,0:T(8,128)(2,1)} %refs_2_.1), custom_call_target="tpu_custom_call" | custom-call | tf_op jit(solution)/shard_map/stage/pallas_call | solution.py:456
  7.8 0.0 collective-permute-done.refs_4_
  7.8 0.0 collective-permute-done.1.refs_5_
  7.8 2.1 %collective-permute-done.2.refs_6_ = bf16[128,256]{1,0:T(8,128)(2,1)S(1)} collective-permute-done((bf16[128,256]{1,0:T(8,128)(2,1)S(1)}, bf16[128,256]{1,0:T(8,128)(2,1)S(1)}, u32[]{:S(2)}, u32[]{:S(2)}) %collective-permute-start.2) | collective-permute-done | bytes 65568 | tf_op jit(solution)/shard_map/ppermute | solution.py:66
  10.0 0.0 collective-permute-done.3.refs_7_
  10.0 1.9 %score.1 = (bf16[2,8,256,128]{3,2,1,0:T(8,128)(2,1)S(1)}, bf16[2,8,256,128]{3,2,1,0:T(8,128)(2,1)S(1)}, bf16[2,384,256]{2,1,0:T(8,128)(2,1)S(1)}, f32[128,256]{1...) custom-call(f32[2,2,256,128]{3,2,1,0:T(8,128)S(1)} %get-tuple-elemen, ...), custom_call_target="tpu_custom_call" | custom-call | tf_op jit(solution)/shard_map/score/pallas_call | solution.py:470
  11.9 2.2 %collective-permute-start.4 = (bf16[128,256]{1,0:T(8,128)(2,1)S(1)}, bf16[128,256]{1,0:T(8,128)(2,1)S(1)}, u32[]{:S(2)}, u32[]{:S(2)}) collective-permute-start(bf16[128,256]{1,0:T(8,128)(2,1)S(1)} %get-tuple-element.40), channel_id=1, source_target_pairs={{0,2},{1,3},{2,0},{3,1},{4,6},{5,7},{6,4},{7,5},{8,10},{9,11},{10,... | collective-permute-start | bytes 196616 | tf_op jit(solution)/shard_map/ppermute | solution.py:66
  14.1 0.0 collective-permute-start.5
  14.1 2.0 %collective-permute-start.6 = (bf16[128,256]{1,0:T(8,128)(2,1)S(1)}, bf16[128,256]{1,0:T(8,128)(2,1)S(1)}, u32[]{:S(2)}, u32[]{:S(2)}) collective-permute-start(bf16[128,256]{1,0:T(8,128)(2,1)S(1)} %get-tuple-element.42), channel_id=1, source_target_pairs={{0,4},{1,5},{2,6},{3,7},{4,0},{5,1},{6,2},{7,3},{8,12},{9,13},{10,... | collective-permute-start | bytes 196616 | tf_op jit(solution)/shard_map/ppermute | solution.py:66
  16.1 0.0 collective-permute-start.7
  16.1 1.8 %output.1 = (bf16[256,1024]{1,0:T(8,128)(2,1)}, bf16[256,1024]{1,0:T(8,128)(2,1)}, f32[256,256]{1,0:T(8,128)S(1)}) custom-call(bf16[2,8,256,128]{3,2,1,0:T(8,128)(2,1)S(1)} %get-tuple-element.33.pb, bf16[2,8,256,128]{3,2,1,0:T(8,128)(2,1)S(1)} %get-tuple-element.34.dsb, bf16[2,384,256]{2,1,0:T(8,128)(2,1)S(1)} %get-tuple-element.35.kv_win, ...), custom_call_target="tpu_custom_call" | custom-call | tf_op jit(solution)/shard_map/output/pallas_call | solution.py:490
  17.9 0.0 collective-permute-done.4.refs_2_
  18.0 0.0 collective-permute-done.5.refs_3_
  18.0 1.3 %collective-permute-done.6.refs_4_ = bf16[128,256]{1,0:T(8,128)(2,1)S(1)} collective-permute-done((bf16[128,256]{1,0:T(8,128)(2,1)S(1)}, bf16[128,256]{1,0:T(8,128)(2,1)S(1)}, u32[]{:S(2)}, u32[]{:S(2)}) %collective-permute-start.6) | collective-permute-done | bytes 65568 | tf_op jit(solution)/shard_map/ppermute | solution.py:66
  19.3 0.0 collective-permute-done.7.refs_5_
  19.3 0.8 %total.1 = (bf16[256,128]{1,0:T(8,128)(2,1)}, bf16[256,128]{1,0:T(8,128)(2,1)}) custom-call(f32[256,256]{1,0:T(8,128)S(1)} %get-tuple-element.38.refs_0_, f32[128,256]{1,0:T(8,128)S(1)} %get-tuple-element.39.refs_1_, bf16[128,256]{1,0:T(8,128)(2,1)S(1)} %collective-permute-done.4.refs_2_, bf16[128,256]{1,0:T(8,128)(2,1)S(1)} %collective-permute-done.5.refs_3_, ...), custom_call_target="tpu_custom_call" | custom-call | tf_op jit(solution)/shard_map/total/pallas_call | solution.py:505
Async XLA Ops:
  1.7 6.1 %collective-permute-start = (bf16[128,256]{1,0:T(8,128)(2,1)S(1)}, bf16[128,256]{1,0:T(8,128)(2,1)S(1)}, u32[]{:S(2)}, u32[]{:S(2)}) collective-permute-start(bf16[128,256]{1,0:T(8,128)(2,1)S(1)} %get-tuple-element.29), channel_id=1, source_target_pairs={{0,2},{1,3},{2,0},{3,1},{4,6},{5,7},{6,4},{7,5},{8,10},{9,11},{10,... | collective-permute-start | bytes 196616 | tf_op jit(solution)/shard_map/ppermute | solution.py:66
  4.8 3.1 %collective-permute-start.1 = (bf16[128,256]{1,0:T(8,128)(2,1)S(1)}, bf16[128,256]{1,0:T(8,128)(2,1)S(1)}, u32[]{:S(2)}, u32[]{:S(2)}) collective-permute-start(bf16[128,256]{1,0:T(8,128)(2,1)S(1)} %get-tuple-element.30), channel_id=1, source_target_pairs={{0,1},{1,0},{2,4},{3,5},{4,2},{5,3},{6,8},{7,9},{8,6},{9,7},{10,12... | collective-permute-start | bytes 196616 | tf_op jit(solution)/shard_map/ppermute | solution.py:66
  4.8 5.2 %collective-permute-start.2 = (bf16[128,256]{1,0:T(8,128)(2,1)S(1)}, bf16[128,256]{1,0:T(8,128)(2,1)S(1)}, u32[]{:S(2)}, u32[]{:S(2)}) collective-permute-start(bf16[128,256]{1,0:T(8,128)(2,1)S(1)} %get-tuple-element.31), channel_id=1, source_target_pairs={{0,4},{1,5},{2,6},{3,7},{4,0},{5,1},{6,2},{7,3},{8,12},{9,13},{10,... | collective-permute-start | bytes 196616 | tf_op jit(solution)/shard_map/ppermute | solution.py:66
  6.3 3.6 %collective-permute-start.3 = (bf16[128,256]{1,0:T(8,128)(2,1)S(1)}, bf16[128,256]{1,0:T(8,128)(2,1)S(1)}, u32[]{:S(2)}, u32[]{:S(2)}) collective-permute-start(bf16[128,256]{1,0:T(8,128)(2,1)S(1)} %get-tuple-element.32), channel_id=1, source_target_pairs={{0,1},{1,0},{2,3},{3,2},{4,8},{5,9},{6,10},{7,11},{8,4},{9,5},{10,... | collective-permute-start | bytes 196616 | tf_op jit(solution)/shard_map/ppermute | solution.py:66
  11.9 6.0 %collective-permute-start.4 = (bf16[128,256]{1,0:T(8,128)(2,1)S(1)}, bf16[128,256]{1,0:T(8,128)(2,1)S(1)}, u32[]{:S(2)}, u32[]{:S(2)}) collective-permute-start(bf16[128,256]{1,0:T(8,128)(2,1)S(1)} %get-tuple-element.40), channel_id=1, source_target_pairs={{0,2},{1,3},{2,0},{3,1},{4,6},{5,7},{6,4},{7,5},{8,10},{9,11},{10,... | collective-permute-start | bytes 196616 | tf_op jit(solution)/shard_map/ppermute | solution.py:66
  14.1 3.9 %collective-permute-start.5 = (bf16[128,256]{1,0:T(8,128)(2,1)S(1)}, bf16[128,256]{1,0:T(8,128)(2,1)S(1)}, u32[]{:S(2)}, u32[]{:S(2)}) collective-permute-start(bf16[128,256]{1,0:T(8,128)(2,1)S(1)} %get-tuple-element.41), channel_id=1, source_target_pairs={{0,1},{1,0},{2,4},{3,5},{4,2},{5,3},{6,8},{7,9},{8,6},{9,7},{10,12... | collective-permute-start | bytes 196616 | tf_op jit(solution)/shard_map/ppermute | solution.py:66
  14.1 5.2 %collective-permute-start.6 = (bf16[128,256]{1,0:T(8,128)(2,1)S(1)}, bf16[128,256]{1,0:T(8,128)(2,1)S(1)}, u32[]{:S(2)}, u32[]{:S(2)}) collective-permute-start(bf16[128,256]{1,0:T(8,128)(2,1)S(1)} %get-tuple-element.42), channel_id=1, source_target_pairs={{0,4},{1,5},{2,6},{3,7},{4,0},{5,1},{6,2},{7,3},{8,12},{9,13},{10,... | collective-permute-start | bytes 196616 | tf_op jit(solution)/shard_map/ppermute | solution.py:66
  16.1 3.2 %collective-permute-start.7 = (bf16[128,256]{1,0:T(8,128)(2,1)S(1)}, bf16[128,256]{1,0:T(8,128)(2,1)S(1)}, u32[]{:S(2)}, u32[]{:S(2)}) collective-permute-start(bf16[128,256]{1,0:T(8,128)(2,1)S(1)} %get-tuple-element.43), channel_id=1, source_target_pairs={{0,1},{1,0},{2,3},{3,2},{4,8},{5,9},{6,10},{7,11},{8,4},{9,5},{10,... | collective-permute-start | bytes 196616 | tf_op jit(solution)/shard_map/ppermute | solution.py:66

commit v7 on v6

--- a/solution.py
+++ b/solution.py
@@ -70,33 +70,36 @@
     return range(-(slot - 1), slot, 2)
 
 
-def pack_kernel(sets, k_hbm, v_hbm, mine, *refs):
-    halves = [s for s in sets if not s["full"]]
-    outs, sems = refs[: len(halves)], refs[len(halves)]
+def pack_kernel(sets, k_hbm, v_hbm, *refs):
+    outs, sems = refs[: len(sets)], refs[len(sets)]
     me = lax.axis_index("ctx")
     length = k_hbm.shape[0] // 2
     width = k_hbm.shape[1]
-    copies = [
-        pltpu.make_async_copy(k_hbm, mine.at[:, :width], sems.at[0]),
-        pltpu.make_async_copy(v_hbm, mine.at[:, width:], sems.at[1]),
-    ]
-    for i, (entry, out) in enumerate(zip(halves, outs)):
+    copies = []
+    for i, (entry, out) in enumerate(zip(sets, outs)):
         first = (me // entry["offset"]) % 2 == entry["colour"]
         rows = pl.ds(pl.multiple_of(jnp.where(first, 0, length), length), length)
-        copies.append(pltpu.make_async_copy(k_hbm.at[rows, :], out.at[:, :width], sems.at[2 * i + 2]))
-        copies.append(pltpu.make_async_copy(v_hbm.at[rows, :], out.at[:, width:], sems.at[2 * i + 3]))
+        for a, hbm in enumerate((k_hbm, v_hbm)):
+            src = hbm if entry["full"] else hbm.at[rows, :]
+            cols = slice(a * width, (a + 1) * width)
+            copies.append(pltpu.make_async_copy(src, out.at[:, cols], sems.at[i, a]))
     for copy in copies:
         copy.start()
     for copy in copies:
         copy.wait()
 
 
-def stage_kernel(ctx_count, docs_hbm, q_hbm, g_hbm, q_all, g_all, bias, docs_ref, sems):
+def stage_kernel(
+    ctx_count, docs_hbm, q_hbm, g_hbm, k_hbm, v_hbm, q_all, g_all, mine, bias, docs_ref, sems
+):
     length = q_hbm.shape[0] // 2
     heads, _, width = q_all.shape
     lengths = pltpu.make_async_copy(docs_hbm, docs_ref, sems.at[2, 0])
     lengths.start()
-    copies = []
+    copies = [
+        pltpu.make_async_copy(k_hbm, mine.at[:, :width], sems.at[2, 1]),
+        pltpu.make_async_copy(v_hbm, mine.at[:, width:], sems.at[2, 2]),
+    ]
     for h in range(heads):
         cols = slice(h * width, (h + 1) * width)
         for a, (src, dst) in enumerate(((q_hbm, q_all), (g_hbm, g_all))):
@@ -435,36 +438,40 @@
     span = (reach + 1) * length
     heads = query_rows.shape[1] // width
     sets = exchanges(ctx_count, reach)
-    fulls = sum(s["full"] for s in sets)
     count = len(sets)
     payloads = [
         pltpu.VMEM((2 * length if s["full"] else length, 2 * width), jnp.bfloat16) for s in sets
     ]
-    mine, *halves = pl.pallas_call(
+    keys_values = off_chip([key_rows, value_rows])
+    packed = pl.pallas_call(
         lambda *refs: pack_kernel(sets, *refs),
-        out_shape=[pltpu.VMEM((tok_dev, 2 * width), jnp.bfloat16)] + payloads[fulls:],
+        out_shape=payloads,
         in_specs=in_place(2),
-        out_specs=in_vmem(1 + count - fulls),
-        scratch_shapes=[pltpu.SemaphoreType.DMA((2 + 2 * (count - fulls),))],
+        out_specs=in_vmem(count),
+        scratch_shapes=[pltpu.SemaphoreType.DMA((count, 2))],
         compiler_params=pltpu.CompilerParams(vmem_limit_bytes=VMEM_LIMIT),
         name="pack",
-    )(*off_chip([key_rows, value_rows]))
-    packed = [mine] * fulls + halves
+    )(*keys_values)
     received = [swap(p, s, ctx_count, head_count) for p, s in zip(packed, sets)]
 
     stack = pltpu.VMEM((heads, tok_dev, width), jnp.bfloat16)
-    q_all, g_all, bias = pl.pallas_call(
+    q_all, g_all, mine, bias = pl.pallas_call(
         lambda *refs: stage_kernel(ctx_count, *refs),
-        out_shape=[stack, stack, pltpu.VMEM((2, 2, reach * length, length), jnp.float32)],
-        in_specs=in_place(3),
-        out_specs=in_vmem(3),
+        out_shape=[
+            stack,
+            stack,
+            pltpu.VMEM((tok_dev, 2 * width), jnp.bfloat16),
+            pltpu.VMEM((2, 2, reach * length, length), jnp.float32),
+        ],
+        in_specs=in_place(5),
+        out_specs=in_vmem(4),
         scratch_shapes=[
             pltpu.SMEM(doc_lengths.shape, jnp.int32),
             pltpu.SemaphoreType.DMA((3, heads)),
         ],
         compiler_params=pltpu.CompilerParams(vmem_limit_bytes=VMEM_LIMIT),
         name="stage",
-    )(*off_chip([doc_lengths, query_rows, out_grad]))
+    )(*off_chip([doc_lengths, query_rows, out_grad]), *keys_values)
 
     low_weights = pltpu.VMEM((2, heads, reach * length, length), jnp.bfloat16)
     pb, dsb, kv_win, folded, *partials = pl.pallas_call(

time: 20.3 us -> 20.2 us (level)
  transfers between devices with their start and end apart: 8 -> 8, of which waited for: 2 -> 2; matrix products, arithmetic and copies ran while one was open for 0% -> 0% of each run, Pallas kernels for 16% -> 17%
where the time goes in v7:
time: 20.2 us; the launch traced here: 20 us
  starting transfers between devices  8.83 us (44%)
  Pallas kernels  7 us (35%)
  waiting for transfers between devices  3.44 us (17%)
  between operations  0.7 us (3%)
    ppermute x8, starting transfers between devices, swap(): return lax.ppermute(value, ('ctx', 'head'), pairs)  8.83 us
    ppermute x8, waiting for transfers between devices, swap(): return lax.ppermute(value, ('ctx', 'head'), pairs)  3.44 us
    pallas_call x1, Pallas kernels, attention(): pl.pallas_call(lambda *refs: score_kernel(sets, ctx_count, reach, *refs),...  1.94 us
    pallas_call x1, Pallas kernels, attention(): pl.pallas_call(output_kernel, out_shape=[jax.ShapeDtypeStruct(query_rows....  1.82 us
    pallas_call x1, Pallas kernels, attention(): pl.pallas_call(lambda *refs: stage_kernel(ctx_count, *refs), out_shape=[s...  1.51 us
    pallas_call x1, Pallas kernels, attention(): pl.pallas_call(lambda *refs: pack_kernel(sets, *refs), out_shape=payloads...  0.96 us
    pallas_call x1, Pallas kernels, attention(): pl.pallas_call(lambda *refs: sum_kernel(sets, ctx_count, *refs), out_shap...  0.77 us
  transfers between devices with their start and end apart: 8, of which 2 were waited for; matrix products, arithmetic and copies ran while one was open for 0% of the time, Pallas kernels for 17%

profile of v7, /device:TPU:0, one launch (start us, length us, event | category | flops | bytes accessed | tf_op | source)
XLA Modules:
  0.0 20.0 jit_solution(11046363429568634463)
XLA Ops:
  0.6 1.0 %pack.1 = (bf16[128,256]{1,0:T(8,128)(2,1)S(1)}, bf16[128,256]{1,0:T(8,128)(2,1)S(1)}, bf16[128,256]{1,0:T(8,128)(2,1)S(1)}, bf16[128,256]{1,0:T(8,128)(2,1)S(1)}) custom-call(bf16[256,128]{1,0:T(8,128)(2,1)} %refs_0_.3, bf16[256,128]{1,0:T(8,128)(2,1)} %refs_1_.3), custom_call_target="tpu_custom_call" | custom-call | tf_op jit(solution)/shard_map/pack/pallas_call | solution.py:446
  1.6 3.1 %collective-permute-start = (bf16[128,256]{1,0:T(8,128)(2,1)S(1)}, bf16[128,256]{1,0:T(8,128)(2,1)S(1)}, u32[]{:S(2)}, u32[]{:S(2)}) collective-permute-start(bf16[128,256]{1,0:T(8,128)(2,1)S(1)} %get-tuple-element.29), channel_id=1, source_target_pairs={{0,2},{1,3},{2,0},{3,1},{4,6},{5,7},{6,4},{7,5},{8,10},{9,11},{10,... | collective-permute-start | bytes 196616 | tf_op jit(solution)/shard_map/ppermute | solution.py:66
  4.7 0.0 collective-permute-start.1
  4.7 1.6 %collective-permute-start.2 = (bf16[128,256]{1,0:T(8,128)(2,1)S(1)}, bf16[128,256]{1,0:T(8,128)(2,1)S(1)}, u32[]{:S(2)}, u32[]{:S(2)}) collective-permute-start(bf16[128,256]{1,0:T(8,128)(2,1)S(1)} %get-tuple-element.31), channel_id=1, source_target_pairs={{0,4},{1,5},{2,6},{3,7},{4,0},{5,1},{6,2},{7,3},{8,12},{9,13},{10,... | collective-permute-start | bytes 196616 | tf_op jit(solution)/shard_map/ppermute | solution.py:66
  6.2 0.0 collective-permute-start.3
  6.2 1.5 %stage.1 = (bf16[8,256,128]{2,1,0:T(8,128)(2,1)S(1)}, bf16[8,256,128]{2,1,0:T(8,128)(2,1)S(1)}, bf16[256,256]{1,0:T(8,128)(2,1)S(1)}, f32[2,2,256,128]{3,2,1,0:T(8,128)S(1)}) custom-call(s32[16]{0:T(128)} %refs_0_.2, bf16[256,1024]{1,0:T(8,128)(2,1)} %refs_1_.2, bf16[256,1024]{1,0:T(8,128)(2,1)} %refs_2_.1, bf16[256,128]{1,0:T(8,128)(2,1)} %refs_0_.3, ...), custom_call_target="tpu_custom_call" | custom-call | tf_op jit(solution)/shard_map/stage/pallas_call | solution.py:458
  7.8 0.0 collective-permute-done.refs_4_
  7.8 0.0 collective-permute-done.1.refs_5_
  7.8 2.1 %collective-permute-done.2.refs_6_ = bf16[128,256]{1,0:T(8,128)(2,1)S(1)} collective-permute-done((bf16[128,256]{1,0:T(8,128)(2,1)S(1)}, bf16[128,256]{1,0:T(8,128)(2,1)S(1)}, u32[]{:S(2)}, u32[]{:S(2)}) %collective-permute-start.2) | collective-permute-done | bytes 65568 | tf_op jit(solution)/shard_map/ppermute | solution.py:66
  9.9 0.0 collective-permute-done.3.refs_7_
  9.9 1.9 %score.1 = (bf16[2,8,256,128]{3,2,1,0:T(8,128)(2,1)S(1)}, bf16[2,8,256,128]{3,2,1,0:T(8,128)(2,1)S(1)}, bf16[2,384,256]{2,1,0:T(8,128)(2,1)S(1)}, f32[128,256]{1...) custom-call(f32[2,2,256,128]{3,2,1,0:T(8,128)S(1)} %get-tuple-elemen, ...), custom_call_target="tpu_custom_call" | custom-call | tf_op jit(solution)/shard_map/score/pallas_call | solution.py:477
  11.8 2.2 %collective-permute-start.4 = (bf16[128,256]{1,0:T(8,128)(2,1)S(1)}, bf16[128,256]{1,0:T(8,128)(2,1)S(1)}, u32[]{:S(2)}, u32[]{:S(2)}) collective-permute-start(bf16[128,256]{1,0:T(8,128)(2,1)S(1)} %get-tuple-element.40), channel_id=1, source_target_pairs={{0,2},{1,3},{2,0},{3,1},{4,6},{5,7},{6,4},{7,5},{8,10},{9,11},{10,... | collective-permute-start | bytes 196616 | tf_op jit(solution)/shard_map/ppermute | solution.py:66
  14.0 0.0 collective-permute-start.5
  14.0 2.0 %collective-permute-start.6 = (bf16[128,256]{1,0:T(8,128)(2,1)S(1)}, bf16[128,256]{1,0:T(8,128)(2,1)S(1)}, u32[]{:S(2)}, u32[]{:S(2)}) collective-permute-start(bf16[128,256]{1,0:T(8,128)(2,1)S(1)} %get-tuple-element.42), channel_id=1, source_target_pairs={{0,4},{1,5},{2,6},{3,7},{4,0},{5,1},{6,2},{7,3},{8,12},{9,13},{10,... | collective-permute-start | bytes 196616 | tf_op jit(solution)/shard_map/ppermute | solution.py:66
  16.0 0.0 collective-permute-start.7
  16.0 1.8 %output.1 = (bf16[256,1024]{1,0:T(8,128)(2,1)}, bf16[256,1024]{1,0:T(8,128)(2,1)}, f32[256,256]{1,0:T(8,128)S(1)}) custom-call(bf16[2,8,256,128]{3,2,1,0:T(8,128)(2,1)S(1)} %get-tuple-element.33.pb, bf16[2,8,256,128]{3,2,1,0:T(8,128)(2,1)S(1)} %get-tuple-element.34.dsb, bf16[2,384,256]{2,1,0:T(8,128)(2,1)S(1)} %get-tuple-element.35.kv_win, ...), custom_call_target="tpu_custom_call" | custom-call | tf_op jit(solution)/shard_map/output/pallas_call | solution.py:497
  17.8 0.0 collective-permute-done.4.refs_2_
  17.9 0.0 collective-permute-done.5.refs_3_
  17.9 1.3 %collective-permute-done.6.refs_4_ = bf16[128,256]{1,0:T(8,128)(2,1)S(1)} collective-permute-done((bf16[128,256]{1,0:T(8,128)(2,1)S(1)}, bf16[128,256]{1,0:T(8,128)(2,1)S(1)}, u32[]{:S(2)}, u32[]{:S(2)}) %collective-permute-start.6) | collective-permute-done | bytes 65568 | tf_op jit(solution)/shard_map/ppermute | solution.py:66
  19.2 0.0 collective-permute-done.7.refs_5_
  19.2 0.8 %total.1 = (bf16[256,128]{1,0:T(8,128)(2,1)}, bf16[256,128]{1,0:T(8,128)(2,1)}) custom-call(f32[256,256]{1,0:T(8,128)S(1)} %get-tuple-element.38.refs_0_, f32[128,256]{1,0:T(8,128)S(1)} %get-tuple-element.39.refs_1_, bf16[128,256]{1,0:T(8,128)(2,1)S(1)} %collective-permute-done.4.refs_2_, bf16[128,256]{1,0:T(8,128)(2,1)S(1)} %collective-permute-done.5.refs_3_, ...), custom_call_target="tpu_custom_call" | custom-call | tf_op jit(solution)/shard_map/total/pallas_call | solution.py:512
Async XLA Ops:
  1.6 6.2 %collective-permute-start = (bf16[128,256]{1,0:T(8,128)(2,1)S(1)}, bf16[128,256]{1,0:T(8,128)(2,1)S(1)}, u32[]{:S(2)}, u32[]{:S(2)}) collective-permute-start(bf16[128,256]{1,0:T(8,128)(2,1)S(1)} %get-tuple-element.29), channel_id=1, source_target_pairs={{0,2},{1,3},{2,0},{3,1},{4,6},{5,7},{6,4},{7,5},{8,10},{9,11},{10,... | collective-permute-start | bytes 196616 | tf_op jit(solution)/shard_map/ppermute | solution.py:66
  4.7 3.1 %collective-permute-start.1 = (bf16[128,256]{1,0:T(8,128)(2,1)S(1)}, bf16[128,256]{1,0:T(8,128)(2,1)S(1)}, u32[]{:S(2)}, u32[]{:S(2)}) collective-permute-start(bf16[128,256]{1,0:T(8,128)(2,1)S(1)} %get-tuple-element.30), channel_id=1, source_target_pairs={{0,1},{1,0},{2,4},{3,5},{4,2},{5,3},{6,8},{7,9},{8,6},{9,7},{10,12... | collective-permute-start | bytes 196616 | tf_op jit(solution)/shard_map/ppermute | solution.py:66
  4.7 5.2 %collective-permute-start.2 = (bf16[128,256]{1,0:T(8,128)(2,1)S(1)}, bf16[128,256]{1,0:T(8,128)(2,1)S(1)}, u32[]{:S(2)}, u32[]{:S(2)}) collective-permute-start(bf16[128,256]{1,0:T(8,128)(2,1)S(1)} %get-tuple-element.31), channel_id=1, source_target_pairs={{0,4},{1,5},{2,6},{3,7},{4,0},{5,1},{6,2},{7,3},{8,12},{9,13},{10,... | collective-permute-start | bytes 196616 | tf_op jit(solution)/shard_map/ppermute | solution.py:66
  6.2 3.6 %collective-permute-start.3 = (bf16[128,256]{1,0:T(8,128)(2,1)S(1)}, bf16[128,256]{1,0:T(8,128)(2,1)S(1)}, u32[]{:S(2)}, u32[]{:S(2)}) collective-permute-start(bf16[128,256]{1,0:T(8,128)(2,1)S(1)} %get-tuple-element.32), channel_id=1, source_target_pairs={{0,1},{1,0},{2,3},{3,2},{4,8},{5,9},{6,10},{7,11},{8,4},{9,5},{10,... | collective-permute-start | bytes 196616 | tf_op jit(solution)/shard_map/ppermute | solution.py:66
  11.8 6.0 %collective-permute-start.4 = (bf16[128,256]{1,0:T(8,128)(2,1)S(1)}, bf16[128,256]{1,0:T(8,128)(2,1)S(1)}, u32[]{:S(2)}, u32[]{:S(2)}) collective-permute-start(bf16[128,256]{1,0:T(8,128)(2,1)S(1)} %get-tuple-element.40), channel_id=1, source_target_pairs={{0,2},{1,3},{2,0},{3,1},{4,6},{5,7},{6,4},{7,5},{8,10},{9,11},{10,... | collective-permute-start | bytes 196616 | tf_op jit(solution)/shard_map/ppermute | solution.py:66
  14.0 3.9 %collective-permute-start.5 = (bf16[128,256]{1,0:T(8,128)(2,1)S(1)}, bf16[128,256]{1,0:T(8,128)(2,1)S(1)}, u32[]{:S(2)}, u32[]{:S(2)}) collective-permute-start(bf16[128,256]{1,0:T(8,128)(2,1)S(1)} %get-tuple-element.41), channel_id=1, source_target_pairs={{0,1},{1,0},{2,4},{3,5},{4,2},{5,3},{6,8},{7,9},{8,6},{9,7},{10,12... | collective-permute-start | bytes 196616 | tf_op jit(solution)/shard_map/ppermute | solution.py:66
  14.0 5.2 %collective-permute-start.6 = (bf16[128,256]{1,0:T(8,128)(2,1)S(1)}, bf16[128,256]{1,0:T(8,128)(2,1)S(1)}, u32[]{:S(2)}, u32[]{:S(2)}) collective-permute-start(bf16[128,256]{1,0:T(8,128)(2,1)S(1)} %get-tuple-element.42), channel_id=1, source_target_pairs={{0,4},{1,5},{2,6},{3,7},{4,0},{5,1},{6,2},{7,3},{8,12},{9,13},{10,... | collective-permute-start | bytes 196616 | tf_op jit(solution)/shard_map/ppermute | solution.py:66
  16.0 3.2 %collective-permute-start.7 = (bf16[128,256]{1,0:T(8,128)(2,1)S(1)}, bf16[128,256]{1,0:T(8,128)(2,1)S(1)}, u32[]{:S(2)}, u32[]{:S(2)}) collective-permute-start(bf16[128,256]{1,0:T(8,128)(2,1)S(1)} %get-tuple-element.43), channel_id=1, source_target_pairs={{0,1},{1,0},{2,3},{3,2},{4,8},{5,9},{6,10},{7,11},{8,4},{9,5},{10,... | collective-permute-start | bytes 196616 | tf_op jit(solution)/shard_map/ppermute | solution.py:66

commit v8 on v7

--- a/solution.py
+++ b/solution.py
@@ -386,30 +386,37 @@
 
 
 def sum_kernel(sets, ctx_count, own_ref, fold_ref, *refs):
-    dk_ref, dv_ref = refs[len(sets) :]
+    dk_hbm, dv_hbm, dk, dv, sems = refs[len(sets) :]
     me = lax.axis_index("ctx")
     length = own_ref.shape[0] // 2
-    width = dk_ref.shape[1]
-    low = own_ref[:length, :] + fold_ref[...]
-    up = own_ref[length:, :]
-    for entry, ref in zip(sets, refs):
-        offset = entry["offset"]
-        first = (me // offset) % 2 == entry["colour"]
-        as_first = first & (me + offset < ctx_count)
-        as_second = jnp.logical_not(first) & (me >= offset)
-        if entry["full"]:
-            low = low + jnp.where(as_first | as_second, ref[:length, :].astype(jnp.float32), 0.0)
-            up = up + jnp.where(as_second, ref[length:, :].astype(jnp.float32), 0.0)
-        else:
-            part = ref[...].astype(jnp.float32)
-            for pair in entry["folds"]:
-                as_first = as_first & (me != pair[0]) | (me == pair[1])
-            low = low + jnp.where(as_first, part, 0.0)
-            up = up + jnp.where(as_second, part, 0.0)
-    dk_ref[:length, :] = low[:, :width].astype(jnp.bfloat16)
-    dk_ref[length:, :] = up[:, :width].astype(jnp.bfloat16)
-    dv_ref[:length, :] = low[:, width:].astype(jnp.bfloat16)
-    dv_ref[length:, :] = up[:, width:].astype(jnp.bfloat16)
+    width = dk.shape[1]
+    copies = []
+    for a, (stage, hbm) in enumerate(((dk, dk_hbm), (dv, dv_hbm))):
+        cols = slice(a * width, (a + 1) * width)
+        low = own_ref[:length, cols] + fold_ref[:, cols]
+        up = own_ref[length:, cols]
+        for entry, ref in zip(sets, refs):
+            offset = entry["offset"]
+            first = (me // offset) % 2 == entry["colour"]
+            as_first = first & (me + offset < ctx_count)
+            as_second = jnp.logical_not(first) & (me >= offset)
+            if entry["full"]:
+                to_low = ref[:length, cols].astype(jnp.float32)
+                low = low + jnp.where(as_first | as_second, to_low, 0.0)
+                up = up + jnp.where(as_second, ref[length:, cols].astype(jnp.float32), 0.0)
+            else:
+                part = ref[:, cols].astype(jnp.float32)
+                for pair in entry["folds"]:
+                    as_first = as_first & (me != pair[0]) | (me == pair[1])
+                low = low + jnp.where(as_first, part, 0.0)
+                up = up + jnp.where(as_second, part, 0.0)
+        stage[:length, :] = low.astype(jnp.bfloat16)
+        stage[length:, :] = up.astype(jnp.bfloat16)
+        copy = pltpu.make_async_copy(stage, hbm, sems.at[a])
+        copy.start()
+        copies.append(copy)
+    for copy in copies:
+        copy.wait()
 
 
 def in_vmem(amount):
@@ -513,7 +520,9 @@
         lambda *refs: sum_kernel(sets, ctx_count, *refs),
         out_shape=[jax.ShapeDtypeStruct(key_rows.shape, jnp.bfloat16)] * 2,
         in_specs=in_vmem(2 + count),
-        out_specs=in_vmem(2),
+        out_specs=in_place(2),
+        scratch_shapes=[pltpu.VMEM(key_rows.shape, jnp.bfloat16)] * 2
+        + [pltpu.SemaphoreType.DMA((2,))],
         compiler_params=pltpu.CompilerParams(vmem_limit_bytes=VMEM_LIMIT),
         name="total",
     )(*on_chip([own, folded, *returned]))

time: 20.2 us -> 20.3 us (level)
  no operation moved by 1% of the time
where the time goes in v8:
time: 20.3 us; the launch traced here: 20 us
  starting transfers between devices  8.83 us (43%)
  Pallas kernels  7.01 us (35%)
  waiting for transfers between devices  3.44 us (17%)
  between operations  0.7 us (3%)
    ppermute x8, starting transfers between devices, swap(): return lax.ppermute(value, ('ctx', 'head'), pairs)  8.83 us
    ppermute x8, waiting for transfers between devices, swap(): return lax.ppermute(value, ('ctx', 'head'), pairs)  3.44 us
    pallas_call x1, Pallas kernels, attention(): pl.pallas_call(lambda *refs: score_kernel(sets, ctx_count, reach, *refs),...  1.94 us
    pallas_call x1, Pallas kernels, attention(): pl.pallas_call(output_kernel, out_shape=[jax.ShapeDtypeStruct(query_rows....  1.82 us
    pallas_call x1, Pallas kernels, attention(): pl.pallas_call(lambda *refs: stage_kernel(ctx_count, *refs), out_shape=[s...  1.51 us
    pallas_call x1, Pallas kernels, attention(): pl.pallas_call(lambda *refs: pack_kernel(sets, *refs), out_shape=payloads...  0.96 us
    pallas_call x1, Pallas kernels, attention(): pl.pallas_call(lambda *refs: sum_kernel(sets, ctx_count, *refs), out_shap...  0.78 us
  transfers between devices with their start and end apart: 8, of which 2 were waited for; matrix products, arithmetic and copies ran while one was open for 0% of the time, Pallas kernels for 17%

profile of v8, /device:TPU:0, one launch (start us, length us, event | category | flops | bytes accessed | tf_op | source)
XLA Modules:
  0.0 20.0 jit_solution(13751181436733514572)
XLA Ops:
  0.6 1.0 %pack.1 = (bf16[128,256]{1,0:T(8,128)(2,1)S(1)}, bf16[128,256]{1,0:T(8,128)(2,1)S(1)}, bf16[128,256]{1,0:T(8,128)(2,1)S(1)}, bf16[128,256]{1,0:T(8,128)(2,1)S(1)}) custom-call(bf16[256,128]{1,0:T(8,128)(2,1)} %refs_0_.3, bf16[256,128]{1,0:T(8,128)(2,1)} %refs_1_.3), custom_call_target="tpu_custom_call" | custom-call | tf_op jit(solution)/shard_map/pack/pallas_call | solution.py:453
  1.6 3.1 %collective-permute-start = (bf16[128,256]{1,0:T(8,128)(2,1)S(1)}, bf16[128,256]{1,0:T(8,128)(2,1)S(1)}, u32[]{:S(2)}, u32[]{:S(2)}) collective-permute-start(bf16[128,256]{1,0:T(8,128)(2,1)S(1)} %get-tuple-element.29), channel_id=1, source_target_pairs={{0,2},{1,3},{2,0},{3,1},{4,6},{5,7},{6,4},{7,5},{8,10},{9,11},{10,... | collective-permute-start | bytes 196616 | tf_op jit(solution)/shard_map/ppermute | solution.py:66
  4.7 0.0 collective-permute-start.1
  4.7 1.6 %collective-permute-start.2 = (bf16[128,256]{1,0:T(8,128)(2,1)S(1)}, bf16[128,256]{1,0:T(8,128)(2,1)S(1)}, u32[]{:S(2)}, u32[]{:S(2)}) collective-permute-start(bf16[128,256]{1,0:T(8,128)(2,1)S(1)} %get-tuple-element.31), channel_id=1, source_target_pairs={{0,4},{1,5},{2,6},{3,7},{4,0},{5,1},{6,2},{7,3},{8,12},{9,13},{10,... | collective-permute-start | bytes 196616 | tf_op jit(solution)/shard_map/ppermute | solution.py:66
  6.2 0.0 collective-permute-start.3
  6.2 1.5 %stage.1 = (bf16[8,256,128]{2,1,0:T(8,128)(2,1)S(1)}, bf16[8,256,128]{2,1,0:T(8,128)(2,1)S(1)}, bf16[256,256]{1,0:T(8,128)(2,1)S(1)}, f32[2,2,256,128]{3,2,1,0:T(8,128)S(1)}) custom-call(s32[16]{0:T(128)} %refs_0_.2, bf16[256,1024]{1,0:T(8,128)(2,1)} %refs_1_.2, bf16[256,1024]{1,0:T(8,128)(2,1)} %refs_2_.1, bf16[256,128]{1,0:T(8,128)(2,1)} %refs_0_.3, ...), custom_call_target="tpu_custom_call" | custom-call | tf_op jit(solution)/shard_map/stage/pallas_call | solution.py:465
  7.8 0.0 collective-permute-done.refs_4_
  7.8 0.0 collective-permute-done.1.refs_5_
  7.8 2.1 %collective-permute-done.2.refs_6_ = bf16[128,256]{1,0:T(8,128)(2,1)S(1)} collective-permute-done((bf16[128,256]{1,0:T(8,128)(2,1)S(1)}, bf16[128,256]{1,0:T(8,128)(2,1)S(1)}, u32[]{:S(2)}, u32[]{:S(2)}) %collective-permute-start.2) | collective-permute-done | bytes 65568 | tf_op jit(solution)/shard_map/ppermute | solution.py:66
  9.9 0.0 collective-permute-done.3.refs_7_
  9.9 1.9 %score.1 = (bf16[2,8,256,128]{3,2,1,0:T(8,128)(2,1)S(1)}, bf16[2,8,256,128]{3,2,1,0:T(8,128)(2,1)S(1)}, bf16[2,384,256]{2,1,0:T(8,128)(2,1)S(1)}, f32[128,256]{1...) custom-call(f32[2,2,256,128]{3,2,1,0:T(8,128)S(1)} %get-tuple-elemen, ...), custom_call_target="tpu_custom_call" | custom-call | tf_op jit(solution)/shard_map/score/pallas_call | solution.py:484
  11.8 2.2 %collective-permute-start.4 = (bf16[128,256]{1,0:T(8,128)(2,1)S(1)}, bf16[128,256]{1,0:T(8,128)(2,1)S(1)}, u32[]{:S(2)}, u32[]{:S(2)}) collective-permute-start(bf16[128,256]{1,0:T(8,128)(2,1)S(1)} %get-tuple-element.40), channel_id=1, source_target_pairs={{0,2},{1,3},{2,0},{3,1},{4,6},{5,7},{6,4},{7,5},{8,10},{9,11},{10,... | collective-permute-start | bytes 196616 | tf_op jit(solution)/shard_map/ppermute | solution.py:66
  14.0 0.0 collective-permute-start.5
  14.0 2.0 %collective-permute-start.6 = (bf16[128,256]{1,0:T(8,128)(2,1)S(1)}, bf16[128,256]{1,0:T(8,128)(2,1)S(1)}, u32[]{:S(2)}, u32[]{:S(2)}) collective-permute-start(bf16[128,256]{1,0:T(8,128)(2,1)S(1)} %get-tuple-element.42), channel_id=1, source_target_pairs={{0,4},{1,5},{2,6},{3,7},{4,0},{5,1},{6,2},{7,3},{8,12},{9,13},{10,... | collective-permute-start | bytes 196616 | tf_op jit(solution)/shard_map/ppermute | solution.py:66
  16.0 0.0 collective-permute-start.7
  16.0 1.8 %output.1 = (bf16[256,1024]{1,0:T(8,128)(2,1)}, bf16[256,1024]{1,0:T(8,128)(2,1)}, f32[256,256]{1,0:T(8,128)S(1)}) custom-call(bf16[2,8,256,128]{3,2,1,0:T(8,128)(2,1)S(1)} %get-tuple-element.33.pb, bf16[2,8,256,128]{3,2,1,0:T(8,128)(2,1)S(1)} %get-tuple-element.34.dsb, bf16[2,384,256]{2,1,0:T(8,128)(2,1)S(1)} %get-tuple-element.35.kv_win, ...), custom_call_target="tpu_custom_call" | custom-call | tf_op jit(solution)/shard_map/output/pallas_call | solution.py:504
  17.8 0.0 collective-permute-done.4.refs_2_
  17.9 0.0 collective-permute-done.5.refs_3_
  17.9 1.3 %collective-permute-done.6.refs_4_ = bf16[128,256]{1,0:T(8,128)(2,1)S(1)} collective-permute-done((bf16[128,256]{1,0:T(8,128)(2,1)S(1)}, bf16[128,256]{1,0:T(8,128)(2,1)S(1)}, u32[]{:S(2)}, u32[]{:S(2)}) %collective-permute-start.6) | collective-permute-done | bytes 65568 | tf_op jit(solution)/shard_map/ppermute | solution.py:66
  19.2 0.0 collective-permute-done.7.refs_5_
  19.2 0.8 %total.1 = (bf16[256,128]{1,0:T(8,128)(2,1)}, bf16[256,128]{1,0:T(8,128)(2,1)}) custom-call(f32[256,256]{1,0:T(8,128)S(1)} %get-tuple-element.38.refs_0_, f32[128,256]{1,0:T(8,128)S(1)} %get-tuple-element.39.refs_1_, bf16[128,256]{1,0:T(8,128)(2,1)S(1)} %collective-permute-done.4.refs_2_, bf16[128,256]{1,0:T(8,128)(2,1)S(1)} %collective-permute-done.5.refs_3_, ...), custom_call_target="tpu_custom_call" | custom-call | tf_op jit(solution)/shard_map/total/pallas_call | solution.py:519
Async XLA Ops:
  1.6 6.2 %collective-permute-start = (bf16[128,256]{1,0:T(8,128)(2,1)S(1)}, bf16[128,256]{1,0:T(8,128)(2,1)S(1)}, u32[]{:S(2)}, u32[]{:S(2)}) collective-permute-start(bf16[128,256]{1,0:T(8,128)(2,1)S(1)} %get-tuple-element.29), channel_id=1, source_target_pairs={{0,2},{1,3},{2,0},{3,1},{4,6},{5,7},{6,4},{7,5},{8,10},{9,11},{10,... | collective-permute-start | bytes 196616 | tf_op jit(solution)/shard_map/ppermute | solution.py:66
  4.7 3.1 %collective-permute-start.1 = (bf16[128,256]{1,0:T(8,128)(2,1)S(1)}, bf16[128,256]{1,0:T(8,128)(2,1)S(1)}, u32[]{:S(2)}, u32[]{:S(2)}) collective-permute-start(bf16[128,256]{1,0:T(8,128)(2,1)S(1)} %get-tuple-element.30), channel_id=1, source_target_pairs={{0,1},{1,0},{2,4},{3,5},{4,2},{5,3},{6,8},{7,9},{8,6},{9,7},{10,12... | collective-permute-start | bytes 196616 | tf_op jit(solution)/shard_map/ppermute | solution.py:66
  4.7 5.2 %collective-permute-start.2 = (bf16[128,256]{1,0:T(8,128)(2,1)S(1)}, bf16[128,256]{1,0:T(8,128)(2,1)S(1)}, u32[]{:S(2)}, u32[]{:S(2)}) collective-permute-start(bf16[128,256]{1,0:T(8,128)(2,1)S(1)} %get-tuple-element.31), channel_id=1, source_target_pairs={{0,4},{1,5},{2,6},{3,7},{4,0},{5,1},{6,2},{7,3},{8,12},{9,13},{10,... | collective-permute-start | bytes 196616 | tf_op jit(solution)/shard_map/ppermute | solution.py:66
  6.2 3.6 %collective-permute-start.3 = (bf16[128,256]{1,0:T(8,128)(2,1)S(1)}, bf16[128,256]{1,0:T(8,128)(2,1)S(1)}, u32[]{:S(2)}, u32[]{:S(2)}) collective-permute-start(bf16[128,256]{1,0:T(8,128)(2,1)S(1)} %get-tuple-element.32), channel_id=1, source_target_pairs={{0,1},{1,0},{2,3},{3,2},{4,8},{5,9},{6,10},{7,11},{8,4},{9,5},{10,... | collective-permute-start | bytes 196616 | tf_op jit(solution)/shard_map/ppermute | solution.py:66
  11.8 6.0 %collective-permute-start.4 = (bf16[128,256]{1,0:T(8,128)(2,1)S(1)}, bf16[128,256]{1,0:T(8,128)(2,1)S(1)}, u32[]{:S(2)}, u32[]{:S(2)}) collective-permute-start(bf16[128,256]{1,0:T(8,128)(2,1)S(1)} %get-tuple-element.40), channel_id=1, source_target_pairs={{0,2},{1,3},{2,0},{3,1},{4,6},{5,7},{6,4},{7,5},{8,10},{9,11},{10,... | collective-permute-start | bytes 196616 | tf_op jit(solution)/shard_map/ppermute | solution.py:66
  14.0 3.9 %collective-permute-start.5 = (bf16[128,256]{1,0:T(8,128)(2,1)S(1)}, bf16[128,256]{1,0:T(8,128)(2,1)S(1)}, u32[]{:S(2)}, u32[]{:S(2)}) collective-permute-start(bf16[128,256]{1,0:T(8,128)(2,1)S(1)} %get-tuple-element.41), channel_id=1, source_target_pairs={{0,1},{1,0},{2,4},{3,5},{4,2},{5,3},{6,8},{7,9},{8,6},{9,7},{10,12... | collective-permute-start | bytes 196616 | tf_op jit(solution)/shard_map/ppermute | solution.py:66
  14.0 5.2 %collective-permute-start.6 = (bf16[128,256]{1,0:T(8,128)(2,1)S(1)}, bf16[128,256]{1,0:T(8,128)(2,1)S(1)}, u32[]{:S(2)}, u32[]{:S(2)}) collective-permute-start(bf16[128,256]{1,0:T(8,128)(2,1)S(1)} %get-tuple-element.42), channel_id=1, source_target_pairs={{0,4},{1,5},{2,6},{3,7},{4,0},{5,1},{6,2},{7,3},{8,12},{9,13},{10,... | collective-permute-start | bytes 196616 | tf_op jit(solution)/shard_map/ppermute | solution.py:66
  16.0 3.2 %collective-permute-start.7 = (bf16[128,256]{1,0:T(8,128)(2,1)S(1)}, bf16[128,256]{1,0:T(8,128)(2,1)S(1)}, u32[]{:S(2)}, u32[]{:S(2)}) collective-permute-start(bf16[128,256]{1,0:T(8,128)(2,1)S(1)} %get-tuple-element.43), channel_id=1, source_target_pairs={{0,1},{1,0},{2,3},{3,2},{4,8},{5,9},{6,10},{7,11},{8,4},{9,5},{10,... | collective-permute-start | bytes 196616 | tf_op jit(solution)/shard_map/ppermute | solution.py:66
